TPU v7x, 32 devices: a whole 2x2x4 slice. The times are simulated.
32 devices in a mesh: wide: 8 (over z, y), narrow: 4 (over x, core).
Axes of the slice: x: 2, y: 2, z: 4, core: 2. Of those that a mesh axis runs over, the one named last changes fastest.
Arguments:
- token_ids: int32 [32, 512], P(('wide', 'narrow')), may hold values from 0 to 30719
- live_lengths: int32 [32], P(('wide', 'narrow')), may hold values from 0 to 512, as said below
- key_keep: int32 [32, 512], P(('wide', 'narrow')), may hold values 0 or 1
- buckets: int32 [32, 512], P(('wide', 'narrow')), may hold values from 0 to 3
- mask_pos: int32 [32, 80], P(('wide', 'narrow')), may hold values from 0 to 511, as said below
- mask_labels: int32 [32, 80], P(('wide', 'narrow')), may hold values from 0 to 30719
- mask_counts: int32 [32], P(('wide', 'narrow')), may hold values from 0 to 80, as said below
- source_logits: bfloat16 [32, 80, 30720], P(('wide', 'narrow')), may hold values from -12 to 12
- embed_table: float32 [31744, 1024], P(('wide', 'narrow')), may hold values from -0.6 to 0.6
- embed_first: float32 [31744, 1024], P(('wide', 'narrow')), may hold values from -6e-05 to 6e-05
- embed_second: float32 [31744, 1024], P(('wide', 'narrow')), may hold values from 1e-12 to 1e-10
- attn_mats: float32 [4, 1024, 1024], P('narrow', None, 'wide')
- attn_moment: float32 [4, 1024, 1024], P('narrow', None, 'wide'), may hold values from -0.0006 to 0.0006
- ffn_mats: float32 [2, 1024, 4096], P(None, None, ('wide', 'narrow')), may hold values from -0.1875 to 0.1875
- ffn_moment: float32 [2, 1024, 4096], P(None, None, ('wide', 'narrow')), may hold values from -0.0006 to 0.0006
- other_params: float32 [1096704], P(('wide', 'narrow'))
- other_first: float32 [1096704], P(('wide', 'narrow')), may hold values from -6e-05 to 6e-05
- other_second: float32 [1096704], P(('wide', 'narrow')), may hold values from 1e-12 to 1e-10
Outputs:
- loss_value: float32 [], replicated
- grad_norm: float32 [], replicated
- embed_new: float32 [31744, 1024], P(('wide', 'narrow'))
- embed_first_new: float32 [31744, 1024], P(('wide', 'narrow'))
- embed_second_new: float32 [31744, 1024], P(('wide', 'narrow'))
- attn_new: float32 [4, 1024, 1024], P('narrow', None, 'wide')
- attn_moment_new: float32 [4, 1024, 1024], P('narrow', None, 'wide')
- ffn_new: float32 [2, 1024, 4096], P(None, None, ('wide', 'narrow'))
- ffn_moment_new: float32 [2, 1024, 4096], P(None, None, ('wide', 'narrow'))
- other_new: float32 [1096704], P(('wide', 'narrow'))
- other_first_new: float32 [1096704], P(('wide', 'narrow'))
- other_second_new: float32 [1096704], P(('wide', 'narrow'))
Inputs may be any that keep to these rules, and one draw needn't show every extreme that they name: `live_lengths`: A window's live slots come first. Even rows (first windows of sequences) have 512 live slots; window 3 has none. mask_counts = live_lengths * 5 // 32 for each window. `mask_pos`: in each window the first mask_counts entries are distinct live positions of the window; the others hold 0.
All inputs are finite; a program needn't handle non-finite values. No bound on the sum of `key_keep` on one device may be relied on, other than what follows from the above.
Results may differ from a plain program's by a relative error of at most 0.0025.
The roundings to bfloat16 on the way count: a program that leaves them out, or rounds other values in their place, can miss the bound.
Values may be sent and summed in bfloat16 or wider, within the bound.
No kernel may reach another device: no remote copies, remote signals or barrier semaphores. Data moves between devices by JAX's collectives and lax.ppermute only.
A program may use at most 576 MiB of HBM per device.

v0:
```python
import math

import jax
import jax.numpy as jnp
from jax import lax
from jax.sharding import PartitionSpec as P

D = 1024
FF = 4096
HEADS = 16
L = 1
V = 30720
SEQ = 1024
WINDOW = 512
NS_ITERS = 3
ADAM_STEP = 5
MPW = 80
NV = 13


highest = lax.Precision.HIGHEST
ln_eps = 1e-05
masked_fill = -1e30
clip_limit = 0.3
ns_a = 3.4445
ns_b = -4.775
ns_c = 2.0315
mu_muon = 0.95
lr_muon = 0.1
muon_shape = 0.2
lr_adam = 0.01
beta_one = 0.9
beta_two = 0.999
adam_eps = 1e-08


def layer_norm(inputs, gain_vec, shift_vec):
    center = inputs - jnp.mean(inputs, -1, keepdims=True)
    spread = jnp.mean(center * center, -1, keepdims=True)
    return center * lax.rsqrt(spread + ln_eps) * gain_vec + shift_vec


def exact_gelu(inputs):
    return jax.nn.gelu(inputs, approximate=False)


def head_tail(head_pre, gain_vec, shift_vec):
    return layer_norm(exact_gelu(head_pre), gain_vec, shift_vec)


def project(inputs, weight):
    return jnp.einsum("bsd,df->bsf", inputs, weight, preferred_element_type=jnp.float32)


def project_back(gradients, weight):
    return jnp.einsum("bsf,df->bsd", gradients, weight, preferred_element_type=jnp.float32)


def outer_sum(inputs, gradients):
    return jnp.einsum("bsd,bsf->df", inputs, gradients, preferred_element_type=jnp.float32)


def col_sum(inputs):
    return jnp.sum(inputs.astype(jnp.float32), axis=(0, 1))


def to_heads(inputs):
    return inputs.reshape(
        inputs.shape[0], inputs.shape[1] // WINDOW, WINDOW, HEADS, inputs.shape[2] // HEADS
    )


def attn_scores(queries, key_proj, allowed):
    raw_scores = jnp.einsum(
        "bnqhe,bnkhe->bnhqk",
        to_heads(queries),
        to_heads(key_proj),
        preferred_element_type=jnp.float32,
    )
    return jnp.where(allowed, raw_scores * (queries.shape[2] // HEADS) ** (-0.5), masked_fill)


def layer_forward(hidden, params, allowed):
    w_query, w_key, w_value, w_out, w_up, w_down, up_bias, vectors = params
    count, length, model_width = hidden.shape
    inputs = hidden.astype(jnp.bfloat16)
    queries = (project(inputs, w_query) + vectors[4]).astype(jnp.bfloat16)
    key_proj = project(inputs, w_key).astype(jnp.bfloat16)
    values = (project(inputs, w_value) + vectors[5]).astype(jnp.bfloat16)
    scores = attn_scores(queries, key_proj, allowed)
    log_total = jax.nn.logsumexp(scores, axis=-1, keepdims=True)
    prob_low = jnp.exp(scores - log_total).astype(jnp.bfloat16)
    context = jnp.einsum(
        "bnhqk,bnkhe->bnqhe", prob_low, to_heads(values), preferred_element_type=jnp.float32
    )
    context = context.reshape(count, length, model_width).astype(jnp.bfloat16)
    attn_sum = hidden + (project(context, w_out) + vectors[6])
    middle, first_pull = jax.vjp(layer_norm, attn_sum, vectors[0], vectors[1])
    middle_low = middle.astype(jnp.bfloat16)
    up_proj = project(middle_low, w_up) + up_bias
    activated, gelu_pull = jax.vjp(exact_gelu, up_proj)
    act_low = activated.astype(jnp.bfloat16)
    ffn_sum = middle + (project_back(act_low, w_down) + vectors[7])
    output, second_pull = jax.vjp(layer_norm, ffn_sum, vectors[2], vectors[3])
    stored = (
        inputs,
        queries,
        key_proj,
        values,
        log_total,
        context,
        first_pull,
        middle_low,
        gelu_pull,
        act_low,
        second_pull,
    )
    return (output, stored)


def layer_backward(grad_out, stored, params, allowed):
    w_query, w_key, w_value, w_out, w_up, w_down, up_bias, vectors = params
    (
        inputs,
        queries,
        key_proj,
        values,
        log_total,
        context,
        first_pull,
        middle_low,
        gelu_pull,
        act_low,
        second_pull,
    ) = stored
    count, length, model_width = grad_out.shape
    grad_ffn, grad_gain_two, grad_shift_two = second_pull(grad_out)
    down_low = grad_ffn.astype(jnp.bfloat16)
    grad_down = outer_sum(down_low, act_low)
    (grad_up,) = gelu_pull(project(down_low, w_down))
    up_low = grad_up.astype(jnp.bfloat16)
    grad_w_up = outer_sum(middle_low, up_low)
    grad_middle = grad_ffn + project_back(up_low, w_up)
    grad_attn, grad_gain_one, grad_shift_one = first_pull(grad_middle)
    attn_low = grad_attn.astype(jnp.bfloat16)
    grad_w_out = outer_sum(context, attn_low)
    grad_context = to_heads(project_back(attn_low, w_out).astype(jnp.bfloat16))
    attn_prob = jnp.exp(attn_scores(queries, key_proj, allowed) - log_total)
    prob_low = attn_prob.astype(jnp.bfloat16)
    grad_prob = jnp.einsum(
        "bnqhe,bnkhe->bnhqk", grad_context, to_heads(values), preferred_element_type=jnp.float32
    )
    grad_values = jnp.einsum(
        "bnhqk,bnqhe->bnkhe", prob_low, grad_context, preferred_element_type=jnp.float32
    )
    grad_values = grad_values.reshape(count, length, model_width).astype(jnp.bfloat16)
    grad_scores = attn_prob * (grad_prob - jnp.sum(grad_prob * attn_prob, -1, keepdims=True))
    grad_raw = (grad_scores * (model_width // HEADS) ** (-0.5)).astype(jnp.bfloat16)
    grad_query = jnp.einsum(
        "bnhqk,bnkhe->bnqhe", grad_raw, to_heads(key_proj), preferred_element_type=jnp.float32
    )
    grad_query = grad_query.reshape(count, length, model_width).astype(jnp.bfloat16)
    grad_key = jnp.einsum(
        "bnhqk,bnqhe->bnkhe", grad_raw, to_heads(queries), preferred_element_type=jnp.float32
    )
    grad_key = grad_key.reshape(count, length, model_width).astype(jnp.bfloat16)
    grad_hidden = (
        grad_attn
        + project_back(grad_query, w_query)
        + project_back(grad_key, w_key)
        + project_back(grad_values, w_value)
    )
    matrices = (
        outer_sum(inputs, grad_query),
        outer_sum(inputs, grad_key),
        outer_sum(inputs, grad_values),
        grad_w_out,
        grad_w_up,
        grad_down,
    )
    vector_grads = jnp.stack(
        [
            grad_gain_one,
            grad_shift_one,
            grad_gain_two,
            grad_shift_two,
            col_sum(grad_query),
            col_sum(grad_values),
            col_sum(attn_low),
            col_sum(down_low),
        ]
    )
    return (grad_hidden, matrices, col_sum(up_low), vector_grads)


def newton_cols(moment, gram_sum):
    first_gram = gram_sum(jnp.einsum("kdc,kec->kde", moment, moment, precision=highest))
    norms = jnp.sqrt(jnp.trace(first_gram, axis1=1, axis2=2))
    scaling = 1.0 / (norms + 1e-07)
    current = moment * scaling[:, None, None]
    gram_mat = first_gram * (scaling * scaling)[:, None, None]
    for step_idx in range(NS_ITERS):
        if step_idx > 0:
            gram_mat = gram_sum(jnp.einsum("kdc,kec->kde", current, current, precision=highest))
        once_mat = jnp.einsum("kde,kec->kdc", gram_mat, current, precision=highest)
        twice_mat = jnp.einsum("kde,kec->kdc", gram_mat, once_mat, precision=highest)
        current = ns_a * current + ns_b * once_mat + ns_c * twice_mat
    return current


def muon_cols(master, moment, gradient, gram_sum, long_side):
    new_moment = mu_muon * moment + gradient
    change = lr_muon * muon_shape * math.sqrt(long_side) * newton_cols(new_moment, gram_sum)
    return (master - change, new_moment)


def adam_step(master, first_moment, second, gradient):
    new_first = beta_one * first_moment + (1.0 - beta_one) * gradient
    new_second = beta_two * second + (1.0 - beta_two) * gradient * gradient
    first_hat = new_first / (1.0 - beta_one**ADAM_STEP)
    second_hat = new_second / (1.0 - beta_two**ADAM_STEP)
    return (master - lr_adam * first_hat / (jnp.sqrt(second_hat) + adam_eps), new_first, new_second)


def square_sum(arrays):
    running = jnp.zeros((), jnp.float32)
    for member in arrays:
        running = running + jnp.sum(member * member)
    return running


def shards(
    token_ids,
    live_lengths,
    key_keep,
    buckets,
    mask_pos,
    mask_labels,
    mask_counts,
    source_logits,
    embed_table,
    embed_first,
    embed_second,
    attn_mats,
    attn_moment,
    ffn_mats,
    ffn_moment,
    other_params,
    other_first,
    other_second,
):
    wide_count = lax.axis_size("wide")
    narrow_count = lax.axis_size("narrow")
    table_low, ffn_low, other_low = (
        lax.all_gather(embed_table.astype(jnp.bfloat16), ("wide", "narrow"), axis=0, tiled=True),
        lax.all_gather(ffn_mats.astype(jnp.bfloat16), ("wide", "narrow"), axis=2, tiled=True),
        lax.all_gather(other_params.astype(jnp.bfloat16), ("wide", "narrow"), axis=0, tiled=True),
    )
    attn_part = lax.all_gather(attn_mats.astype(jnp.bfloat16), "wide", axis=2, tiled=True)
    attn_low = lax.all_gather(attn_part, "narrow", axis=0, tiled=True)
    masked_total = lax.psum(jnp.sum(mask_counts).astype(jnp.float32), ("wide", "narrow"))
    offset = V + L * FF
    dec_bias = other_low[:V].astype(jnp.float32)
    up_biases = other_low[V:offset].reshape(L, FF).astype(jnp.float32)
    vectors = other_low[offset : offset + NV * D].reshape(NV, D).astype(jnp.float32)
    head_weight = other_low[offset + NV * D :].reshape(D, D)
    win_count = token_ids.shape[0]
    device = lax.axis_index("wide") * narrow_count + lax.axis_index("narrow")
    rows_here = jnp.arange(win_count, dtype=jnp.int32) + device * win_count
    places = jnp.arange(WINDOW, dtype=jnp.int32)
    positions = V + (rows_here % (SEQ // WINDOW) * WINDOW)[:, None] + places[None, :]
    is_valid = (places[None, :] < live_lengths[:, None]) & (key_keep == 1)
    key_ok = is_valid.reshape(win_count, 1, 1, 1, WINDOW)
    bucket_ids = buckets.reshape(win_count, 1, WINDOW)
    same_bucket = bucket_ids[:, :, None, :, None] == bucket_ids[:, :, None, None, :]
    allowed = same_bucket & key_ok | jnp.eye(WINDOW, dtype=bool)
    embedded = table_low[token_ids].astype(jnp.float32) + table_low[positions].astype(jnp.float32)
    hidden, embed_pull = jax.vjp(layer_norm, embedded, vectors[0], vectors[1])
    layer_params = [
        (
            attn_low[0],
            attn_low[L],
            attn_low[2 * L],
            attn_low[3 * L],
            ffn_low[0],
            ffn_low[L],
            up_biases[0],
            vectors[2:10],
        )
    ]
    params = layer_params[0]
    hidden, stored = layer_forward(hidden, params, allowed)
    stored_all = [stored]
    flat_hidden = hidden.reshape(win_count * WINDOW, D)
    row_index = (jnp.arange(win_count, dtype=jnp.int32)[:, None] * WINDOW + mask_pos).reshape(-1)
    head_in = flat_hidden[row_index].astype(jnp.bfloat16)
    head_pre = jnp.dot(head_in, head_weight, preferred_element_type=jnp.float32) + vectors[NV - 3]
    head_out, head_pull = jax.vjp(head_tail, head_pre, vectors[NV - 2], vectors[NV - 1])
    head_low = head_out.astype(jnp.bfloat16)
    word_rows = table_low[:V]
    logits = (
        jnp.einsum("rd,vd->rv", head_low, word_rows, preferred_element_type=jnp.float32) + dec_bias
    )
    log_prob = jax.nn.log_softmax(logits, axis=-1)
    source_log = jax.nn.log_softmax(source_logits.reshape(-1, V).astype(jnp.float32), axis=-1)
    source_prob = jnp.exp(source_log)
    label_hits = jnp.arange(V, dtype=jnp.int32)[None, :] == mask_labels.reshape(-1)[:, None]
    picked = jnp.sum(jnp.where(label_hits, log_prob, 0.0), -1)
    diverge = jnp.sum(source_prob * (source_log - log_prob), -1)
    is_live = (
        (jnp.arange(MPW, dtype=jnp.int32)[None, :] < mask_counts[:, None])
        .reshape(-1)
        .astype(jnp.float32)
    )
    loss_part = jnp.sum((diverge - picked) * is_live)
    grad_logits = (
        (2.0 * jnp.exp(log_prob) - label_hits.astype(jnp.float32) - source_prob) * is_live[:, None]
    ).astype(jnp.bfloat16)
    grad_dec = jnp.sum(grad_logits.astype(jnp.float32), 0)
    grad_head_out = jnp.dot(grad_logits, word_rows, preferred_element_type=jnp.float32)
    grad_pre, grad_head_gain, grad_head_shift = head_pull(grad_head_out)
    pre_low = grad_pre.astype(jnp.bfloat16)
    grad_head_w = jnp.einsum("rd,rf->df", head_in, pre_low, preferred_element_type=jnp.float32)
    grad_head_in = jnp.einsum("rf,df->rd", pre_low, head_weight, preferred_element_type=jnp.float32)
    grad_hidden = jnp.zeros((win_count * WINDOW, D), jnp.float32).at[row_index].add(grad_head_in)
    grad_hidden = grad_hidden.reshape(win_count, WINDOW, D)
    layer_mats = [None] * L
    up_grads = [None] * L
    vec_grads = [None] * L
    for layer_idx in reversed(range(L)):
        grad_hidden, layer_mats[layer_idx], up_grads[layer_idx], vec_grads[layer_idx] = (
            layer_backward(grad_hidden, stored_all[layer_idx], layer_params[layer_idx], allowed)
        )
    grad_embed, grad_emb_gain, grad_emb_shift = embed_pull(grad_hidden)
    flat_embed = grad_embed.reshape(-1, D)
    grad_words = jnp.einsum("rv,rd->vd", grad_logits, head_low, preferred_element_type=jnp.float32)
    table_rows = jnp.concatenate([token_ids.reshape(-1), positions.reshape(-1)])
    grad_table = jnp.concatenate([grad_words, jnp.zeros((SEQ, D), jnp.float32)], axis=0)
    grad_table = grad_table.at[table_rows].add(jnp.concatenate([flat_embed, flat_embed], axis=0))
    grad_attn = jnp.stack(
        [layer_mats[layer_idx][kind_idx] for kind_idx in range(4) for layer_idx in range(L)]
    )
    grad_ffn = jnp.stack(
        [layer_mats[layer_idx][kind_idx] for kind_idx in (4, 5) for layer_idx in range(L)]
    )
    vector_block = jnp.concatenate(
        [jnp.stack([grad_emb_gain, grad_emb_shift])]
        + vec_grads
        + [jnp.stack([jnp.sum(pre_low.astype(jnp.float32), 0), grad_head_gain, grad_head_shift])],
        axis=0,
    )
    grad_other = jnp.concatenate(
        [
            grad_dec,
            jnp.stack(up_grads).reshape(-1),
            vector_block.reshape(-1),
            grad_head_w.reshape(-1),
        ]
    )
    owned = grad_attn.shape[0] // narrow_count
    col_width = D // wide_count
    attn_order = grad_attn.reshape(narrow_count, owned, D, wide_count, col_width)
    attn_order = attn_order.transpose(3, 0, 1, 2, 4).reshape(
        wide_count * narrow_count * owned, D, col_width
    )
    table_grad, attn_grad, ffn_grad, other_grad = (
        lax.psum_scatter(grad_table, ("wide", "narrow"), scatter_dimension=0, tiled=True),
        lax.psum_scatter(attn_order, ("wide", "narrow"), scatter_dimension=0, tiled=True),
        lax.psum_scatter(grad_ffn, ("wide", "narrow"), scatter_dimension=2, tiled=True),
        lax.psum_scatter(grad_other, ("wide", "narrow"), scatter_dimension=0, tiled=True),
    )
    squares = square_sum((table_grad, attn_grad, ffn_grad, other_grad))
    sq_total, loss_total = lax.psum((squares, loss_part), ("wide", "narrow"))
    grad_norm = jnp.sqrt(sq_total) / masked_total
    loss_value = loss_total / masked_total
    factor = jnp.minimum(1.0, clip_limit / grad_norm)
    scaling = factor / masked_total

    def attn_gram(gram_part):
        return lax.psum(gram_part.astype(jnp.bfloat16), "wide").astype(jnp.float32)

    def ffn_gram(gram_part):
        return lax.psum(gram_part, ("wide", "narrow"))

    embed_new, embed_first_new, embed_second_new = adam_step(
        embed_table, embed_first, embed_second, table_grad * scaling
    )
    attn_new, attn_moment_new = muon_cols(attn_mats, attn_moment, attn_grad * scaling, attn_gram, D)
    ffn_new, ffn_moment_new = muon_cols(
        ffn_mats, ffn_moment, ffn_grad * scaling, ffn_gram, max(D, FF)
    )
    other_new, other_first_new, other_second_new = adam_step(
        other_params, other_first, other_second, other_grad * scaling
    )
    return (
        loss_value,
        grad_norm,
        embed_new,
        embed_first_new,
        embed_second_new,
        attn_new,
        attn_moment_new,
        ffn_new,
        ffn_moment_new,
        other_new,
        other_first_new,
        other_second_new,
    )


def solution(mesh):
    in_specs = (
        P(("wide", "narrow"), None),
        P(("wide", "narrow")),
        P(("wide", "narrow"), None),
        P(("wide", "narrow"), None),
        P(("wide", "narrow"), None),
        P(("wide", "narrow"), None),
        P(("wide", "narrow")),
        P(("wide", "narrow"), None, None),
        P(("wide", "narrow"), None),
        P(("wide", "narrow"), None),
        P(("wide", "narrow"), None),
        P("narrow", None, "wide"),
        P("narrow", None, "wide"),
        P(None, None, ("wide", "narrow")),
        P(None, None, ("wide", "narrow")),
        P(("wide", "narrow")),
        P(("wide", "narrow")),
        P(("wide", "narrow")),
    )
    out_specs = (
        P(),
        P(),
        P(("wide", "narrow"), None),
        P(("wide", "narrow"), None),
        P(("wide", "narrow"), None),
        P("narrow", None, "wide"),
        P("narrow", None, "wide"),
        P(None, None, ("wide", "narrow")),
        P(None, None, ("wide", "narrow")),
        P(("wide", "narrow")),
        P(("wide", "narrow")),
        P(("wide", "narrow")),
    )
    return jax.shard_map(shards, mesh=mesh, in_specs=in_specs, out_specs=out_specs, check_vma=False)
```

profile of v0, /device:TPU:0, one launch (start us, length us, event | category | flops | bytes accessed | tf_op | source)
XLA Modules:
  0.0 3889.3 jit_solution(4324708692029966590)
XLA Ops:
  17.3 50.0 %all-gather.7.cloned.1.call-done = bf16[1,1024,1024]{2,1,0:T(8,128)(2,1)} async-done(((bf16[1,1024,128]{2,1,0:T(8,128)(2,1)}), bf16[1,1024,1024]{2,1,0:T(8,128)(2,1)}) %all-gather.7.cloned.1.call-update) | async-done | bytes 2097168 | tf_op jit(solution)/shard_map/all_gather | solution.py:259
  79.1 403.7 %all-reduce.26.cloned.1.call-done = bf16[1096704]{0:T(1024)(128)(2,1)} async-done(((bf16[1096704]{0:T(1024)(128)(2,1)}), bf16[1096704]{0:T(1024)(128)(2,1)}) %all-reduce.26.cloned.1.call-update) | async-done | bytes 2193424
  495.6 4.9 gather_fusion
  519.6 8.7 fusion.11
  528.3 9.3 exponential_reduce_fusion
  537.7 8.1 convolution_convert_fusion.3
  551.6 74.0 %all-gather.11.cloned.1.call-done = bf16[2,1024,4096]{2,1,0:T(8,128)(2,1)} async-done(((bf16[2,1024,128]{2,1,0:T(8,128)(2,1)}), bf16[2,1024,4096]{2,1,0:T(8,128)(2,1)}) %all-gather.11.cloned.1.call-update) | async-done | bytes 16777232 | tf_op jit(solution)/shard_map/all_gather | solution.py:256
  625.6 27.2 multiply_convert_fusion.1
  652.8 9.2 fusion.183
  667.6 30.6 fusion.184
  698.3 5.4 exponential_reduce_fusion.1
  704.8 12.9 convert_reduce_fusion.1
  717.7 24.2 fusion.170
  755.5 14.3 convert_reduce_fusion.2
  769.9 9.8 multiply_reduce_fusion.3
  786.5 8.1 fusion.188
  794.7 29.3 convert_reduce_fusion.6
  824.0 29.4 fusion.85
  853.5 9.5 convert_reduce_fusion.5
  872.1 5.4 multiply_reduce_fusion.4
  886.0 5.1 fusion.175
  897.8 6.2 copy.71
  905.2 6.6 convolution_bitcast_fusion
  911.8 8.5 convolution_bitcast_fusion.1
  920.3 19.0 pad_maximum_fusion
  940.3 44.0 %fusion.164 = f32[30720,1024]{1,0:T(8,128)} fusion(bf16[80,30720]{1,0:T(8,128)(2,1)} %get-tuple-element.40, f32[80,1024]{1,0:T(8,128)S(1)} %copy-done.25, f32[1024]{0:T(1024)S(1)} %copy-done.75, f32[1024]{0:T(1024)S(1)} %copy-done.65, f32[80]{0:T(128)S(1)} %copy-done.104, f32[80]{0:T(128)S(1)} %copy-done.91), kind=kOutput, calls=%fused_computation.284 | convolution fusion | flops 5033574400 | bytes 131080832 | tf_op jit(solution)/shard_map/rv,rd->vd/dot_general | solution.py:336
  984.3 84.5 %concatenate.39 = f32[31744,1024]{1,0:T(8,128)} pad(f32[30720,1024]{1,0:T(8,128)} %fusion.164, f32[]{:T(128)} %constant.80.clone.1), padding=0_1024x0_0 | pad | bytes 255852544 | tf_op jit(solution)/shard_map/concatenate | solution.py:338
  1071.8 150.9 %scatter_fusion = f32[31744,1024]{1,0:T(8,128)} fusion(f32[31744,1024]{1,0:T(8,128)} %concatenate.39, s32[1024]{0:T(1024)S(1)} %bitcast.304, f32[1024,1024]{1,0:T(8,128)} %pad_maximum_fusion.2), kind=kCustom, calls=%fused_computation.4 | custom fusion | flops 1048576 | bytes 12587008 | tf_op jit(solution)/shard_map/scatter-add | solution.py:339
  1227.4 340.0 %reduce-scatter.9.cloned.1.call-done = f32[2,1024,128]{2,1,0:T(8,128)} async-done(((f32[2,1024,4096]{2,1,0:T(8,128)}), f32[2,1024,128]{2,1,0:T(8,128)}) %reduce-scatter.9.cloned.1.call-update) | async-done | bytes 1048592 | tf_op jit(solution)/shard_map/reduce_scatter | solution.py:369
  1569.5 1363.8 %reduce-scatter.11.cloned.1.call-done = f32[992,1024]{1,0:T(8,128)} async-done(((f32[31744,1024]{1,0:T(8,128)}), f32[992,1024]{1,0:T(8,128)}) %reduce-scatter.11.cloned.1.call-update) | async-done | bytes 4063248
  2939.7 47.0 %all-reduce.4 = (f32[]{:T(128)}, f32[]{:T(128)}, f32[]{:T(128)}) all-reduce(f32[]{:T(128)} %fusion.147, f32[]{:T(128)S(6)} %convert_element_type.387, f32[]{:T(128)S(6)} %add.529), channel_id=1, replica_groups=mesh['wide'=8,'narrow'=4] {'wide','narrow'}, use_global_device_ids=true, to_apply=%region_15.17 | all-reduce | flops 3 | bytes 24 | tf_op jit(solution)/shard_map/psum | solution.py:373
  2994.5 8.8 fusion.189
  3005.0 91.6 %all-reduce.14.cloned.1.call-done = bf16[1,1024,1024]{2,1,0:T(8,128)(2,1)} async-done(((bf16[1,1024,1024]{2,1,0:T(8,128)(2,1)}), bf16[1,1024,1024]{2,1,0:T(8,128)(2,1)}) %all-reduce.14.cloned.1.call-update) | async-done | bytes 2097168 | tf_op jit(solution)/shard_map/psum | solution.py:380
  3099.9 5.1 fusion.63
  3115.1 165.5 %all-reduce.20.cloned.1.call-done = f32[2,1024,1024]{2,1,0:T(8,128)} async-done(((f32[2,1024,1024]{2,1,0:T(8,128)}), f32[2,1024,1024]{2,1,0:T(8,128)}) %all-reduce.20.cloned.1.call-update) | async-done | bytes 8388624 | tf_op jit(solution)/shard_map/psum | solution.py:383
  3286.3 7.4 fusion.53
  3293.8 7.7 fusion.93
  3301.4 8.8 fusion.190
  3310.3 76.8 %all-reduce.16.cloned.1.call-done = bf16[1024,1024]{1,0:T(8,128)(2,1)} async-done(((bf16[1024,1024]{1,0:T(8,128)(2,1)}), bf16[1024,1024]{1,0:T(8,128)(2,1)}) %all-reduce.16.cloned.1.call-update) | async-done | bytes 2097168 | tf_op jit(solution)/shard_map/psum | solution.py:380
  3397.6 173.5 %all-reduce.22.cloned.1.call-done = f32[2,1024,1024]{2,1,0:T(8,128)} async-done(((f32[2,1024,1024]{2,1,0:T(8,128)}), f32[2,1024,1024]{2,1,0:T(8,128)}) %all-reduce.22.cloned.1.call-update) | async-done | bytes 8388624 | tf_op jit(solution)/shard_map/psum | solution.py:383
  3571.1 9.8 fusion.191
  3581.0 7.1 fusion.99
  3588.1 9.0 fusion.192
  3601.1 10.9 divide_subtract_fusion
  3612.0 65.1 %all-reduce.18.cloned.1.call-done = bf16[1024,1024]{1,0:T(8,128)(2,1)} async-done(((bf16[1024,1024]{1,0:T(8,128)(2,1)}), bf16[1024,1024]{1,0:T(8,128)(2,1)}) %all-reduce.18.cloned.1.call-update) | async-done | bytes 2097168 | tf_op jit(solution)/shard_map/psum | solution.py:380
  3683.3 177.7 %all-reduce.24.cloned.1.call-done = f32[2,1024,1024]{2,1,0:T(8,128)} async-done(((f32[2,1024,1024]{2,1,0:T(8,128)}), f32[2,1024,1024]{2,1,0:T(8,128)}) %all-reduce.24.cloned.1.call-update) | async-done | bytes 8388624 | tf_op jit(solution)/shard_map/psum | solution.py:383
  3861.0 10.0 fusion.193
  3871.1 8.1 fusion.98
  (394 shorter events, 167.8 us)
Async XLA Ops:
  8.0 59.3 %all-gather.7.cloned.1.call-start = ((), (), s32[]{:S(2)}) async-start(), calls=%async_computation.4 | async-start | bytes 2359296 | tf_op jit(solution)/shard_map/all_gather | solution.py:259
  9.9 473.0 %all-reduce.26.cloned.1.call-start = ((), (), s32[]{:S(2)}) async-start(), calls=%async_computation.15 | async-start | bytes 4386816
  13.3 54.1 %copy-start.26 = (f32[2,1024,128]{2,1,0:T(8,128)S(1)}, f32[2,1024,128]{2,1,0:T(8,128)}, u32[]{:S(2)}) copy-start(f32[2,1024,128]{2,1,0:T(8,128)} %param.32) | copy-start | bytes 3145732
  13.3 478.1 %all-gather.5.cloned.1.call-start = ((), (), s32[]{:S(2)}) async-start(), calls=%async_computation.3 | async-start | bytes 67043328 | tf_op jit(solution)/shard_map/all_gather | solution.py:255
  17.2 484.3 %all-gather.9.cloned.1.call-start = ((), (), s32[]{:S(2)}) async-start(), calls=%async_computation.5 | async-start | bytes 10485760 | tf_op jit(solution)/shard_map/all_gather | solution.py:260
  67.3 558.2 %all-gather.11.cloned.1.call-start = ((), (), s32[]{:S(2)}) async-start(), calls=%async_computation.6 | async-start | bytes 17301504 | tf_op jit(solution)/shard_map/all_gather | solution.py:256
  68.2 1155.7 %all-reduce.28.cloned.1.call-start = ((), (), s32[]{:S(2)}) async-start(), calls=%async_computation.16 | async-start | bytes 8773632
  79.1 458.6 %copy-start.41 = (pred[512,512]{0,1:T(8,128)(4,1)}, pred[512,512]{0,1:T(8,128)(4,1)S(1)}, u32[]{:S(2)}) copy-start(pred[512,512]{0,1:T(8,128)(4,1)S(1)} %fusion.119) | copy-start | bytes 786436
  489.9 55.9 %copy-start.76 = (f32[1024]{0:T(1024)}, f32[1024]{0:T(1024)S(1)}, u32[]{:S(2)}) copy-start(f32[1024]{0:T(1024)S(1)} %get-tuple-element.72) | copy-start | bytes 12292
  489.9 56.0 %copy-start.78 = (f32[1024]{0:T(1024)}, f32[1024]{0:T(1024)S(1)}, u32[]{:S(2)}) copy-start(f32[1024]{0:T(1024)S(1)} %get-tuple-element.73) | copy-start | bytes 12292
  489.9 162.9 %copy-start.85 = (f32[1024]{0:T(1024)}, f32[1024]{0:T(1024)S(1)}, u32[]{:S(2)}) copy-start(f32[1024]{0:T(1024)S(1)} %get-tuple-element.68) | copy-start | bytes 12292
  489.9 162.9 %copy-start.107 = (f32[1024]{0:T(1024)}, f32[1024]{0:T(1024)S(1)}, u32[]{:S(2)}) copy-start(f32[1024]{0:T(1024)S(1)} %get-tuple-element.67) | copy-start | bytes 12292
  489.9 177.7 %copy-start.74 = (f32[1024]{0:T(1024)}, f32[1024]{0:T(1024)S(1)}, u32[]{:S(2)}) copy-start(f32[1024]{0:T(1024)S(1)} %get-tuple-element.62) | copy-start | bytes 12292
  489.9 254.1 %copy-start.64 = (f32[1024]{0:T(1024)}, f32[1024]{0:T(1024)S(1)}, u32[]{:S(2)}) copy-start(f32[1024]{0:T(1024)S(1)} %get-tuple-element.61) | copy-start | bytes 12292
  495.6 50.2 %copy-start.7 = (bf16[512,1024]{1,0:T(8,128)(2,1)}, bf16[512,1024]{1,0:T(8,128)(2,1)S(1)}, u32[]{:S(2)}) copy-start(bf16[512,1024]{1,0:T(8,128)(2,1)S(1)} %gather_fusion.1) | copy-start | bytes 3145732
  500.6 45.3 %copy-start.9 = (bf16[512,1024]{1,0:T(8,128)(2,1)}, bf16[512,1024]{1,0:T(8,128)(2,1)S(1)}, u32[]{:S(2)}) copy-start(bf16[512,1024]{1,0:T(8,128)(2,1)S(1)} %gather_fusion) | copy-start | bytes 3145732
  500.9 44.9 %copy-start.68 = (f32[512]{0:T(512)}, f32[512]{0:T(512)S(1)}, u32[]{:S(2)}) copy-start(f32[512]{0:T(512)S(1)} %broadcast_multiply_fusion.2) | copy-start | bytes 6148
  501.4 44.4 %copy-start.96 = (f32[512]{0:T(512)}, f32[512]{0:T(512)S(1)}, u32[]{:S(2)}) copy-start(f32[512]{0:T(512)S(1)} %fusion.144) | copy-start | bytes 6148
  545.9 79.7 %copy-start.82 = (f32[4096]{0:T(1024)S(1)}, f32[4096]{0:T(1024)}, u32[]{:S(2)}) copy-start(f32[4096]{0:T(1024)} %slice_convert_fusion.2) | copy-start | bytes 49156
  551.5 101.2 %copy-start.72 = (f32[512]{0:T(512)}, f32[512]{0:T(512)S(1)}, u32[]{:S(2)}) copy-start(f32[512]{0:T(512)S(1)} %multiply_reduce_fusion.9) | copy-start | bytes 6148
  551.6 101.2 %copy-start.93 = (f32[512]{0:T(512)}, f32[512]{0:T(512)S(1)}, u32[]{:S(2)}) copy-start(f32[512]{0:T(512)S(1)} %fusion.145) | copy-start | bytes 6148
  625.6 27.2 copy-start.110
  667.3 76.7 %copy-start.24 = (f32[80,1024]{1,0:T(8,128)}, f32[80,1024]{1,0:T(8,128)S(1)}, u32[]{:S(2)}) copy-start(f32[80,1024]{1,0:T(8,128)S(1)} %get-tuple-element.54) | copy-start | bytes 983044
  667.4 30.9 copy-start.90
  667.6 30.7 copy-start.120
  667.6 30.7 copy-start.103
  794.7 29.3 copy-start.30
  824.0 29.5 copy-start.67
  883.3 342.3 %reduce-scatter.7.cloned.1.call-start = ((), (), s32[]{:S(2)}) async-start(), calls=%async_computation.7 | async-start | bytes 17301504 | tf_op jit(solution)/shard_map/reduce_scatter | solution.py:368
  904.0 663.4 %reduce-scatter.9.cloned.1.call-start = ((), (), s32[]{:S(2)}) async-start(), calls=%async_computation.8 | async-start | bytes 34603008 | tf_op jit(solution)/shard_map/reduce_scatter | solution.py:369
  939.4 1993.9 %reduce-scatter.11.cloned.1.call-start = ((), (), s32[]{:S(2)}) async-start(), calls=%async_computation.17 | async-start | bytes 134086656
  984.3 84.5 %copy-start.98 = (f32[512]{0:T(512)S(1)}, f32[512]{0:T(512)}, u32[]{:S(2)}) copy-start(f32[512]{0:T(512)} %get-tuple-element.47) | copy-start | bytes 6148
  984.3 84.5 %copy-start.13 = (f32[512,1024]{1,0:T(8,128)S(1)}, f32[512,1024]{1,0:T(8,128)}, u32[]{:S(2)}) copy-start(f32[512,1024]{1,0:T(8,128)} %get-tuple-element.48) | copy-start | bytes 6291460
  1222.7 1766.1 %copy-start.59 = (f32[1,1024,128]{2,1,0:T(8,128)S(1)}, f32[1,1024,128]{2,1,0:T(8,128)}, u32[]{:S(2)}) copy-start(f32[1,1024,128]{2,1,0:T(8,128)} %param.31) | copy-start | bytes 1572868
  1222.7 1873.9 %all-reduce.14.cloned.1.call-start = ((), (), s32[]{:S(2)}) async-start(), calls=%async_computation.9 | async-start | bytes 4194304 | tf_op jit(solution)/shard_map/psum | solution.py:380
  1225.6 1763.2 %copy-start.43 = (f32[1,1024,128]{2,1,0:T(8,128)S(1)}, f32[1,1024,128]{2,1,0:T(8,128)}, u32[]{:S(2)}) copy-start(f32[1,1024,128]{2,1,0:T(8,128)} %reduce-scatter.7.cloned.1.call-done) | copy-start | bytes 1572868
  1569.5 1424.8 %copy-start.34 = (f32[2,1024,128]{2,1,0:T(8,128)S(1)}, f32[2,1024,128]{2,1,0:T(8,128)}, u32[]{:S(2)}) copy-start(f32[2,1024,128]{2,1,0:T(8,128)} %reduce-scatter.9.cloned.1.call-done) | copy-start | bytes 3145732
  1569.5 1424.8 %copy-start.47 = (f32[2,1024,128]{2,1,0:T(8,128)S(1)}, f32[2,1024,128]{2,1,0:T(8,128)}, u32[]{:S(2)}) copy-start(f32[2,1024,128]{2,1,0:T(8,128)} %param.33) | copy-start | bytes 3145732
  2994.3 286.3 %all-reduce.20.cloned.1.call-start = ((), (), s32[]{:S(2)}) async-start(), calls=%async_computation.12 | async-start | bytes 16777216 | tf_op jit(solution)/shard_map/psum | solution.py:383
  2994.5 299.3 %copy-start.4 = (f32[2,1024,128]{2,1,0:T(8,128)}, f32[2,1024,128]{2,1,0:T(8,128)S(1)}, u32[]{:S(2)}) copy-start(f32[2,1024,128]{2,1,0:T(8,128)S(1)} %multiply_add_fusion.4) | copy-start | bytes 3145732
  3003.3 383.8 %all-reduce.16.cloned.1.call-start = ((), (), s32[]{:S(2)}) async-start(), calls=%async_computation.10 | async-start | bytes 4194304 | tf_op jit(solution)/shard_map/psum | solution.py:380
  3110.3 170.3 %copy-start.33 = (pred[1024,1024]{1,0:T(8,128)(4,1)S(1)}, pred[1024,1024]{1,0:T(8,128)(4,1)}, u32[]{:S(2)}) copy-start(pred[1024,1024]{1,0:T(8,128)(4,1)} %iota_compare_fusion.1) | copy-start | bytes 3145732
  3114.9 456.3 %all-reduce.22.cloned.1.call-start = ((), (), s32[]{:S(2)}) async-start(), calls=%async_computation.13 | async-start | bytes 16777216 | tf_op jit(solution)/shard_map/psum | solution.py:383
  3310.2 76.9 %copy-start.23 = (f32[1,1024,128]{2,1,0:T(8,128)S(1)}, f32[1,1024,128]{2,1,0:T(8,128)}, u32[]{:S(2)}) copy-start(f32[1,1024,128]{2,1,0:T(8,128)} %copy-done.22) | copy-start | bytes 1572868
  3310.3 366.9 %all-reduce.18.cloned.1.call-start = ((), (), s32[]{:S(2)}) async-start(), calls=%async_computation.11 | async-start | bytes 4194304 | tf_op jit(solution)/shard_map/psum | solution.py:380
  3397.2 463.9 %all-reduce.24.cloned.1.call-start = ((), (), s32[]{:S(2)}) async-start(), calls=%async_computation.14 | async-start | bytes 16777216 | tf_op jit(solution)/shard_map/psum | solution.py:383
  3601.1 79.6 %copy-start.44 = (f32[1,1024,128]{2,1,0:T(8,128)S(1)}, f32[1,1024,128]{2,1,0:T(8,128)}, u32[]{:S(2)}) copy-start(f32[1,1024,128]{2,1,0:T(8,128)} %param.30) | copy-start | bytes 1572868
  3683.3 187.8 %copy-start.27 = (f32[2,1024,128]{2,1,0:T(8,128)S(1)}, f32[2,1024,128]{2,1,0:T(8,128)}, u32[]{:S(2)}) copy-start(f32[2,1024,128]{2,1,0:T(8,128)} %param.32) | copy-start | bytes 3145732
  (93 other events, 499.8 us)
Sparse Core Ops, SparseCore 0:
  11.4 55.7 all-gather.6
  70.7 346.1 all-gather.4
  418.5 57.0 all-gather.8
  478.9 146.5 all-gather.10
  2994.4 102.2 all-reduce.13
  3102.2 178.2 all-reduce.19
  3284.7 102.3 all-reduce.15
  3392.8 178.2 all-reduce.21
  3574.8 102.3 all-reduce.17
  3682.7 178.3 all-reduce.23
Sparse Core Ops, SparseCore 1:
  16.5 466.3 all-reduce.25
  883.4 141.0 all-reduce.27
  1026.7 182.3 reduce-scatter.6
  1211.4 356.0 reduce-scatter.8
  1569.8 1363.4 reduce-scatter.10
where the time goes:
time: 3900 us; the launch traced here: 3890 us
  waiting for transfers between devices  2980 us (76%)
  matrix products  423 us (11%)
  other arithmetic  274 us (7%)
  local copies, waits for them, and re-layouts  132 us (3%)
  blocking collectives  47 us (1%)
    unnamed x18, waiting for transfers between devices  1770 us
    psum x3, waiting for transfers between devices, ffn_gram(): return lax.psum(gram_part, ('wide', 'narrow'))  517 us
    reduce_scatter x1, waiting for transfers between devices, shards(): lax.psum_scatter(grad_ffn, ('wide', 'narrow'), scatter_dimension=2, tiled...  340 us
    psum x3, waiting for transfers between devices, attn_gram(): return lax.psum(gram_part.astype(jnp.bfloat16), 'wide').astype(jnp.float32)  234 us
    scatter-add x1, other arithmetic, shards(): grad_table.at[table_rows]  151 us
    concatenate x1, local copies, waits for them, and re-layouts, shards(): jnp.concatenate([grad_words, jnp.zeros((SEQ, D), jnp.float32)], axis=0)  84.5 us
  transfers between devices with their start and end apart: 15, of which 11 were waited for; matrix products, arithmetic and copies ran while one was open for 14% of the time, Pallas kernels for 0%

commit v1 on v0

v1 whole, which is shorter than its diff:
```python
import functools
import math

import jax
import jax.numpy as jnp
import numpy as np
from jax import lax
from jax.experimental import pallas as pl
from jax.experimental.pallas import tpu as pltpu
from jax.sharding import Mesh
from jax.sharding import PartitionSpec as P

D = 1024
FF = 4096
HEADS = 16
L = 1
V = 30720
SEQ = 1024
WINDOW = 512
NS_ITERS = 3
ADAM_STEP = 5
MPW = 80
NV = 13


high = lax.Precision.HIGH
lanes = 128
tile = 16
slots = 32
ln_eps = 1e-05
masked_fill = -1e30
clip_limit = 0.3
ns_a = 3.4445
ns_b = -4.775
ns_c = 2.0315
mu_muon = 0.95
lr_muon = 0.1
muon_shape = 0.2
lr_adam = 0.01
beta_one = 0.9
beta_two = 0.999
adam_eps = 1e-08


def layer_norm(inputs, gain_vec, shift_vec):
    center = inputs - jnp.mean(inputs, -1, keepdims=True)
    spread = jnp.mean(center * center, -1, keepdims=True)
    return center * lax.rsqrt(spread + ln_eps) * gain_vec + shift_vec


def exact_gelu(inputs):
    return jax.nn.gelu(inputs, approximate=False)


def head_tail(head_pre, gain_vec, shift_vec):
    return layer_norm(exact_gelu(head_pre), gain_vec, shift_vec)


def project(inputs, weight):
    return jnp.einsum("bsd,df->bsf", inputs, weight, preferred_element_type=jnp.float32)


def project_back(gradients, weight):
    return jnp.einsum("bsf,df->bsd", gradients, weight, preferred_element_type=jnp.float32)


def col_sum(inputs):
    return jnp.sum(inputs.astype(jnp.float32), axis=(0, 1))


def to_heads(inputs):
    return inputs.reshape(
        inputs.shape[0], inputs.shape[1] // WINDOW, WINDOW, HEADS, inputs.shape[2] // HEADS
    )


def attn_scores(queries, key_proj, allowed):
    raw_scores = jnp.einsum(
        "bnqhe,bnkhe->bnhqk",
        to_heads(queries),
        to_heads(key_proj),
        preferred_element_type=jnp.float32,
    )
    return jnp.where(allowed, raw_scores * (queries.shape[2] // HEADS) ** (-0.5), masked_fill)


def share(values, axis):
    return jnp.concatenate([values, exchange(values, side_bit)], axis=axis)


def swap_pick(for_first, for_second, axis):
    first = lax.axis_index("side") == 0
    keep = jnp.where(first, for_first, for_second)
    got = exchange(jnp.where(first, for_second, for_first), side_bit)
    return jnp.concatenate([keep, got], axis=axis)


def share_half(values):
    side = lax.axis_index("side")
    half = values.shape[1] // 2
    keep = lax.dynamic_slice_in_dim(values, side * half, half, axis=1)
    got = exchange(lax.dynamic_slice_in_dim(values, (1 - side) * half, half, axis=1), side_bit)
    return jnp.concatenate([keep, got])


def layer_forward(hidden, params, allowed):
    w_query, w_key, w_value, w_out, w_up, w_down, up_bias, vectors = params
    count, length, model_width = hidden.shape
    inputs = hidden.astype(jnp.bfloat16)
    queries = (project(inputs, w_query) + vectors[4]).astype(jnp.bfloat16)
    key_proj = project(inputs, w_key).astype(jnp.bfloat16)
    values = (project(inputs, w_value) + vectors[5]).astype(jnp.bfloat16)
    scores = attn_scores(queries, key_proj, allowed)
    log_total = jax.nn.logsumexp(scores, axis=-1, keepdims=True)
    prob_low = jnp.exp(scores - log_total).astype(jnp.bfloat16)
    context = jnp.einsum(
        "bnhqk,bnkhe->bnqhe", prob_low, to_heads(values), preferred_element_type=jnp.float32
    )
    context = context.reshape(count, length, model_width).astype(jnp.bfloat16)
    attn_sum = hidden + (project(context, w_out) + vectors[6])
    middle, first_pull = jax.vjp(layer_norm, attn_sum, vectors[0], vectors[1])
    middle_low = middle.astype(jnp.bfloat16)
    up_proj = project(middle_low, w_up) + up_bias
    activated, gelu_pull = jax.vjp(exact_gelu, up_proj)
    act_low = activated.astype(jnp.bfloat16)
    ffn_sum = middle + (project_back(act_low, w_down) + vectors[7])
    output, second_pull = jax.vjp(layer_norm, ffn_sum, vectors[2], vectors[3])
    stored = (
        inputs,
        queries,
        key_proj,
        values,
        log_total,
        context,
        first_pull,
        middle_low,
        gelu_pull,
        act_low,
        second_pull,
    )
    return (output, stored)


def layer_backward(grad_out, stored, params, allowed):
    w_query, w_key, w_value, w_out, w_up, w_down, _, _ = params
    (
        inputs,
        queries,
        key_proj,
        values,
        log_total,
        context,
        first_pull,
        middle_low,
        gelu_pull,
        act_low,
        second_pull,
    ) = stored
    count, length, model_width = grad_out.shape
    grad_ffn, grad_gain_two, grad_shift_two = second_pull(grad_out)
    down_low = grad_ffn.astype(jnp.bfloat16)
    (grad_up,) = gelu_pull(project(down_low, w_down))
    up_low = grad_up.astype(jnp.bfloat16)
    wide_count = lax.axis_size("wide")
    operands = (
        share(middle_low[0].T, 1),
        share(down_low[0].T, 1),
        share_half(up_low[0]),
        share_half(act_low[0]),
    )
    if FF // (4 * wide_count) == lanes:
        grad_mats_ffn = ffn_weight_grads(*operands, wide_count)
    else:
        blocks = jnp.stack([jnp.dot(*operands[::2], preferred_element_type=jnp.float32),
                            jnp.dot(*operands[1::2], preferred_element_type=jnp.float32)])
        blocks = blocks.reshape(2, D, wide_count, 2, -1).transpose(2, 3, 0, 1, 4)
        grad_mats_ffn = in_routes(blocks, wide_count)
    grad_ffn, *grad_mats_ffn = lax.optimization_barrier((grad_ffn, *grad_mats_ffn))
    grad_middle = grad_ffn + project_back(up_low, w_up)
    grad_attn, grad_gain_one, grad_shift_one = first_pull(grad_middle)
    attn_low = grad_attn.astype(jnp.bfloat16)
    grad_context = to_heads(project_back(attn_low, w_out).astype(jnp.bfloat16))
    attn_prob = jnp.exp(attn_scores(queries, key_proj, allowed) - log_total)
    prob_low = attn_prob.astype(jnp.bfloat16)
    grad_prob = jnp.einsum(
        "bnqhe,bnkhe->bnhqk", grad_context, to_heads(values), preferred_element_type=jnp.float32
    )
    grad_value = jnp.einsum(
        "bnhqk,bnqhe->bnkhe", prob_low, grad_context, preferred_element_type=jnp.float32
    )
    grad_value = grad_value.reshape(count, length, model_width).astype(jnp.bfloat16)
    grad_scores = attn_prob * (grad_prob - jnp.sum(grad_prob * attn_prob, -1, keepdims=True))
    grad_raw = (grad_scores * (model_width // HEADS) ** (-0.5)).astype(jnp.bfloat16)
    grad_query = jnp.einsum(
        "bnhqk,bnkhe->bnqhe", grad_raw, to_heads(key_proj), preferred_element_type=jnp.float32
    )
    grad_query = grad_query.reshape(count, length, model_width).astype(jnp.bfloat16)
    grad_key = jnp.einsum(
        "bnhqk,bnqhe->bnkhe", grad_raw, to_heads(queries), preferred_element_type=jnp.float32
    )
    grad_key = grad_key.reshape(count, length, model_width).astype(jnp.bfloat16)
    grad_hidden = (
        grad_attn
        + project_back(grad_query, w_query)
        + project_back(grad_key, w_key)
        + project_back(grad_value, w_value)
    )
    operands = (
        share(inputs[0].T, 1),
        swap_pick(inputs[0].T, context[0].T, 1),
        swap_pick(grad_query[0], grad_key[0], 0),
        swap_pick(grad_value[0], attn_low[0], 0),
    )
    if D // wide_count == lanes:
        grad_mats_attn = attn_weight_grads(*operands, wide_count)
    else:
        blocks = jnp.stack([jnp.dot(*operands[::2], preferred_element_type=jnp.float32),
                            jnp.dot(*operands[1::2], preferred_element_type=jnp.float32)])
        blocks = blocks.reshape(2, 1, D, wide_count, -1).transpose(3, 0, 1, 2, 4)
        grad_mats_attn = in_routes(blocks, wide_count)
    matrices = (grad_mats_attn, grad_mats_ffn)
    vector_grads = jnp.stack(
        [
            grad_gain_one,
            grad_shift_one,
            grad_gain_two,
            grad_shift_two,
            col_sum(grad_query),
            col_sum(grad_value),
            col_sum(attn_low),
            col_sum(down_low),
        ]
    )
    return (grad_hidden, matrices, col_sum(up_low), vector_grads)


def slab_product(matrix, columns):
    return jnp.einsum(
        "kde,kec->kdc", matrix, columns, precision=high, preferred_element_type=jnp.float32
    )


def newton_cols(moment, gram):
    norms = jnp.sqrt(jnp.trace(gram, axis1=1, axis2=2))
    scaling = 1.0 / (norms + 1e-07)
    current = moment * scaling[:, None, None]
    gram = gram * (scaling * scaling)[:, None, None]
    for step_idx in range(NS_ITERS):
        if step_idx + 1 < NS_ITERS:
            poly = ns_b * gram + ns_c * jnp.einsum("kde,kef->kdf", gram, gram)
            current = ns_a * current + slab_product(poly, current)
            half = ns_a * gram + jnp.einsum("kde,kef->kdf", poly, gram)
            gram = ns_a * half + jnp.einsum("kde,kef->kdf", half, poly)
        else:
            once = slab_product(gram, current)
            current = ns_a * current + ns_b * once + ns_c * slab_product(gram, once)
    return current


def gather_columns(columns, with_pair):
    wide_count = lax.axis_size("wide")
    return gather_relative(columns[0].astype(jnp.bfloat16), wide_count, 0, tile, with_pair)


def gram_of(found):
    return jnp.einsum("wdc,wec->de", found, found, preferred_element_type=jnp.float32)[None]


def relative_order(part, taken):
    names = [bit for bit in wide_bits(lax.axis_size("wide"))[::-1] + [("pair", 1)] if bit in taken]
    dims = [names.index(bit) for bit in taken[::-1]]
    split = part.reshape((2,) * len(taken) + part.shape[1:])
    turn = [dims.index(place) for place in range(len(taken))]
    split = split.transpose(turn + list(range(len(taken), split.ndim)))
    return split.reshape(part.shape)


def muon_cols(master, new_moment, gram, long_side):
    change = lr_muon * muon_shape * math.sqrt(long_side) * newton_cols(new_moment, gram)
    return master - change


def adam_step(master, first_moment, second, gradient):
    new_first = beta_one * first_moment + (1.0 - beta_one) * gradient
    new_second = beta_two * second + (1.0 - beta_two) * gradient * gradient
    first_hat = new_first / (1.0 - beta_one**ADAM_STEP)
    second_hat = new_second / (1.0 - beta_two**ADAM_STEP)
    return (master - lr_adam * first_hat / (jnp.sqrt(second_hat) + adam_eps), new_first, new_second)


def square_sum(arrays):
    running = jnp.zeros((), jnp.float32)
    for member in arrays:
        running = running + jnp.sum(member * member)
    return running


everyone = ("wide", "pair", "side")
side_bit = ("side", 1)


def swap_all(blocks, axes=everyone):
    return lax.all_to_all(blocks, axes, 0, 0, tiled=True)


def spread(values, devices):
    size = values.shape[0]
    row = jnp.pad(values, (0, -size % lanes))
    return swap_all(jnp.broadcast_to(row[None], (devices, row.shape[0])))[:, :size]


def wide_bits(wide_count):
    return [("wide", 1 << k) for k in range(wide_count.bit_length() - 1)]


def routes(wide_count, with_pair=True):
    bits = wide_bits(wide_count)
    near, far, across = bits[:1], bits[1:], [("pair", 1)] if with_pair else []
    return [across + near + far, near + far + across, far + across + near]


def my_bit(bit):
    axis, mask = bit
    return lax.axis_index(axis) // mask % 2


def exchange(values, bit):
    axis, mask = bit
    steps = [(here, here ^ mask) for here in range(lax.axis_size(axis))]
    return lax.ppermute(values, axis, steps)


def halve(values, bit, dim):
    mine = lax.dynamic_index_in_dim(values, my_bit(bit), dim, keepdims=False)
    theirs = lax.dynamic_index_in_dim(values, 1 - my_bit(bit), dim, keepdims=False)
    return mine + exchange(theirs, bit)


def double(values, bit, dim):
    theirs = exchange(values, bit)
    first = my_bit(bit) == 0
    pair = [jnp.where(first, values, theirs), jnp.where(first, theirs, values)]
    return jnp.stack(pair, axis=dim)


def cuts(length, unit):
    whole = length // unit
    sizes = [(whole + 2) // 3 * unit, (whole + 1) // 3 * unit]
    sizes.append(length - sum(sizes))
    starts = [0, sizes[0], sizes[0] + sizes[1]]
    return [(start, start + size) for start, size in zip(starts, sizes) if size]


def reduce_blocks(values, wide_count, axis, unit):
    bits = wide_bits(wide_count)[::-1] + [("pair", 1)]
    parts = []
    for route, (start, stop) in zip(routes(wide_count), cuts(values.shape[2 + axis], unit)):
        part = lax.slice_in_dim(values, start, stop, axis=2 + axis)
        part = part.reshape((2,) * len(bits) + part.shape[2:])
        left = list(bits)
        for bit in route:
            part = halve(part, bit, left.index(bit))
            left.remove(bit)
        parts.append(part)
    return jnp.concatenate(parts, axis=axis)


def here16():
    return lax.axis_index("wide") * 2 + lax.axis_index("pair")


def reduce_relative(parts, wide_count):
    done = []
    for part, route in zip(parts, routes(wide_count)):
        for bit in route:
            part = part[0] + exchange(part[1], bit)
        done.append(part)
    return done


def reduce_rows(values, wide_count):
    bits = wide_bits(wide_count)[::-1] + [("pair", 1)]
    parts = []
    for route, (start, stop) in zip(routes(wide_count), cuts(values.shape[-1], lanes)):
        part = values[..., start:stop].reshape((2,) * len(bits) + (values.shape[1], stop - start))
        left = list(bits)
        for bit in route:
            dim = left.index(bit)
            left.remove(bit)
            keep = lax.index_in_dim(part, 0, dim, keepdims=False)
            part = keep + exchange(lax.index_in_dim(part, 1, dim, keepdims=False), bit)
        parts.append(part)
    return jnp.concatenate(parts, axis=-1)


def gather_relative(block, wide_count, axis, unit, with_pair=True):
    parts = []
    for route, (start, stop) in zip(routes(wide_count, with_pair), cuts(block.shape[axis], unit)):
        part = lax.slice_in_dim(block, start, stop, axis=axis)[None]
        for bit in route[::-1]:
            part = jnp.concatenate([part, exchange(part, bit)])
        parts.append(relative_order(part, route[::-1]))
    return jnp.concatenate(parts, axis=1 + axis)


def route_shape(route, covered):
    wide = [bit for bit in route if bit not in covered]
    shape = tuple(2 if bit in covered else 1 for bit in route)

    def index(step):
        low = 1 << len(covered) - 1
        return tuple(
            0 if bit in covered else step * low // bit[1] % 2 for bit in route
        )

    assert wide
    return shape, index


def weight_grads(kernel, operands, column_specs, covered, steps, members, wide_count):
    here = jnp.stack([lax.axis_index("wide"), lax.axis_index("pair")]).astype(jnp.int32)
    shapes, specs = [], []
    for route, (start, stop) in zip(routes(wide_count), cuts(D, tile)):
        block, index = route_shape(route, covered)
        tail = (members, stop - start, lanes)
        shapes.append(jax.ShapeDtypeStruct((2,) * len(route) + tail, jnp.float32))
        specs.append(
            pl.BlockSpec(block + tail, lambda step, _, index=index: index(step) + (0, 0, 0))
        )
    return pl.pallas_call(
        kernel,
        grid_spec=pltpu.PrefetchScalarGridSpec(
            num_scalar_prefetch=1, grid=(steps,), in_specs=column_specs, out_specs=specs
        ),
        out_shape=shapes,
    )(here, *operands)


def put(refs, wide_count, covered, where, member, values):
    for ref, route, (start, stop) in zip(refs, routes(wide_count), cuts(D, tile)):
        place = tuple(where[bit] if bit in covered else 0 for bit in route)
        ref[place + (member,)] = values[start:stop]


def ffn_grads_kernel(here, up_rows, down_rows, up_cols, down_cols, *refs, wide_count):
    flip = here[1] == 0
    pair = ("pair", 1)
    for member, (rows, cols) in enumerate(((up_rows, up_cols), (down_rows, down_cols))):
        both = jnp.dot(rows[...], cols[...], preferred_element_type=jnp.float32)
        low, top = both[:, :lanes], both[:, lanes:]
        put(refs, wide_count, [pair], {pair: 0}, member, jnp.where(flip, low, top))
        put(refs, wide_count, [pair], {pair: 1}, member, jnp.where(flip, top, low))


def ffn_weight_grads(up_rows, down_rows, up_cols, down_cols, wide_count):
    whole = pl.BlockSpec(up_rows.shape, lambda step, here: (0, 0))
    cols = pl.BlockSpec((up_cols.shape[0], 2 * lanes), lambda step, here: (0, step ^ here[0]))
    kernel = functools.partial(ffn_grads_kernel, wide_count=wide_count)
    operands = (up_rows, down_rows, up_cols, down_cols)
    specs = [whole, whole, cols, cols]
    return weight_grads(kernel, operands, specs, [("pair", 1)], wide_count, 2, wide_count)


def attn_grads_kernel(here, one_rows, two_rows, one_cols, two_cols, *refs, wide_count):
    swap = here[0] % 2 == 0
    flip = here[1] == 0
    pair, near = ("pair", 1), ("wide", 1)
    blocks = []
    for rows, cols in ((one_rows, one_cols), (two_rows, two_cols)):
        both = jnp.dot(rows[...], cols[...], preferred_element_type=jnp.float32)
        low, top = both[:, :lanes], both[:, lanes:]
        blocks.append((jnp.where(swap, low, top), jnp.where(swap, top, low)))
    for step in range(2):
        one, two = blocks[0][step], blocks[1][step]
        first, second = jnp.where(flip, one, two), jnp.where(flip, two, one)
        put(refs, wide_count, [pair, near], {pair: 0, near: step}, 0, first)
        put(refs, wide_count, [pair, near], {pair: 1, near: step}, 0, second)


def attn_weight_grads(one_rows, two_rows, one_cols, two_cols, wide_count):
    whole = pl.BlockSpec(one_rows.shape, lambda step, here: (0, 0))
    cols = pl.BlockSpec((one_cols.shape[0], 2 * lanes), lambda step, here: (0, step ^ here[0] // 2))
    kernel = functools.partial(attn_grads_kernel, wide_count=wide_count)
    operands = (one_rows, two_rows, one_cols, two_cols)
    specs = [whole, whole, cols, cols]
    covered = [("pair", 1), ("wide", 1)]
    return weight_grads(kernel, operands, specs, covered, wide_count // 2, 1, wide_count)


def in_routes(blocks, wide_count):
    count = wide_count * 2
    order = jnp.arange(count) ^ here16()
    blocks = jnp.take(blocks.reshape((count,) + blocks.shape[2:]), order, axis=0)
    bits = wide_bits(wide_count)[::-1] + [("pair", 1)]
    parts = []
    for route, (start, stop) in zip(routes(wide_count), cuts(D, tile)):
        part = blocks[:, :, start:stop].reshape((2,) * len(bits) + blocks[:, :, start:stop].shape[1:])
        dims = [bits.index(bit) for bit in route]
        parts.append(part.transpose(dims + list(range(len(bits), part.ndim))))
    return parts


def gather_blocks(block, wide_count, axis, unit):
    bits = wide_bits(wide_count)[::-1] + [("pair", 1)]
    parts = []
    for route, (start, stop) in zip(routes(wide_count), cuts(block.shape[axis], unit)):
        part = lax.slice_in_dim(block, start, stop, axis=axis)
        have = []
        for bit in route[::-1]:
            have = sorted(have + [bit], key=bits.index)
            part = double(part, bit, have.index(bit))
        parts.append(part.reshape((wide_count, 2) + part.shape[len(bits) :]))
    return jnp.concatenate(parts, axis=2 + axis)


def select_rows(index, rows, precision=None):
    hits = index[:, None] == jnp.arange(rows.shape[0], dtype=jnp.int32)[None, :]
    return jnp.dot(
        hits.astype(rows.dtype), rows, precision=precision, preferred_element_type=jnp.float32
    )


def logit_grads_kernel(facts, logits_ref, source_ref, rows_ref, grad_ref, loss_ref, dec_ref):
    step = pl.program_id(0)

    @pl.when(step == 0)
    def _():
        loss_ref[...] = jnp.zeros_like(loss_ref)
        dec_ref[...] = jnp.zeros_like(dec_ref)

    columns = lax.broadcasted_iota(jnp.int32, logits_ref.shape, 1) + facts[0]
    is_word = columns < V
    rows = rows_ref[...]
    log_prob = logits_ref[...] - rows[:, 0:1]
    source_log = source_ref[0].astype(jnp.float32) - rows[:, 1:2]
    source_prob = jnp.where(is_word, jnp.exp(source_log), 0.0)
    hits = columns == rows[:, 3:4].astype(jnp.int32)
    keep = is_word & (rows[:, 2:3] > 0.5)
    losses = source_prob * (source_log - log_prob) - jnp.where(hits, log_prob, 0.0)
    loss_ref[...] += jnp.sum(jnp.where(keep, losses, 0.0), axis=0, keepdims=True)
    grads = 2.0 * jnp.exp(log_prob) - jnp.where(hits, 1.0, 0.0) - source_prob
    grads = jnp.where(keep, grads, 0.0).astype(jnp.bfloat16)
    grad_ref[...] = grads
    dec_ref[...] += jnp.sum(grads.astype(jnp.float32), axis=0, keepdims=True)


def logit_grads(facts, logits, source, row_facts, devices):
    owned = logits.shape[1]
    group = devices // 2

    def source_block(step, facts):
        return ((step % group ^ facts[1]) * 2 + (step // group ^ facts[2]), 0, 0)

    line = pl.BlockSpec((1, owned), lambda step, facts: (0, 0))
    grads, losses, dec = pl.pallas_call(
        logit_grads_kernel,
        grid_spec=pltpu.PrefetchScalarGridSpec(
            num_scalar_prefetch=1,
            grid=(devices,),
            in_specs=[
                pl.BlockSpec((MPW, owned), lambda step, facts: (step, 0)),
                pl.BlockSpec((1, MPW, owned), source_block),
                pl.BlockSpec((MPW, 4), lambda step, facts: (step, 0)),
            ],
            out_specs=[pl.BlockSpec((MPW, owned), lambda step, facts: (step, 0)), line, line],
        ),
        out_shape=[
            jax.ShapeDtypeStruct(logits.shape, jnp.bfloat16),
            jax.ShapeDtypeStruct((1, owned), jnp.float32),
            jax.ShapeDtypeStruct((1, owned), jnp.float32),
        ],
    )(facts, logits, source, row_facts)
    return grads, losses, dec[0]


def pick_rows(values, index):
    hits = index[:, None] == jnp.arange(values.shape[0], dtype=jnp.int32)[None, :]
    return jnp.sum(jnp.where(hits[:, :, None], values[None], 0), axis=1)


def add_rows(index, rows, count):
    hits = jnp.arange(count, dtype=jnp.int32)[:, None] == index[None, :]
    return jnp.dot(
        hits.astype(rows.dtype), rows, precision=high, preferred_element_type=jnp.float32
    )


def position_plan(devices, owned):
    group = devices // 2
    place = np.arange(SEQ)
    owner = (V + place) // owned
    target = 2 * (place % WINDOW % group) + place // WINDOW
    rank = np.zeros(SEQ, np.int64)
    seen = {}
    for p in range(SEQ):
        pair = (owner[p], target[p])
        rank[p] = seen.get(pair, 0)
        seen[pair] = rank[p] + 1
    assert rank.max() < slots
    return owner, target, rank


def flat_blocks(size, devices):
    total = size * devices
    starts = [dev * size // (tile * lanes) * tile for dev in range(devices)] + [total // lanes]
    ends = [-(-(dev + 1) * size // (tile * lanes)) * tile for dev in range(devices)]
    rows = max(end - start for start, end in zip(starts, ends))
    return starts, rows


def place_flat(share, device, devices):
    size = share.shape[0]
    _, rows = flat_blocks(size, devices)
    offset = device * size % (tile * lanes)
    block = lax.dynamic_update_slice(jnp.zeros((rows * lanes,), share.dtype), share, (offset,))
    return block.reshape(rows, lanes)


def join_flat(blocks, size):
    devices, rows = blocks.shape[:2]
    starts, _ = flat_blocks(size, devices)
    pieces, carry = [], None
    for dev in range(devices):
        length = starts[dev + 1] - starts[dev]
        first = blocks[dev, :tile] if carry is None else blocks[dev, :tile] + carry
        pieces += [first, blocks[dev, tile:length]]
        carry = blocks[dev, length : length + tile] if length < rows else None
    return jnp.concatenate(pieces)


def scatter_flat(flat_rows, size, device, devices):
    wide_count = lax.axis_size("wide")
    starts, rows = flat_blocks(size, devices)
    padded = jnp.pad(flat_rows, ((0, rows), (0, 0)))
    blocks = jnp.stack([padded[starts[dev] : starts[dev] + rows] for dev in range(devices)])
    bits = wide_bits(wide_count)[::-1] + [("pair", 1), side_bit]
    part = blocks.reshape((2,) * len(bits) + blocks.shape[1:])
    for bit in [side_bit] + routes(wide_count)[0]:
        part = halve(part, bit, bits.index(bit))
        bits.remove(bit)
    return lax.dynamic_slice(part.reshape(-1), (device * size % (tile * lanes),), (size,))


def shards(
    token_ids,
    live_lengths,
    key_keep,
    buckets,
    mask_pos,
    mask_labels,
    mask_counts,
    source_logits,
    embed_table,
    embed_first,
    embed_second,
    attn_mats,
    attn_moment,
    ffn_mats,
    ffn_moment,
    other_params,
    other_first,
    other_second,
):
    wide_count = lax.axis_size("wide")
    narrow_count = lax.axis_size("pair") * 2
    devices = wide_count * narrow_count
    device = lax.axis_index(everyone).astype(jnp.int32)
    owned = embed_table.shape[0]
    size = other_params.shape[0]
    col_width = attn_mats.shape[2]
    ffn_width = ffn_mats.shape[2]
    kinds = attn_mats.shape[0]
    table_low = embed_table.astype(jnp.bfloat16)

    attn_own = attn_mats.astype(jnp.bfloat16)
    other_own = place_flat(other_params.astype(jnp.bfloat16), device, devices)
    if col_width == lanes:
        merged = jnp.concatenate([attn_own.reshape(-1, lanes), other_own])
        merged = lax.all_gather(merged, everyone)
        attn_all, other_all = merged[:, : kinds * D], merged[:, kinds * D :]
    else:
        attn_all = lax.all_gather(attn_own, everyone)
        other_all = lax.all_gather(other_own, everyone)
    other_flat = join_flat(other_all, size)
    attn_all = attn_all.reshape(wide_count, narrow_count * kinds, D, col_width)
    attn_low = attn_all.transpose(1, 2, 0, 3).reshape(narrow_count * kinds, D, D)
    ffn_all = lax.all_gather(ffn_mats.astype(jnp.bfloat16), everyone)
    bias_rows = V // lanes
    up_rows = bias_rows + L * FF // lanes
    vec_rows = up_rows + NV * D // lanes
    dec_bias = lax.dynamic_slice(other_flat.reshape(-1), (device * owned,), (owned,))
    dec_bias = dec_bias.astype(jnp.float32)
    up_biases = other_flat[bias_rows:up_rows].reshape(devices // 2, 2, ffn_width)
    up_biases = up_biases.transpose(1, 0, 2).reshape(L, FF).astype(jnp.float32)
    vectors = other_flat[up_rows:vec_rows].reshape(NV, D).astype(jnp.float32)
    head_weight = other_flat[vec_rows:].reshape(D, D)

    win_count = token_ids.shape[0]
    assert win_count == 1 and SEQ == 2 * WINDOW
    group = devices // 2
    per_place = WINDOW // group
    half = device % 2
    owner_of, target_of, rank_of = position_plan(devices, owned)
    tokens = token_ids.reshape(-1)
    token_owner = tokens // owned
    token_local = tokens - token_owner * owned
    order = jnp.arange(WINDOW, dtype=jnp.int32)
    earlier = order[None, :] < order[:, None]
    same = tokens[:, None] == tokens[None, :]
    is_first = ~jnp.any(same & earlier, axis=1)
    same_owner = token_owner[:, None] == token_owner[None, :]
    rank = jnp.sum((same_owner & earlier & is_first[None, :]).astype(jnp.int32), axis=1)
    taken = np.zeros((devices, devices), np.int32)
    np.add.at(taken, (target_of, owner_of), 1)
    taken_here = lax.dynamic_index_in_dim(jnp.asarray(taken), device, 0, keepdims=False)
    owners = jnp.arange(devices, dtype=jnp.int32)
    offset = jnp.sum(jnp.where(token_owner[:, None] == owners[None, :], taken_here[None], 0), 1)
    first_slot = jnp.where(is_first, offset + rank, 0)
    slot = jnp.sum(jnp.where(same & is_first[None, :], first_slot[None, :], 0), axis=1)

    def address(round_idx):
        there = slot - round_idx * slots
        return jnp.where((there >= 0) & (there < slots), token_owner * slots + there, -1)

    def requests(addresses):
        cells = jnp.arange(devices * slots, dtype=jnp.int32)
        hits = (cells[:, None] == addresses[None, :]) & is_first[None, :]
        return jnp.sum(jnp.where(hits, token_local[None, :] + 1, 0), axis=1)

    now = address(0)
    labels_at = slots + 2
    message = jnp.concatenate(
        [
            requests(now).reshape(devices, slots),
            jnp.broadcast_to(jnp.max(slot)[None, None], (devices, 1)),
            jnp.broadcast_to(mask_counts.reshape(1, 1), (devices, 1)),
            jnp.broadcast_to(mask_labels.reshape(1, MPW), (devices, MPW)),
            jnp.zeros((devices, lanes - labels_at - MPW), jnp.int32),
        ],
        axis=1,
    )
    message = swap_all(message)
    rounds = jnp.max(message[:, slots]) // slots + 1
    counts_all = message[:, slots + 1]
    labels_all = message[:, labels_at : labels_at + MPW].reshape(-1)
    masked_total = jnp.sum(counts_all).astype(jnp.float32)
    place = np.arange(SEQ)
    cell_of = jnp.asarray(target_of * slots + rank_of, jnp.int32)
    local_of = jnp.asarray(V + place - owner_of * owned + 1, jnp.int32)
    mine = jnp.asarray(owner_of, jnp.int32) == device
    cells = jnp.arange(devices * slots, dtype=jnp.int32)
    place_hits = (cells[:, None] == cell_of[None, :]) & mine[None, :]
    place_rows = jnp.sum(jnp.where(place_hits, local_of[None, :], 0), axis=1)
    asked = message[:, :slots].reshape(-1) + place_rows - 1
    held = (owner_of * slots + rank_of).reshape(2, per_place, group).transpose(0, 2, 1)
    held = jnp.asarray(held.reshape(devices, per_place), jnp.int32)
    held = lax.dynamic_index_in_dim(held, half * group + device // 2, 0, keepdims=False)

    def fetch(asked_rows):
        rows = select_rows(asked_rows, table_low).astype(jnp.bfloat16)
        return swap_all(rows.reshape(devices, slots, D)).reshape(-1, D)

    def ask_again(addresses):
        return swap_all(requests(addresses).reshape(devices, slots)).reshape(-1) - 1

    fetched = fetch(asked)
    source_own = source_logits.reshape(MPW, V)
    source_max = jnp.max(source_own, axis=1).astype(jnp.float32)
    source_sum = jnp.sum(jnp.exp(source_own.astype(jnp.float32) - source_max[:, None]), axis=1)
    source_total = source_max + jnp.log(source_sum)
    source_cut = jnp.pad(source_own, ((0, 0), (0, devices * owned - V)))
    source_cut = source_cut.reshape(MPW, devices, owned).transpose(1, 0, 2)
    fetched, source_cut, source_total = lax.optimization_barrier(
        (fetched, source_cut, source_total)
    )
    ffn_all, source_cut = lax.optimization_barrier((ffn_all, source_cut))
    ffn_low = ffn_all.reshape(devices // 2, 2, 2 * L, D, ffn_width)
    ffn_low = ffn_low.transpose(2, 3, 1, 0, 4).reshape(2 * L, D, FF)
    source_here = swap_all(source_cut)
    token_rows = select_rows(now, fetched)
    place_part = select_rows(held, fetched).astype(jnp.bfloat16)
    place_all = gather_blocks(place_part, wide_count, 1, 128).reshape(group, per_place, D)
    place_all = place_all.transpose(1, 0, 2).reshape(WINDOW, D).astype(jnp.float32)

    def more_rows(state):
        round_idx, rows = state
        addresses = address(round_idx)
        return (round_idx + 1, rows + select_rows(addresses, fetch(ask_again(addresses))))

    _, token_rows = lax.while_loop(
        lambda state: state[0] < rounds, more_rows, (jnp.int32(1), token_rows)
    )

    is_valid = (order[None, :] < live_lengths[:, None]) & (key_keep == 1)
    key_ok = is_valid.reshape(win_count, 1, 1, 1, WINDOW)
    bucket_ids = buckets.reshape(win_count, 1, WINDOW)
    same_bucket = bucket_ids[:, :, None, :, None] == bucket_ids[:, :, None, None, :]
    allowed = same_bucket & key_ok | jnp.eye(WINDOW, dtype=bool)
    embedded = (token_rows + place_all).reshape(win_count, WINDOW, D)
    hidden, embed_pull = jax.vjp(layer_norm, embedded, vectors[0], vectors[1])
    params = (
        attn_low[0],
        attn_low[1],
        attn_low[2],
        attn_low[3],
        ffn_low[0],
        ffn_low[1],
        up_biases[0],
        vectors[2:10],
    )
    hidden, stored = layer_forward(hidden, params, allowed)
    picks = mask_pos.reshape(-1)
    head_in = select_rows(picks, hidden.reshape(WINDOW, D).astype(jnp.bfloat16))
    head_in = head_in.astype(jnp.bfloat16)
    head_pre = jnp.dot(head_in, head_weight, preferred_element_type=jnp.float32) + vectors[NV - 3]
    head_out, head_pull = jax.vjp(head_tail, head_pre, vectors[NV - 2], vectors[NV - 1])
    head_low = head_out.astype(jnp.bfloat16)

    rows_all = devices * MPW
    side = lax.axis_index("side").astype(jnp.int32)
    here = here16().astype(jnp.int32)
    order_rows = jnp.arange(devices, dtype=jnp.int32)
    rank_of_dev = (order_rows % 2 ^ side) * group + (order_rows // 2 ^ here)
    dev_of_rank = (order_rows % group ^ here) * 2 + (order_rows // group ^ side)
    head_all = gather_relative(head_low, wide_count, 1, lanes)
    head_all = jnp.concatenate([head_all, exchange(head_all, side_bit)]).reshape(rows_all, D)
    labels_all = pick_rows(labels_all.reshape(devices, MPW), dev_of_rank).reshape(rows_all, 1)
    is_live = jnp.arange(MPW, dtype=jnp.int32)[None, :] < pick_rows(counts_all[:, None], dev_of_rank)
    word_ids = device * owned + jnp.arange(owned, dtype=jnp.int32)
    is_word = (word_ids < V)[None, :]
    logits = jnp.einsum("rd,vd->rv", head_all, table_low, preferred_element_type=jnp.float32)
    logits = jnp.where(is_word, logits + dec_bias[None, :], masked_fill)
    top_here = jnp.max(logits, axis=1)
    sum_here = jnp.sum(jnp.exp(logits - top_here[:, None]), axis=1)
    stats = jnp.concatenate(
        [
            top_here.reshape(devices, MPW),
            sum_here.reshape(devices, MPW),
            jnp.zeros((devices, 2 * lanes - 2 * MPW), jnp.float32),
        ],
        axis=1,
    )
    stats, source_here = lax.optimization_barrier((stats, source_here))
    stats = swap_all(pick_rows(stats, rank_of_dev))
    tops = stats[:, :MPW]
    top = jnp.max(tops, axis=0)
    total = top + jnp.log(jnp.sum(stats[:, MPW : 2 * MPW] * jnp.exp(tops - top[None]), axis=0))
    totals = spread(jnp.concatenate([total, source_total]), devices)
    totals = pick_rows(totals, dev_of_rank)
    row_facts = jnp.concatenate(
        [
            totals[:, :MPW].reshape(rows_all, 1),
            totals[:, MPW:].reshape(rows_all, 1),
            is_live.reshape(rows_all, 1).astype(jnp.float32),
            labels_all.astype(jnp.float32),
        ],
        axis=1,
    )
    place_facts = jnp.stack([device * owned, here, side]).astype(jnp.int32)
    grad_logits, losses, grad_dec = logit_grads(
        place_facts, logits, source_here, row_facts, devices
    )
    loss_part = jnp.sum(losses)
    give = jnp.dot(grad_logits[rows_all // 2 :], table_low, preferred_element_type=jnp.float32)
    got = exchange(give, side_bit)
    keep = jnp.dot(grad_logits[: rows_all // 2], table_low, preferred_element_type=jnp.float32)
    grad_head_out = reduce_rows((keep + got).reshape(group, MPW, D), wide_count)
    grad_words = jnp.einsum("rv,rd->vd", grad_logits, head_all, preferred_element_type=jnp.float32)

    grad_pre, grad_head_gain, grad_head_shift = head_pull(grad_head_out)
    pre_low = grad_pre.astype(jnp.bfloat16)
    grad_head_w = jnp.einsum("rd,rf->df", head_in, pre_low, preferred_element_type=jnp.float32)
    grad_head_in = jnp.einsum("rf,df->rd", pre_low, head_weight, preferred_element_type=jnp.float32)
    grad_hidden = add_rows(picks, grad_head_in, WINDOW).reshape(win_count, WINDOW, D)
    grad_hidden, layer_mats, up_grad, vec_grads = layer_backward(
        grad_hidden, stored, params, allowed
    )
    grad_embed, grad_emb_gain, grad_emb_shift = embed_pull(grad_hidden)
    flat_embed = grad_embed.reshape(WINDOW, D)

    ffn_grad = jnp.concatenate(reduce_relative(layer_mats[1], wide_count), axis=1)
    attn_grad = jnp.concatenate(reduce_relative(layer_mats[0], wide_count), axis=1)
    dec_block = jnp.zeros((devices * owned,), jnp.float32)
    dec_block = lax.dynamic_update_slice(dec_block, grad_dec, (device * owned,))[:V]
    vector_block = jnp.concatenate(
        [jnp.stack([grad_emb_gain, grad_emb_shift])]
        + [vec_grads]
        + [jnp.stack([jnp.sum(pre_low.astype(jnp.float32), 0), grad_head_gain, grad_head_shift])],
        axis=0,
    )
    grad_other = jnp.concatenate(
        [
            dec_block.reshape(-1, lanes),
            up_grad.reshape(2, devices // 2, ffn_width).transpose(1, 0, 2).reshape(-1, lanes),
            vector_block.reshape(-1, lanes),
            grad_head_w.reshape(-1, lanes),
        ]
    )
    other_grad = scatter_flat(grad_other, size, device, devices)

    place_grad = flat_embed.reshape(per_place, group, D).transpose(1, 0, 2)
    place_grad = place_grad.reshape(wide_count, narrow_count // 2, per_place, D)
    place_grad = reduce_blocks(place_grad, wide_count, 1, 128)
    sent = add_rows(now, flat_embed, devices * slots) + add_rows(held, place_grad, devices * slots)
    arrived = swap_all(sent.reshape(devices, slots, D)).reshape(-1, D)
    table_grad = grad_words + add_rows(asked, arrived, owned)

    def more_grads(state):
        round_idx, grads = state
        addresses = address(round_idx)
        asked_rows = ask_again(addresses)
        sent = add_rows(addresses, flat_embed, devices * slots)
        arrived = swap_all(sent.reshape(devices, slots, D)).reshape(-1, D)
        return (round_idx + 1, grads + add_rows(asked_rows, arrived, owned))

    _, table_grad = lax.while_loop(
        lambda state: state[0] < rounds, more_grads, (jnp.int32(1), table_grad)
    )

    squares = square_sum((table_grad, attn_grad, ffn_grad, other_grad))
    sums = jnp.sum(spread(jnp.stack([squares, loss_part]), devices), axis=0)
    grad_norm = jnp.sqrt(sums[0]) / masked_total
    loss_value = sums[1] / masked_total
    factor = jnp.minimum(1.0, clip_limit / grad_norm)
    scaling = factor / masked_total

    attn_moment_new = mu_muon * attn_moment + attn_grad * scaling
    ffn_moment_new = mu_muon * ffn_moment + ffn_grad * scaling
    second = lax.axis_index("side") == 1
    keep = jnp.where(second, ffn_moment_new[1], ffn_moment_new[0])
    got = exchange(jnp.where(second, ffn_moment_new[0], ffn_moment_new[1]), side_bit)
    ffn_pair = jnp.concatenate([keep, got], axis=1)[None]
    ffn_found = gather_columns(ffn_pair, True)
    attn_found = gather_columns(attn_moment_new, False)
    ffn_found, attn_found = lax.optimization_barrier((ffn_found, attn_found))
    attn_new = muon_cols(attn_mats, attn_moment_new, gram_of(attn_found), D)
    ffn_turn = newton_cols(ffn_pair, gram_of(ffn_found))[0]
    keep, give = ffn_turn[:, :ffn_width], ffn_turn[:, ffn_width:]
    got = exchange(give, side_bit)
    ffn_turn = jnp.stack([jnp.where(second, got, keep), jnp.where(second, keep, got)])
    ffn_new = ffn_mats - lr_muon * muon_shape * math.sqrt(max(D, FF)) * ffn_turn
    embed_new, embed_first_new, embed_second_new = adam_step(
        embed_table, embed_first, embed_second, table_grad * scaling
    )
    other_new, other_first_new, other_second_new = adam_step(
        other_params, other_first, other_second, other_grad * scaling
    )
    return (
        loss_value,
        grad_norm,
        embed_new,
        embed_first_new,
        embed_second_new,
        attn_new,
        attn_moment_new,
        ffn_new,
        ffn_moment_new,
        other_new,
        other_first_new,
        other_second_new,
    )


def solution(mesh):
    wide_count, narrow_count = mesh.shape["wide"], mesh.shape["narrow"]
    assert narrow_count % 2 == 0
    split = Mesh(
        np.asarray(mesh.devices).reshape(wide_count, narrow_count // 2, 2), everyone
    )
    rows, narrow = P(everyone), ("pair", "side")
    attn_spec, ffn_spec = P(narrow, None, "wide"), P(None, None, everyone)
    in_specs = (rows,) * 11 + (attn_spec,) * 2 + (ffn_spec,) * 2 + (rows,) * 3
    out_specs = (P(), P()) + (rows,) * 3 + (attn_spec,) * 2 + (ffn_spec,) * 2 + (rows,) * 3

    return jax.shard_map(
        shards, mesh=split, in_specs=in_specs, out_specs=out_specs, check_vma=False
    )
```

time: 3900 us -> 1760 us (0.45)
  waiting for transfers between devices: 2980 us -> 765 us
  local copies, waits for them, and re-layouts: 132 us -> 280 us
  starting transfers between devices: 1.61 us -> 136 us
  matrix products: 423 us -> 311 us
  other arithmetic: 274 us -> 166 us
  Pallas kernels: 0 us -> 53.9 us
  blocking collectives: 47 us -> 0 us
    unnamed x18 -> x2, waiting for transfers between devices: 1770 us -> 0.03 us
    psum x6 -> x0, waiting for transfers between devices: 750 us -> none  [the longest x3 517 us: ffn_gram(): return lax.psum(gram_part, ('wide', 'narrow'))]
    ppermute x0 -> x110, waiting for transfers between devices: none -> 695 us  [exchange(): return lax.ppermute(values, axis, steps)]
    reduce_scatter x2 -> x0, waiting for transfers between devices: 340 us -> none  [the longest x1 340 us: shards(): lax.psum_scatter(grad_ffn, ('wide', 'narrow'), scatter_dimension=2, tiled...]
    scatter-add x2 -> x0, other arithmetic: 154 us -> none  [the longest x1 151 us: shards(): grad_table.at[table_rows]]
    all_gather x4 -> x2, waiting for transfers between devices: 124 us -> 0.04 us  [the longest x1 0.02 us: shards(): merged = lax.all_gather(merged, everyone)]
    ppermute x0 -> x110, starting transfers between devices: none -> 101 us  [exchange(): return lax.ppermute(values, axis, steps)]
    dot_general x27 -> x34, matrix products: 231 us -> 130 us  [the longest x8 17.1 us: slab_product(): jnp.einsum('kde,kec->kdc', matrix, columns, precision=high, preferred_ele...]
  transfers between devices with their start and end apart: 15 -> 119, of which waited for: 11 -> 67; matrix products, arithmetic and copies ran while one was open for 14% -> 27% of each run, Pallas kernels for 0% -> 1%
where the time goes in v1:
time: 1760 us; the launch traced here: 1740 us
  waiting for transfers between devices  765 us (43%)
  matrix products  311 us (18%)
  local copies, waits for them, and re-layouts  280 us (16%)
  other arithmetic  166 us (9%)
  starting transfers between devices  136 us (8%)
  Pallas kernels  53.9 us (3%)
  between operations  31.2 us (2%)
    ppermute x110, waiting for transfers between devices, exchange(): return lax.ppermute(values, axis, steps)  695 us
    ppermute x110, starting transfers between devices, exchange(): return lax.ppermute(values, axis, steps)  101 us
    all_to_all x7, waiting for transfers between devices, swap_all(): return lax.all_to_all(blocks, axes, 0, 0, tiled=True)  70.3 us
    dot_general x6, matrix products, project(): jnp.einsum('bsd,df->bsf', inputs, weight, preferred_element_type=jnp.floa...  53.2 us
    unnamed x487, local copies, waits for them, and re-layouts  46 us
    another operation x29, local copies, waits for them, and re-layouts, scatter_flat(): jnp.stack([padded[starts[dev]:starts[dev] + rows] for dev in range(device...  44.6 us
  transfers between devices with their start and end apart: 119, of which 67 were waited for; matrix products, arithmetic and copies ran while one was open for 27% of the time, Pallas kernels for 1%

profile of v1, /device:TPU:0, one launch (start us, length us, event | category | flops | bytes accessed | tf_op | source)
XLA Modules:
  0.0 1743.8 jit_solution(672998695370195687)
XLA Ops:
  53.1 10.3 reshape.1716
  63.4 7.7 copy.506
  80.9 47.9 %all-to-all-done.5 = bf16[32,32,1024]{2,1,0:T(8,128)(2,1)S(1)} async-done(((bf16[32,32,1024]{2,1,0:T(8,128)(2,1)}), bf16[32,32,1024]{2,1,0:T(8,128)(2,1)S(1)}, u32[]{:S(2)}, u32[]{:S(2)}) %all-to-all-start.5) | async-done | bytes 2097184 | tf_op jit(solution)/shard_map/all_to_all | solution.py:303
  166.6 8.0 slice.1282
  273.8 8.8 fusion.17
  282.6 9.3 exponential_reduce_fusion
  291.9 8.2 convolution_convert_fusion.1
  303.8 11.6 fusion.334
  315.3 11.9 copy.399
  327.2 11.9 copy.401
  339.1 28.0 %multiply_convert_fusion.1 = (bf16[512,4096]{1,0:T(8,128)(2,1)S(1)}, f32[512,4096]{1,0:T(8,128)}, f32[512,4096]{1,0:T(8,128)}) fusion(f32[4096]{0:T(1024)S(1)} %bitcast.1417, bf16[1024,4096]{0,1:T(8,128)(2,1)} %bitcast.1289, f32[512,1024]{1,0:T(8,128)} %copy-done.2, f32[1024]{0:T(1024)S(1)} %get-tuple-element.590, f32[1024]{0:T(1024)S(1)} %get-tuple-element.591, ...), kind=kOutput, calls=%fused_computation.45 | convolution fusion | flops 4436000768 | bytes 31485952 | tf_op jit(solution)/shard_map/bsd,df->bsf/dot_general | solution.py:60
  390.8 14.3 collective-permute-done.20
  412.1 87.8 %collective-permute-done.12 = bf16[1,80,384]{2,1,0:T(8,128)(2,1)S(1)} collective-permute-done((bf16[1,80,384]{2,1,0:T(8,128)(2,1)S(1)}, bf16[1,80,384]{2,1,0:T(8,128)(2,1)S(1)}, u32[]{:S(2)}, u32[]{:S(2)}) %collective-permute-start.12) | collective-permute-done | bytes 61472 | tf_op jit(solution)/shard_map/ppermute | solution.py:330
  540.9 11.6 fusion.349
  586.7 26.1 %shard_map.310 = (bf16[2560,992]{1,0:T(8,128)(2,1)}, f32[1,992]{1,0:T(1,128)}, f32[1,992]{1,0:T(1,128)}) custom-call(s32[3]{0:T(128)} %pad_add_fusion.facts, f32[2560,992]{1,0:T(8,128)} %get-tuple-element.612.logits_ref, bf16[32,80,992]{2,1,0:T(8,128)(2,1)} %all-to-all-done.6.source_ref, f32[2560,4]{1,0:T(8,128)} %copy.407.rows_ref), custom_call_target="tpu_custom_call" | custom-call | tf_op jit(solution)/shard_map/pallas_call | solution.py:555
  612.8 7.6 fusion.79
  637.7 15.1 collective-permute-done.34
  656.3 13.3 collective-permute-done.35
  671.1 22.2 %collective-permute-done.30 = f32[2,2,2,80,384]{4,3,2,0,1:T(8,128)S(1)} collective-permute-done((f32[2,2,2,80,384]{4,3,2,0,1:T(8,128)S(1)}, f32[2,2,2,80,384]{4,3,2,0,1:T(8,128)S(1)}, u32[]{:S(2)}, u32[]{:S(2)}) %collective-permute-start.30) | collective-permute-done | bytes 983072 | tf_op jit(solution)/shard_map/ppermute | solution.py:330
  695.6 11.8 collective-permute-done.37
  707.6 13.5 collective-permute-done.31
  728.6 12.8 collective-permute-done.32
  760.1 13.1 convert_reduce_fusion
  877.8 17.2 shard_map.311
  895.0 11.5 fusion.82
  915.4 9.5 fusion.353
  925.0 9.7 convert_reduce_fusion.3
  934.6 24.8 %fusion.129 = bf16[16,64,512]{2,1,0:T(8,128)(2,1)} fusion(bf16[512,16,64]{0,2,1:T(8,128)(2,1)} %bitcast.1335, f32[16,512,512]{1,2,0:T(8,128)} %fusion.353, f32[16,512,512]{1,2,0:T(8,128)} %get-tuple-element.604, f32[16,512]{1,0:T(8,128)} %copy-done.117, pred[512,512]{0,1:T(8,128)(4,1)S(1)} %copy-done.49), kind=kOutput, calls=%fused_computation.230 | convolution fusion | flops 583541248 | bytes 35946496 | tf_op jit(solution)/shard_map/bnhqk,bnqhe->bnkhe/dot_general | solution.py:198
  959.5 27.8 %broadcast_select_fusion.1 = (bf16[16,64,512]{2,1,0:T(8,128)(2,1)}, bf16[16,64,512]{2,1,0:T(8,128)(2,1)}, bf16[16,64,512]{2,1,0:T(8,128)(2,1)}) fusion(bf16[16,64,512]{2,1,0:T(8,128)(2,1)} %fusion.129, pred[]{:T(512)S(6)} %eq.526, bf16[512,16,64]{0,2,1:T(8,128)(2,1)S(1)} %bitcast.1333, f32[16,512,512]{1,2,0:T(8,128)} %fusion.353, ...), kind=kOutput, calls=%fused_computation.305 | convolution fusion | flops 584589824 | bytes 39092224 | tf_op jit(solution)/shard_map/bnhqk,bnkhe->bnqhe/dot_general | solution.py:194
  1057.6 33.1 %collective-permute-done.46 = f32[2,2,2,32,384]{4,2,1,0,3:T(2,128)S(1)} collective-permute-done((f32[2,2,2,32,384]{4,2,1,0,3:T(2,128)}, f32[2,2,2,32,384]{4,2,1,0,3:T(2,128)S(1)}, u32[]{:S(2)}, u32[]{:S(2)}) %collective-permute-start.46) | collective-permute-done | bytes 393248 | tf_op jit(solution)/shard_map/ppermute | solution.py:330
  1136.3 10.6 shard_map.312
  1160.2 11.0 collective-permute-done.62
  1172.1 56.0 %collective-permute-done.66 = f32[2,2,2,1,336,128]{5,4,2,1,0,3:T(8,128)S(1)} collective-permute-done((f32[2,2,2,1,336,128]{5,4,2,1,0,3:T(8,128)S(1)}, f32[2,2,2,1,336,128]{5,4,2,1,0,3:T(8,128)S(1)}, u32[]{:S(2)}, u32[]{:S(2)}) %collective-permute-start.66) | collective-permute-done | bytes 1376288 | tf_op jit(solution)/shard_map/ppermute | solution.py:330
  1238.8 13.7 collective-permute-done.70
  1254.2 17.0 collective-permute-done.63
  1277.5 47.5 %collective-permute-done.64 = f32[2,1,336,128]{3,2,0,1:T(8,128)S(1)} collective-permute-done((f32[2,1,336,128]{3,2,0,1:T(8,128)S(1)}, f32[2,1,336,128]{3,2,0,1:T(8,128)S(1)}, u32[]{:S(2)}, u32[]{:S(2)}) %collective-permute-start.64) | collective-permute-done | bytes 344096 | tf_op jit(solution)/shard_map/ppermute | solution.py:330
  1338.0 69.5 %collective-permute-done.60 = f32[2,1,352,128]{3,2,0,1:T(8,128)S(1)} collective-permute-done((f32[2,1,352,128]{3,2,0,1:T(8,128)}, f32[2,1,352,128]{3,2,0,1:T(8,128)S(1)}, u32[]{:S(2)}, u32[]{:S(2)}) %collective-permute-start.60) | collective-permute-done | bytes 360480 | tf_op jit(solution)/shard_map/ppermute | solution.py:330
  1409.7 8.0 collective-permute-done.69
  1419.3 13.3 collective-permute-done.61
  1448.6 25.9 %collective-permute-done.86 = f32[288,128]{1,0:T(8,128)S(1)} collective-permute-done((f32[288,128]{1,0:T(8,128)S(1)}, f32[288,128]{1,0:T(8,128)S(1)}, u32[]{:S(2)}, u32[]{:S(2)}) %collective-permute-start.86) | collective-permute-done | bytes 147488 | tf_op jit(solution)/shard_map/ppermute | solution.py:330
  1485.2 10.4 collective-permute-done.73
  1503.7 8.8 convolution_add_fusion.2
  1538.7 8.6 divide_subtract_fusion
  1572.4 12.0 collective-permute-done.88
  1591.7 11.4 collective-permute-done.89
  1605.5 11.9 collective-permute-done.94
  1631.2 20.4 %collective-permute-done.95 = bf16[8,336,256]{2,1,0:T(8,128)(2,1)S(1)} collective-permute-done((bf16[8,336,256]{2,1,0:T(8,128)(2,1)S(1)}, bf16[8,336,256]{2,1,0:T(8,128)(2,1)S(1)}, u32[]{:S(2)}, u32[]{:S(2)}) %collective-permute-start.95) | collective-permute-done | bytes 1376288 | tf_op jit(solution)/shard_map/ppermute | solution.py:330
  1659.4 11.5 fusion.47
  (1189 shorter events, 799.0 us)
Async XLA Ops:
  7.2 159.5 %all-gather.5.cloned.1.call-start = ((), (), s32[]{:S(2)}) async-start(), calls=%async_computation.11 | async-start | bytes 11083776 | tf_op jit(solution)/shard_map/all_gather | solution.py:679
  40.0 88.8 %all-to-all-start.5 = ((bf16[32,32,1024]{2,1,0:T(8,128)(2,1)}), bf16[32,32,1024]{2,1,0:T(8,128)(2,1)S(1)}, u32[]{:S(2)}, u32[]{:S(2)}) async-start(bf16[32,32,1024]{2,1,0:T(8,128)(2,1)} %bitcast.1365), calls=%async_computation.5 | async-start | bytes 4194304 | tf_op jit(solution)/shard_map/all_to_all | solution.py:303
  44.0 259.8 %all-gather.7.cloned.1.call-start = ((), (), s32[]{:S(2)}) async-start(), calls=%async_computation.12 | async-start | bytes 17301504 | tf_op jit(solution)/shard_map/all_gather | solution.py:687
  374.2 184.4 %all-to-all-start.6 = ((bf16[32,80,992]{2,1,0:T(8,128)(2,1)}), bf16[32,80,992]{2,1,0:T(8,128)(2,1)}, u32[]{:S(2)}, u32[]{:S(2)}) async-start(bf16[32,80,992]{2,1,0:T(8,128)(2,1)} %bitcast.1210), calls=%async_computation.6 | async-start | bytes 10485760 | tf_op jit(solution)/shard_map/all_to_all | solution.py:303
  386.9 113.0 %collective-permute-start.12 = (bf16[1,80,384]{2,1,0:T(8,128)(2,1)S(1)}, bf16[1,80,384]{2,1,0:T(8,128)(2,1)S(1)}, u32[]{:S(2)}, u32[]{:S(2)}) collective-permute-start(bf16[1,80,384]{2,1,0:T(8,128)(2,1)S(1)} %get-tuple-element.554), channel_id=1, source_target_pairs={{0,16},{4,20},{8,24},{12,28},{16,0},{20,4},{24,8},{28,12},{1,17},{... | collective-permute-start | bytes 184328 | tf_op jit(solution)/shard_map/ppermute | solution.py:330
  389.3 110.7 %collective-permute-start.16 = (bf16[1,80,384]{2,1,0:T(8,128)(2,1)S(1)}, bf16[1,80,384]{2,1,0:T(8,128)(2,1)S(1)}, u32[]{:S(2)}, u32[]{:S(2)}) collective-permute-start(bf16[1,80,384]{2,1,0:T(8,128)(2,1)S(1)} %get-tuple-element.555), channel_id=1, source_target_pairs={{0,2},{2,0},{1,3},{3,1},{4,6},{6,4},{5,7},{7,5},{8,10},{10,8},{9,1... | collective-permute-start | bytes 184328 | tf_op jit(solution)/shard_map/ppermute | solution.py:330
  405.1 97.2 %collective-permute-start.21 = (bf16[2,80,256]{2,1,0:T(8,128)(2,1)S(1)}, bf16[2,80,256]{2,1,0:T(8,128)(2,1)S(1)}, u32[]{:S(2)}, u32[]{:S(2)}) collective-permute-start(bf16[2,80,256]{2,1,0:T(8,128)(2,1)S(1)} %pad_maximum_fusion.57), channel_id=1, source_target_pairs={{0,2},{2,0},{1,3},{3,1},{4,6},{6,4},{5,7},{7,5},{8,10},{10,8},{9,1... | collective-permute-start | bytes 245768 | tf_op jit(solution)/shard_map/ppermute | solution.py:330
  625.6 152.4 %collective-permute-start.38 = (bf16[1024,512]{0,1:T(8,128)(2,1)S(1)}, bf16[1024,512]{0,1:T(8,128)(2,1)}, u32[]{:S(2)}, u32[]{:S(2)}) collective-permute-start(bf16[1024,512]{0,1:T(8,128)(2,1)S(1)} %fusion.320), channel_id=1, source_target_pairs={{0,1},{1,0},{2,3},{3,2},{4,5},{5,4},{6,7},{7,6},{8,9},{9,8},{10,11... | collective-permute-start | bytes 3145736 | tf_op jit(solution)/shard_map/ppermute | solution.py:330
  628.1 156.7 %collective-permute-start.55 = (bf16[1024,512]{0,1:T(8,128)(2,1)}, bf16[1024,512]{0,1:T(8,128)(2,1)}, u32[]{:S(2)}, u32[]{:S(2)}) collective-permute-start(bf16[1024,512]{0,1:T(8,128)(2,1)} %get-tuple-element.519), channel_id=1, source_target_pairs={{0,1},{1,0},{2,3},{3,2},{4,5},{5,4},{6,7},{7,6},{8,9},{9,8},{10,11... | collective-permute-start | bytes 3145736 | tf_op jit(solution)/shard_map/ppermute | solution.py:330
  629.6 161.9 %collective-permute-start.54 = (bf16[1024,512]{0,1:T(8,128)(2,1)}, bf16[1024,512]{0,1:T(8,128)(2,1)}, u32[]{:S(2)}, u32[]{:S(2)}) collective-permute-start(bf16[1024,512]{0,1:T(8,128)(2,1)} %fusion.432), channel_id=1, source_target_pairs={{0,1},{1,0},{2,3},{3,2},{4,5},{5,4},{6,7},{7,6},{8,9},{9,8},{10,11... | collective-permute-start | bytes 3145736 | tf_op jit(solution)/shard_map/ppermute | solution.py:330
  637.2 33.2 %collective-permute-start.26 = (f32[2,2,2,80,384]{4,3,0,1,2:T(8,128)S(1)}, f32[2,2,2,80,384]{4,3,0,1,2:T(8,128)S(1)}, u32[]{:S(2)}, u32[]{:S(2)}) collective-permute-start(f32[2,2,2,80,384]{4,3,0,1,2:T(8,128)S(1)} %bitcast.1381), channel_id=1, source_target_pairs={{0,2},{2,0},{1,3},{3,1},{4,6},{6,4},{5,7},{7,5},{8,10},{10,8},{9,1... | collective-permute-start | bytes 2949128 | tf_op jit(solution)/shard_map/ppermute | solution.py:330
  707.3 91.3 %collective-permute-start.41 = (bf16[512,2048]{1,0:T(8,128)(2,1)}, bf16[512,2048]{1,0:T(8,128)(2,1)}, u32[]{:S(2)}, u32[]{:S(2)}) collective-permute-start(bf16[512,2048]{1,0:T(8,128)(2,1)} %get-tuple-element.510), channel_id=1, source_target_pairs={{0,1},{1,0},{2,3},{3,2},{4,5},{5,4},{6,7},{7,6},{8,9},{9,8},{10,11... | collective-permute-start | bytes 6291464 | tf_op jit(solution)/shard_map/ppermute | solution.py:330
  778.0 94.9 %collective-permute-start.40 = (bf16[512,2048]{1,0:T(8,128)(2,1)}, bf16[512,2048]{1,0:T(8,128)(2,1)}, u32[]{:S(2)}, u32[]{:S(2)}) collective-permute-start(bf16[512,2048]{1,0:T(8,128)(2,1)} %get-tuple-element.512), channel_id=1, source_target_pairs={{0,1},{1,0},{2,3},{3,2},{4,5},{5,4},{6,7},{7,6},{8,9},{9,8},{10,11... | collective-permute-start | bytes 6291464 | tf_op jit(solution)/shard_map/ppermute | solution.py:330
  805.2 61.0 %collective-permute-start.39 = (bf16[1024,512]{0,1:T(8,128)(2,1)S(1)}, bf16[1024,512]{0,1:T(8,128)(2,1)}, u32[]{:S(2)}, u32[]{:S(2)}) collective-permute-start(bf16[1024,512]{0,1:T(8,128)(2,1)S(1)} %bitcast.1343), channel_id=1, source_target_pairs={{0,1},{1,0},{2,3},{3,2},{4,5},{5,4},{6,7},{7,6},{8,9},{9,8},{10,11... | collective-permute-start | bytes 3145736 | tf_op jit(solution)/shard_map/ppermute | solution.py:330
  1014.8 141.5 %collective-permute-start.82 = (f32[2,2,2,2,288,128]{5,4,3,2,1,0:T(8,128)}, f32[2,2,2,2,288,128]{5,4,3,2,1,0:T(8,128)}, u32[]{:S(2)}, u32[]{:S(2)}) collective-permute-start(f32[2,2,2,2,288,128]{5,4,3,2,1,0:T(8,128)} %dynamic-slice_bitcast_fusion), channel_id=1, source_target_pairs={{0,1},{1,0},{2,3},{3,2},{4,5},{5,4},{6,7},{7,6},{8,9},{9,8},{10,11... | collective-permute-start | bytes 7077896 | tf_op jit(solution)/shard_map/ppermute | solution.py:330
  1020.5 208.1 %collective-permute-start.74 = (f32[2,2,2,2,336,128]{5,4,3,2,1,0:T(8,128)}, f32[2,2,2,2,336,128]{5,4,3,2,1,0:T(8,128)}, u32[]{:S(2)}, u32[]{:S(2)}) collective-permute-start(f32[2,2,2,2,336,128]{5,4,3,2,1,0:T(8,128)} %slice_bitcast_fusion.2), channel_id=1, source_target_pairs={{0,4},{4,0},{8,12},{12,8},{16,20},{20,16},{24,28},{28,24},{1,5},{5... | collective-permute-start | bytes 8257544 | tf_op jit(solution)/shard_map/ppermute | solution.py:330
  1024.6 107.3 %collective-permute-start.57 = (bf16[512,1024]{1,0:T(8,128)(2,1)}, bf16[512,1024]{1,0:T(8,128)(2,1)}, u32[]{:S(2)}, u32[]{:S(2)}) collective-permute-start(bf16[512,1024]{1,0:T(8,128)(2,1)} %get-tuple-element.515), channel_id=1, source_target_pairs={{0,1},{1,0},{2,3},{3,2},{4,5},{5,4},{6,7},{7,6},{8,9},{9,8},{10,11... | collective-permute-start | bytes 3145736 | tf_op jit(solution)/shard_map/ppermute | solution.py:330
  1051.3 39.4 %collective-permute-start.46 = (f32[2,2,2,32,384]{4,2,1,0,3:T(2,128)}, f32[2,2,2,32,384]{4,2,1,0,3:T(2,128)S(1)}, u32[]{:S(2)}, u32[]{:S(2)}) collective-permute-start(f32[2,2,2,32,384]{4,2,1,0,3:T(2,128)} %dynamic-slice_bitcast_fusion.3), channel_id=1, source_target_pairs={{0,4},{4,0},{8,12},{12,8},{16,20},{20,16},{24,28},{28,24},{1,5},{5... | collective-permute-start | bytes 1179656 | tf_op jit(solution)/shard_map/ppermute | solution.py:330
  1056.4 78.3 %collective-permute-start.56 = (bf16[512,1024]{1,0:T(8,128)(2,1)}, bf16[512,1024]{1,0:T(8,128)(2,1)S(1)}, u32[]{:S(2)}, u32[]{:S(2)}) collective-permute-start(bf16[512,1024]{1,0:T(8,128)(2,1)} %copy.421), channel_id=1, source_target_pairs={{0,1},{1,0},{2,3},{3,2},{4,5},{5,4},{6,7},{7,6},{8,9},{9,8},{10,11... | collective-permute-start | bytes 3145736 | tf_op jit(solution)/shard_map/ppermute | solution.py:330
  1131.8 103.1 %collective-permute-start.78 = (f32[2,2,2,2,336,128]{5,4,3,2,1,0:T(8,128)}, f32[2,2,2,2,336,128]{5,4,3,2,1,0:T(8,128)}, u32[]{:S(2)}, u32[]{:S(2)}) collective-permute-start(f32[2,2,2,2,336,128]{5,4,3,2,1,0:T(8,128)} %slice_bitcast_fusion.1), channel_id=1, source_target_pairs={{0,8},{4,12},{8,0},{12,4},{16,24},{20,28},{24,16},{28,20},{1,9},{5... | collective-permute-start | bytes 8257544 | tf_op jit(solution)/shard_map/ppermute | solution.py:330
  1150.8 77.3 %collective-permute-start.66 = (f32[2,2,2,1,336,128]{5,4,2,1,0,3:T(8,128)S(1)}, f32[2,2,2,1,336,128]{5,4,2,1,0,3:T(8,128)S(1)}, u32[]{:S(2)}, u32[]{:S(2)}) collective-permute-start(f32[2,2,2,1,336,128]{5,4,2,1,0,3:T(8,128)S(1)} %slice_bitcast_fusion.13), channel_id=1, source_target_pairs={{0,8},{4,12},{8,0},{12,4},{16,24},{20,28},{24,16},{28,20},{1,9},{5... | collective-permute-start | bytes 4128776 | tf_op jit(solution)/shard_map/ppermute | solution.py:330
  1156.2 72.1 %collective-permute-start.58 = (f32[2,2,2,1,352,128]{5,4,2,1,0,3:T(8,128)S(1)}, f32[2,2,2,1,352,128]{5,4,2,1,0,3:T(8,128)S(1)}, u32[]{:S(2)}, u32[]{:S(2)}) collective-permute-start(f32[2,2,2,1,352,128]{5,4,2,1,0,3:T(8,128)S(1)} %slice_bitcast_fusion.6), channel_id=1, source_target_pairs={{0,2},{2,0},{1,3},{3,1},{4,6},{6,4},{5,7},{7,5},{8,10},{10,8},{9,1... | collective-permute-start | bytes 4325384 | tf_op jit(solution)/shard_map/ppermute | solution.py:330
  1171.2 81.3 %collective-permute-start.70 = (f32[2,2,2,2,352,128]{5,4,3,2,1,0:T(8,128)S(1)}, f32[2,2,2,2,352,128]{5,4,3,2,1,0:T(8,128)S(1)}, u32[]{:S(2)}, u32[]{:S(2)}) collective-permute-start(f32[2,2,2,2,352,128]{5,4,3,2,1,0:T(8,128)S(1)} %copy-done.41), channel_id=1, source_target_pairs={{0,2},{2,0},{1,3},{3,1},{4,6},{6,4},{5,7},{7,5},{8,10},{10,8},{9,1... | collective-permute-start | bytes 8650760 | tf_op jit(solution)/shard_map/ppermute | solution.py:330
  1228.1 106.0 %collective-permute-start.83 = (f32[2,2,2,288,128]{4,3,2,1,0:T(8,128)}, f32[2,2,2,288,128]{4,3,2,1,0:T(8,128)}, u32[]{:S(2)}, u32[]{:S(2)}) collective-permute-start(f32[2,2,2,288,128]{4,3,2,1,0:T(8,128)} %dynamic-slice_bitcast_fusion.1), channel_id=1, source_target_pairs={{0,2},{2,0},{1,3},{3,1},{4,6},{6,4},{5,7},{7,5},{8,10},{10,8},{9,1... | collective-permute-start | bytes 3538952 | tf_op jit(solution)/shard_map/ppermute | solution.py:330
  1228.3 42.9 %collective-permute-start.63 = (f32[2,2,1,336,128]{4,3,1,0,2:T(8,128)S(1)}, f32[2,2,1,336,128]{4,3,1,0,2:T(8,128)S(1)}, u32[]{:S(2)}, u32[]{:S(2)}) collective-permute-start(f32[2,2,1,336,128]{4,3,1,0,2:T(8,128)S(1)} %slice_bitcast_fusion.25), channel_id=1, source_target_pairs={{0,8},{4,12},{8,0},{12,4},{16,24},{20,28},{24,16},{28,20},{1,9},{5... | collective-permute-start | bytes 2064392 | tf_op jit(solution)/shard_map/ppermute | solution.py:330
  1228.6 42.8 %collective-permute-start.67 = (f32[2,2,1,336,128]{4,3,1,0,2:T(8,128)S(1)}, f32[2,2,1,336,128]{4,3,1,0,2:T(8,128)S(1)}, u32[]{:S(2)}, u32[]{:S(2)}) collective-permute-start(f32[2,2,1,336,128]{4,3,1,0,2:T(8,128)S(1)} %slice_bitcast_fusion.23), channel_id=1, source_target_pairs={{0,16},{4,20},{8,24},{12,28},{16,0},{20,4},{24,8},{28,12},{1,17},{... | collective-permute-start | bytes 2064392 | tf_op jit(solution)/shard_map/ppermute | solution.py:330
  1234.9 38.1 %collective-permute-start.59 = (f32[2,2,1,352,128]{4,3,1,0,2:T(8,128)S(1)}, f32[2,2,1,352,128]{4,3,1,0,2:T(8,128)S(1)}, u32[]{:S(2)}, u32[]{:S(2)}) collective-permute-start(f32[2,2,1,352,128]{4,3,1,0,2:T(8,128)S(1)} %slice_bitcast_fusion.17), channel_id=1, source_target_pairs={{0,4},{4,0},{8,12},{12,8},{16,20},{20,16},{24,28},{28,24},{1,5},{5... | collective-permute-start | bytes 2162696 | tf_op jit(solution)/shard_map/ppermute | solution.py:330
  1252.5 181.1 %collective-permute-start.75 = (f32[2,2,2,336,128]{4,3,2,1,0:T(8,128)}, f32[2,2,2,336,128]{4,3,2,1,0:T(8,128)}, u32[]{:S(2)}, u32[]{:S(2)}) collective-permute-start(f32[2,2,2,336,128]{4,3,2,1,0:T(8,128)} %slice_bitcast_fusion.9), channel_id=1, source_target_pairs={{0,8},{4,12},{8,0},{12,4},{16,24},{20,28},{24,16},{28,20},{1,9},{5... | collective-permute-start | bytes 4128776 | tf_op jit(solution)/shard_map/ppermute | solution.py:330
  1271.2 166.6 %collective-permute-start.79 = (f32[2,2,2,336,128]{4,3,2,1,0:T(8,128)}, f32[2,2,2,336,128]{4,3,2,1,0:T(8,128)}, u32[]{:S(2)}, u32[]{:S(2)}) collective-permute-start(f32[2,2,2,336,128]{4,3,2,1,0:T(8,128)} %slice_bitcast_fusion.7), channel_id=1, source_target_pairs={{0,16},{4,20},{8,24},{12,28},{16,0},{20,4},{24,8},{28,12},{1,17},{... | collective-permute-start | bytes 4128776 | tf_op jit(solution)/shard_map/ppermute | solution.py:330
  1271.5 168.5 %collective-permute-start.71 = (f32[2,2,2,352,128]{4,3,2,1,0:T(8,128)}, f32[2,2,2,352,128]{4,3,2,1,0:T(8,128)}, u32[]{:S(2)}, u32[]{:S(2)}) collective-permute-start(f32[2,2,2,352,128]{4,3,2,1,0:T(8,128)} %slice_bitcast_fusion.3), channel_id=1, source_target_pairs={{0,4},{4,0},{8,12},{12,8},{16,20},{20,16},{24,28},{28,24},{1,5},{5... | collective-permute-start | bytes 4325384 | tf_op jit(solution)/shard_map/ppermute | solution.py:330
  1273.0 52.0 %collective-permute-start.64 = (f32[2,1,336,128]{3,2,0,1:T(8,128)S(1)}, f32[2,1,336,128]{3,2,0,1:T(8,128)S(1)}, u32[]{:S(2)}, u32[]{:S(2)}) collective-permute-start(f32[2,1,336,128]{3,2,0,1:T(8,128)S(1)} %slice_bitcast_fusion.41), channel_id=1, source_target_pairs={{0,16},{4,20},{8,24},{12,28},{16,0},{20,4},{24,8},{28,12},{1,17},{... | collective-permute-start | bytes 1032200 | tf_op jit(solution)/shard_map/ppermute | solution.py:330
  1327.0 169.5 %all-to-all-start.9 = ((f32[32,32,1024]{2,1,0:T(8,128)}), f32[32,32,1024]{2,1,0:T(8,128)}, u32[]{:S(2)}, u32[]{:S(2)}) async-start(f32[32,32,1024]{2,1,0:T(8,128)} %bitcast.1212), calls=%async_computation.9 | async-start | bytes 8388608 | tf_op jit(solution)/shard_map/all_to_all | solution.py:303
  1332.5 75.0 %collective-permute-start.60 = (f32[2,1,352,128]{3,2,0,1:T(8,128)}, f32[2,1,352,128]{3,2,0,1:T(8,128)S(1)}, u32[]{:S(2)}, u32[]{:S(2)}) collective-permute-start(f32[2,1,352,128]{3,2,0,1:T(8,128)} %slice_bitcast_fusion.33), channel_id=1, source_target_pairs={{0,8},{4,12},{8,0},{12,4},{16,24},{20,28},{24,16},{28,20},{1,9},{5... | collective-permute-start | bytes 1081352 | tf_op jit(solution)/shard_map/ppermute | solution.py:330
  1334.1 74.6 %collective-permute-start.65 = (f32[1,336,128]{2,1,0:T(8,128)S(1)}, f32[1,336,128]{2,1,0:T(8,128)S(1)}, u32[]{:S(2)}, u32[]{:S(2)}) collective-permute-start(f32[1,336,128]{2,1,0:T(8,128)S(1)} %slice_bitcast_fusion.56), channel_id=1, source_target_pairs={{0,2},{2,0},{1,3},{3,1},{4,6},{6,4},{5,7},{7,5},{8,10},{10,8},{9,1... | collective-permute-start | bytes 516104 | tf_op jit(solution)/shard_map/ppermute | solution.py:330
  1408.7 24.7 %collective-permute-start.84 = (f32[2,2,288,128]{3,2,1,0:T(8,128)S(1)}, f32[2,2,288,128]{3,2,1,0:T(8,128)S(1)}, u32[]{:S(2)}, u32[]{:S(2)}) collective-permute-start(f32[2,2,288,128]{3,2,1,0:T(8,128)S(1)} %dynamic-slice_bitcast_fusion.2), channel_id=1, source_target_pairs={{0,4},{4,0},{8,12},{12,8},{16,20},{20,16},{24,28},{28,24},{1,5},{5... | collective-permute-start | bytes 1769480 | tf_op jit(solution)/shard_map/ppermute | solution.py:330
  1435.4 39.8 %collective-permute-start.76 = (f32[2,2,336,128]{3,2,1,0:T(8,128)S(1)}, f32[2,2,336,128]{3,2,1,0:T(8,128)S(1)}, u32[]{:S(2)}, u32[]{:S(2)}) collective-permute-start(f32[2,2,336,128]{3,2,1,0:T(8,128)S(1)} %slice_bitcast_fusion.21), channel_id=1, source_target_pairs={{0,16},{4,20},{8,24},{12,28},{16,0},{20,4},{24,8},{28,12},{1,17},{... | collective-permute-start | bytes 2064392 | tf_op jit(solution)/shard_map/ppermute | solution.py:330
  1439.4 37.1 %collective-permute-start.80 = (f32[2,2,336,128]{3,2,1,0:T(8,128)S(1)}, f32[2,2,336,128]{3,2,1,0:T(8,128)S(1)}, u32[]{:S(2)}, u32[]{:S(2)}) collective-permute-start(f32[2,2,336,128]{3,2,1,0:T(8,128)S(1)} %slice_bitcast_fusion.19), channel_id=1, source_target_pairs={{0,2},{2,0},{1,3},{3,1},{4,6},{6,4},{5,7},{7,5},{8,10},{10,8},{9,1... | collective-permute-start | bytes 2064392 | tf_op jit(solution)/shard_map/ppermute | solution.py:330
  1446.5 28.0 %collective-permute-start.86 = (f32[288,128]{1,0:T(8,128)S(1)}, f32[288,128]{1,0:T(8,128)S(1)}, u32[]{:S(2)}, u32[]{:S(2)}) collective-permute-start(f32[288,128]{1,0:T(8,128)S(1)} %dynamic-slice_bitcast_fusion.7), channel_id=1, source_target_pairs={{0,16},{4,20},{8,24},{12,28},{16,0},{20,4},{24,8},{28,12},{1,17},{... | collective-permute-start | bytes 442376 | tf_op jit(solution)/shard_map/ppermute | solution.py:330
  1446.6 31.7 %collective-permute-start.72 = (f32[2,2,352,128]{3,2,1,0:T(8,128)S(1)}, f32[2,2,352,128]{3,2,1,0:T(8,128)S(1)}, u32[]{:S(2)}, u32[]{:S(2)}) collective-permute-start(f32[2,2,352,128]{3,2,1,0:T(8,128)S(1)} %slice_bitcast_fusion.15), channel_id=1, source_target_pairs={{0,8},{4,12},{8,0},{12,4},{16,24},{20,28},{24,16},{28,20},{1,9},{5... | collective-permute-start | bytes 2162696 | tf_op jit(solution)/shard_map/ppermute | solution.py:330
  1558.8 44.4 %collective-permute-start.105 = (bf16[4,336,128]{2,1,0:T(8,128)(2,1)S(1)}, bf16[4,336,128]{2,1,0:T(8,128)(2,1)S(1)}, u32[]{:S(2)}, u32[]{:S(2)}) collective-permute-start(bf16[4,336,128]{2,1,0:T(8,128)(2,1)S(1)} %pad_maximum_fusion.34), channel_id=1, source_target_pairs={{0,4},{4,0},{8,12},{12,8},{16,20},{20,16},{24,28},{28,24},{1,5},{5... | collective-permute-start | bytes 1032200 | tf_op jit(solution)/shard_map/ppermute | solution.py:330
  1562.7 41.6 %collective-permute-start.108 = (bf16[4,336,128]{2,1,0:T(8,128)(2,1)S(1)}, bf16[4,336,128]{2,1,0:T(8,128)(2,1)S(1)}, u32[]{:S(2)}, u32[]{:S(2)}) collective-permute-start(bf16[4,336,128]{2,1,0:T(8,128)(2,1)S(1)} %pad_maximum_fusion.35), channel_id=1, source_target_pairs={{0,8},{4,12},{8,0},{12,4},{16,24},{20,28},{24,16},{28,20},{1,9},{5... | collective-permute-start | bytes 1032200 | tf_op jit(solution)/shard_map/ppermute | solution.py:330
  1591.6 25.9 %collective-permute-start.94 = (bf16[4,336,256]{2,1,0:T(8,128)(2,1)S(1)}, bf16[4,336,256]{2,1,0:T(8,128)(2,1)S(1)}, u32[]{:S(2)}, u32[]{:S(2)}) collective-permute-start(bf16[4,336,256]{2,1,0:T(8,128)(2,1)S(1)} %pad_maximum_fusion.19), channel_id=1, source_target_pairs={{0,8},{4,12},{8,0},{12,4},{16,24},{20,28},{24,16},{28,20},{1,9},{5... | collective-permute-start | bytes 2064392 | tf_op jit(solution)/shard_map/ppermute | solution.py:330
  1603.2 25.6 %collective-permute-start.98 = (bf16[4,336,256]{2,1,0:T(8,128)(2,1)S(1)}, bf16[4,336,256]{2,1,0:T(8,128)(2,1)S(1)}, u32[]{:S(2)}, u32[]{:S(2)}) collective-permute-start(bf16[4,336,256]{2,1,0:T(8,128)(2,1)S(1)} %pad_maximum_fusion.20), channel_id=1, source_target_pairs={{0,16},{4,20},{8,24},{12,28},{16,0},{20,4},{24,8},{28,12},{1,17},{... | collective-permute-start | bytes 2064392 | tf_op jit(solution)/shard_map/ppermute | solution.py:330
  1603.3 25.7 %collective-permute-start.90 = (bf16[4,352,256]{2,1,0:T(8,128)(2,1)S(1)}, bf16[4,352,256]{2,1,0:T(8,128)(2,1)S(1)}, u32[]{:S(2)}, u32[]{:S(2)}) collective-permute-start(bf16[4,352,256]{2,1,0:T(8,128)(2,1)S(1)} %pad_maximum_fusion.17), channel_id=1, source_target_pairs={{0,4},{4,0},{8,12},{12,8},{16,20},{20,16},{24,28},{28,24},{1,5},{5... | collective-permute-start | bytes 2162696 | tf_op jit(solution)/shard_map/ppermute | solution.py:330
  1617.6 34.0 %collective-permute-start.95 = (bf16[8,336,256]{2,1,0:T(8,128)(2,1)S(1)}, bf16[8,336,256]{2,1,0:T(8,128)(2,1)S(1)}, u32[]{:S(2)}, u32[]{:S(2)}) collective-permute-start(bf16[8,336,256]{2,1,0:T(8,128)(2,1)S(1)} %pad_maximum_fusion.13), channel_id=1, source_target_pairs={{0,4},{4,0},{8,12},{12,8},{16,20},{20,16},{24,28},{28,24},{1,5},{5... | collective-permute-start | bytes 4128776 | tf_op jit(solution)/shard_map/ppermute | solution.py:330
  1628.9 29.3 %collective-permute-start.99 = (bf16[8,336,256]{2,1,0:T(8,128)(2,1)S(1)}, bf16[8,336,256]{2,1,0:T(8,128)(2,1)S(1)}, u32[]{:S(2)}, u32[]{:S(2)}) collective-permute-start(bf16[8,336,256]{2,1,0:T(8,128)(2,1)S(1)} %pad_maximum_fusion.14), channel_id=1, source_target_pairs={{0,8},{4,12},{8,0},{12,4},{16,24},{20,28},{24,16},{28,20},{1,9},{5... | collective-permute-start | bytes 4128776 | tf_op jit(solution)/shard_map/ppermute | solution.py:330
  1629.1 29.3 %collective-permute-start.91 = (bf16[8,352,256]{2,1,0:T(8,128)(2,1)S(1)}, bf16[8,352,256]{2,1,0:T(8,128)(2,1)S(1)}, u32[]{:S(2)}, u32[]{:S(2)}) collective-permute-start(bf16[8,352,256]{2,1,0:T(8,128)(2,1)S(1)} %pad_maximum_fusion.12), channel_id=1, source_target_pairs={{0,2},{2,0},{1,3},{3,1},{4,6},{6,4},{5,7},{7,5},{8,10},{10,8},{9,1... | collective-permute-start | bytes 4325384 | tf_op jit(solution)/shard_map/ppermute | solution.py:330
  1699.2 33.0 %collective-permute-start.109 = (f32[1024,128]{1,0:T(8,128)}, f32[1024,128]{1,0:T(8,128)}, u32[]{:S(2)}, u32[]{:S(2)}) collective-permute-start(f32[1024,128]{1,0:T(8,128)} %slice.1514), channel_id=1, source_target_pairs={{0,1},{1,0},{2,3},{3,2},{4,5},{5,4},{6,7},{7,6},{8,9},{9,8},{10,11... | collective-permute-start | bytes 1572872 | tf_op jit(solution)/shard_map/ppermute | solution.py:330
  (267 other events, 4302.5 us)
Sparse Core Ops, SparseCore 0:
  11.4 124.1 all-gather.4
  139.0 114.6 all-gather.6

commit v2 on v1

--- a/solution.py
+++ b/solution.py
@@ -175,7 +175,8 @@
                             jnp.dot(*operands[1::2], preferred_element_type=jnp.float32)])
         blocks = blocks.reshape(2, D, wide_count, 2, -1).transpose(2, 3, 0, 1, 4)
         grad_mats_ffn = in_routes(blocks, wide_count)
-    grad_ffn, *grad_mats_ffn = lax.optimization_barrier((grad_ffn, *grad_mats_ffn))
+    grad_ffn, parts = tied(grad_ffn, grad_mats_ffn)
+    parts = reduce_step(parts, wide_count, 0)
     grad_middle = grad_ffn + project_back(up_low, w_up)
     grad_attn, grad_gain_one, grad_shift_one = first_pull(grad_middle)
     attn_low = grad_attn.astype(jnp.bfloat16)
@@ -191,20 +192,27 @@
     grad_value = grad_value.reshape(count, length, model_width).astype(jnp.bfloat16)
     grad_scores = attn_prob * (grad_prob - jnp.sum(grad_prob * attn_prob, -1, keepdims=True))
     grad_raw = (grad_scores * (model_width // HEADS) ** (-0.5)).astype(jnp.bfloat16)
+    late_keys, parts = tied(key_proj, parts)
+    parts = reduce_step(parts, wide_count, 1)
     grad_query = jnp.einsum(
-        "bnhqk,bnkhe->bnqhe", grad_raw, to_heads(key_proj), preferred_element_type=jnp.float32
+        "bnhqk,bnkhe->bnqhe", grad_raw, to_heads(late_keys), preferred_element_type=jnp.float32
     )
     grad_query = grad_query.reshape(count, length, model_width).astype(jnp.bfloat16)
     grad_key = jnp.einsum(
         "bnhqk,bnqhe->bnkhe", grad_raw, to_heads(queries), preferred_element_type=jnp.float32
     )
     grad_key = grad_key.reshape(count, length, model_width).astype(jnp.bfloat16)
+    grad_query, parts = tied(grad_query, parts)
+    parts = reduce_step(parts, wide_count, 2)
     grad_hidden = (
         grad_attn
         + project_back(grad_query, w_query)
         + project_back(grad_key, w_key)
         + project_back(grad_value, w_value)
     )
+    grad_hidden, parts = tied(grad_hidden, parts)
+    for step in range(3, len(routes(wide_count)[0])):
+        parts = reduce_step(parts, wide_count, step)
     operands = (
         share(inputs[0].T, 1),
         swap_pick(inputs[0].T, context[0].T, 1),
@@ -218,7 +226,7 @@
                             jnp.dot(*operands[1::2], preferred_element_type=jnp.float32)])
         blocks = blocks.reshape(2, 1, D, wide_count, -1).transpose(3, 0, 1, 2, 4)
         grad_mats_attn = in_routes(blocks, wide_count)
-    matrices = (grad_mats_attn, grad_mats_ffn)
+    matrices = (grad_mats_attn, parts)
     vector_grads = jnp.stack(
         [
             grad_gain_one,
@@ -367,6 +375,18 @@
 
 def here16():
     return lax.axis_index("wide") * 2 + lax.axis_index("pair")
+
+
+def reduce_step(parts, wide_count, step):
+    return [
+        part[0] + exchange(part[1], route[step])
+        for part, route in zip(parts, routes(wide_count))
+    ]
+
+
+def tied(value, parts):
+    value, *parts = lax.optimization_barrier((value, *parts))
+    return value, parts
 
 
 def reduce_relative(parts, wide_count):
@@ -616,23 +636,51 @@
     return block.reshape(rows, lanes)
 
 
+def join_kernel(blocks_ref, out_ref, *, starts):
+    rows = blocks_ref.shape[1]
+    for dev in range(len(starts) - 1):
+        length = starts[dev + 1] - starts[dev]
+        out_ref[starts[dev] : starts[dev + 1]] = blocks_ref[dev, :length]
+    for dev in range(1, len(starts) - 1):
+        length = starts[dev] - starts[dev - 1]
+        if length < rows:
+            shared = slice(starts[dev], starts[dev] + tile)
+            both = blocks_ref[dev, :tile].astype(jnp.float32)
+            both += blocks_ref[dev - 1, length : length + tile].astype(jnp.float32)
+            out_ref[shared] = both.astype(out_ref.dtype)
+
+
 def join_flat(blocks, size):
-    devices, rows = blocks.shape[:2]
-    starts, _ = flat_blocks(size, devices)
-    pieces, carry = [], None
-    for dev in range(devices):
-        length = starts[dev + 1] - starts[dev]
-        first = blocks[dev, :tile] if carry is None else blocks[dev, :tile] + carry
-        pieces += [first, blocks[dev, tile:length]]
-        carry = blocks[dev, length : length + tile] if length < rows else None
-    return jnp.concatenate(pieces)
-
-
-def scatter_flat(flat_rows, size, device, devices):
+    starts, _ = flat_blocks(size, blocks.shape[0])
+    starts[-1] += -starts[-1] % tile
+    return pl.pallas_call(
+        functools.partial(join_kernel, starts=starts),
+        out_shape=jax.ShapeDtypeStruct((starts[-1], lanes), blocks.dtype),
+    )(blocks)
+
+
+def split_kernel(front_ref, rest_ref, out_ref, *, starts):
+    front, rows = front_ref.shape[0], out_ref.shape[1]
+    total = front + rest_ref.shape[0]
+    for dev, start in enumerate(starts[:-1]):
+        stop = min(start + rows, total)
+        middle = min(max(start, front), stop)
+        if start < middle:
+            out_ref[dev, : middle - start] = front_ref[start:middle]
+        if middle < stop:
+            out_ref[dev, middle - start : stop - start] = rest_ref[middle - front : stop - front]
+        if stop < start + rows:
+            left = start + rows - stop
+            out_ref[dev, rows - left :] = jnp.zeros((left, lanes), out_ref.dtype)
+
+
+def scatter_flat(front, rest, size, device, devices):
     wide_count = lax.axis_size("wide")
     starts, rows = flat_blocks(size, devices)
-    padded = jnp.pad(flat_rows, ((0, rows), (0, 0)))
-    blocks = jnp.stack([padded[starts[dev] : starts[dev] + rows] for dev in range(devices)])
+    blocks = pl.pallas_call(
+        functools.partial(split_kernel, starts=starts),
+        out_shape=jax.ShapeDtypeStruct((devices, rows, lanes), front.dtype),
+    )(front, rest)
     bits = wide_bits(wide_count)[::-1] + [("pair", 1), side_bit]
     part = blocks.reshape((2,) * len(bits) + blocks.shape[1:])
     for bit in [side_bit] + routes(wide_count)[0]:
@@ -693,7 +741,7 @@
     up_biases = other_flat[bias_rows:up_rows].reshape(devices // 2, 2, ffn_width)
     up_biases = up_biases.transpose(1, 0, 2).reshape(L, FF).astype(jnp.float32)
     vectors = other_flat[up_rows:vec_rows].reshape(NV, D).astype(jnp.float32)
-    head_weight = other_flat[vec_rows:].reshape(D, D)
+    head_weight = other_flat[vec_rows : vec_rows + D * D // lanes].reshape(D, D)
 
     win_count = token_ids.shape[0]
     assert win_count == 1 and SEQ == 2 * WINDOW
@@ -866,6 +914,7 @@
     keep = jnp.dot(grad_logits[: rows_all // 2], table_low, preferred_element_type=jnp.float32)
     grad_head_out = reduce_rows((keep + got).reshape(group, MPW, D), wide_count)
     grad_words = jnp.einsum("rv,rd->vd", grad_logits, head_all, preferred_element_type=jnp.float32)
+    grad_head_out, grad_words = lax.optimization_barrier((grad_head_out, grad_words))
 
     grad_pre, grad_head_gain, grad_head_shift = head_pull(grad_head_out)
     pre_low = grad_pre.astype(jnp.bfloat16)
@@ -878,8 +927,9 @@
     grad_embed, grad_emb_gain, grad_emb_shift = embed_pull(grad_hidden)
     flat_embed = grad_embed.reshape(WINDOW, D)
 
-    ffn_grad = jnp.concatenate(reduce_relative(layer_mats[1], wide_count), axis=1)
-    attn_grad = jnp.concatenate(reduce_relative(layer_mats[0], wide_count), axis=1)
+    ffn_parts, attn_parts = layer_mats[1], layer_mats[0]
+    flat_embed, ffn_parts = tied(flat_embed, ffn_parts)
+    ffn_grad = jnp.concatenate(ffn_parts, axis=1)
     dec_block = jnp.zeros((devices * owned,), jnp.float32)
     dec_block = lax.dynamic_update_slice(dec_block, grad_dec, (device * owned,))[:V]
     vector_block = jnp.concatenate(
@@ -888,19 +938,20 @@
         + [jnp.stack([jnp.sum(pre_low.astype(jnp.float32), 0), grad_head_gain, grad_head_shift])],
         axis=0,
     )
-    grad_other = jnp.concatenate(
+    front = jnp.concatenate(
         [
             dec_block.reshape(-1, lanes),
             up_grad.reshape(2, devices // 2, ffn_width).transpose(1, 0, 2).reshape(-1, lanes),
             vector_block.reshape(-1, lanes),
-            grad_head_w.reshape(-1, lanes),
         ]
     )
-    other_grad = scatter_flat(grad_other, size, device, devices)
+    other_grad = scatter_flat(front, grad_head_w.reshape(-1, lanes), size, device, devices)
 
     place_grad = flat_embed.reshape(per_place, group, D).transpose(1, 0, 2)
     place_grad = place_grad.reshape(wide_count, narrow_count // 2, per_place, D)
     place_grad = reduce_blocks(place_grad, wide_count, 1, 128)
+    place_grad, attn_parts = tied(place_grad, attn_parts)
+    attn_grad = jnp.concatenate(reduce_relative(attn_parts, wide_count), axis=1)
     sent = add_rows(now, flat_embed, devices * slots) + add_rows(held, place_grad, devices * slots)
     arrived = swap_all(sent.reshape(devices, slots, D)).reshape(-1, D)
     table_grad = grad_words + add_rows(asked, arrived, owned)
@@ -930,9 +981,8 @@
     keep = jnp.where(second, ffn_moment_new[1], ffn_moment_new[0])
     got = exchange(jnp.where(second, ffn_moment_new[0], ffn_moment_new[1]), side_bit)
     ffn_pair = jnp.concatenate([keep, got], axis=1)[None]
+    attn_found = gather_columns(attn_moment_new, False)
     ffn_found = gather_columns(ffn_pair, True)
-    attn_found = gather_columns(attn_moment_new, False)
-    ffn_found, attn_found = lax.optimization_barrier((ffn_found, attn_found))
     attn_new = muon_cols(attn_mats, attn_moment_new, gram_of(attn_found), D)
     ffn_turn = newton_cols(ffn_pair, gram_of(ffn_found))[0]
     keep, give = ffn_turn[:, :ffn_width], ffn_turn[:, ffn_width:]

time: 1760 us -> 1510 us (0.86)
  waiting for transfers between devices: 765 us -> 614 us
  local copies, waits for them, and re-layouts: 280 us -> 205 us
    ppermute x110, waiting for transfers between devices: 695 us -> 540 us  [exchange(): return lax.ppermute(values, axis, steps)]
    another operation x29 -> x0, local copies, waits for them, and re-layouts: 44.6 us -> none  [scatter_flat(): jnp.stack([padded[starts[dev]:starts[dev] + rows] for dev in range(device...]
    unnamed x487 -> x354, local copies, waits for them, and re-layouts: 46 us -> 13.2 us
    unnamed x43 -> x6, other arithmetic: 22.8 us -> 0.01 us
    add x0 -> x12, other arithmetic: none -> 22.1 us  [reduce_step(): part[0] + exchange(part[1], route[step])]
  transfers between devices with their start and end apart: 119 -> 119, of which waited for: 67 -> 65; matrix products, arithmetic and copies ran while one was open for 27% -> 32% of each run, Pallas kernels for 1% -> 1%
where the time goes in v2:
time: 1510 us; the launch traced here: 1500 us
  waiting for transfers between devices  614 us (41%)
  matrix products  303 us (20%)
  local copies, waits for them, and re-layouts  205 us (14%)
  other arithmetic  152 us (10%)
  starting transfers between devices  135 us (9%)
  Pallas kernels  62 us (4%)
  between operations  30.4 us (2%)
    ppermute x110, waiting for transfers between devices, exchange(): return lax.ppermute(values, axis, steps)  540 us
    ppermute x110, starting transfers between devices, exchange(): return lax.ppermute(values, axis, steps)  104 us
    all_to_all x7, waiting for transfers between devices, swap_all(): return lax.all_to_all(blocks, axes, 0, 0, tiled=True)  73.1 us
    dot_general x6, matrix products, project(): jnp.einsum('bsd,df->bsf', inputs, weight, preferred_element_type=jnp.floa...  53.3 us
  transfers between devices with their start and end apart: 119, of which 65 were waited for; matrix products, arithmetic and copies ran while one was open for 32% of the time, Pallas kernels for 1%

profile of v2, /device:TPU:0, one launch (start us, length us, event | category | flops | bytes accessed | tf_op | source)
XLA Modules:
  0.0 1500.8 jit_solution(1317071189291928921)
XLA Ops:
  18.7 7.3 all-to-all-start.4
  46.9 10.6 reshape.1625
  57.6 7.7 copy.506
  78.4 50.3 %all-to-all-done.5 = bf16[32,32,1024]{2,1,0:T(8,128)(2,1)S(1)} async-done(((bf16[32,32,1024]{2,1,0:T(8,128)(2,1)}), bf16[32,32,1024]{2,1,0:T(8,128)(2,1)S(1)}, u32[]{:S(2)}, u32[]{:S(2)}) %all-to-all-start.5) | async-done | bytes 2097184 | tf_op jit(solution)/shard_map/all_to_all | solution.py:311
  149.0 7.4 collective-permute-done.6
  172.4 7.7 slice.588
  187.6 11.4 copy.392
  200.7 7.3 fusion.297
  230.6 10.0 fusion.17
  240.6 9.5 exponential_reduce_fusion
  250.2 9.0 convolution_convert_fusion.1
  262.7 11.7 fusion.296
  274.4 11.9 copy.397
  286.3 11.9 copy.399
  298.2 27.9 %multiply_convert_fusion.1 = (bf16[512,4096]{1,0:T(8,128)(2,1)S(1)}, f32[512,4096]{1,0:T(8,128)}, f32[512,4096]{1,0:T(8,128)}) fusion(f32[4096]{0:T(1024)S(1)} %bitcast.931, bf16[1024,4096]{0,1:T(8,128)(2,1)} %bitcast.812, f32[512,1024]{1,0:T(8,128)} %copy-done.2, f32[1024]{0:T(1024)S(1)} %get-tuple-element.478, f32[1024]{0:T(1024)S(1)} %get-tuple-element.479, ...), kind=kOutput, calls=%fused_computation.50 | convolution fusion | flops 4436000768 | bytes 31485952 | tf_op jit(solution)/shard_map/bsd,df->bsf/dot_general | solution.py:60
  347.0 12.1 collective-permute-done.20
  359.1 9.4 collective-permute-start.21
  379.0 80.4 %collective-permute-done.12 = bf16[1,80,384]{2,1,0:T(8,128)(2,1)S(1)} collective-permute-done((bf16[1,80,384]{2,1,0:T(8,128)(2,1)S(1)}, bf16[1,80,384]{2,1,0:T(8,128)(2,1)S(1)}, u32[]{:S(2)}, u32[]{:S(2)}) %collective-permute-start.12) | collective-permute-done | bytes 61472 | tf_op jit(solution)/shard_map/ppermute | solution.py:338
  497.4 11.6 fusion.309
  539.4 26.0 %shard_map.311 = (bf16[2560,992]{1,0:T(8,128)(2,1)}, f32[1,992]{1,0:T(1,128)}, f32[1,992]{1,0:T(1,128)}) custom-call(s32[3]{0:T(128)} %pad_add_fusion.facts, f32[2560,992]{1,0:T(8,128)} %get-tuple-element.500.logits_ref, bf16[32,80,992]{2,1,0:T(8,128)(2,1)} %all-to-all-done.6.source_ref, f32[2560,4]{1,0:T(8,128)} %copy.405.rows_ref), custom_call_target="tpu_custom_call" | custom-call | tf_op jit(solution)/shard_map/pallas_call | solution.py:575
  565.4 7.6 fusion.85
  592.2 15.0 collective-permute-done.34
  615.3 8.7 collective-permute-done.35
  626.3 22.3 %collective-permute-done.26 = f32[2,2,2,80,384]{4,3,0,1,2:T(8,128)S(1)} collective-permute-done((f32[2,2,2,80,384]{4,3,0,1,2:T(8,128)S(1)}, f32[2,2,2,80,384]{4,3,0,1,2:T(8,128)S(1)}, u32[]{:S(2)}, u32[]{:S(2)}) %collective-permute-start.26) | collective-permute-done | bytes 983072 | tf_op jit(solution)/shard_map/ppermute | solution.py:338
  660.7 9.8 collective-permute-done.27
  670.6 10.4 collective-permute-done.32
  707.0 12.6 convert_reduce_fusion
  771.9 17.2 %shard_map.312 = (f32[2,2,2,2,2,352,128]{6,5,4,3,2,1,0:T(8,128)}, f32[2,2,2,2,2,336,128]{6,5,4,3,2,1,0:T(8,128)}, f32[2,2,2,2,2,336,128]{6,5,4,3,2,1,0:T(8,128)}) custom-call(s32[2]{0:T(128)} %pad_add_fusion.1.here, bf16[1024,1024]{1,0:T(8,128)(2,1)} %copy.412.up_rows, bf16[1024,1024]{1,0:T(8,128)(2,1)} %copy.413.down_rows, ...), custom_call_target="tpu_custom_call" | custom-call | tf_op jit(solution)/shard_map/pallas_call | solution.py:450
  789.1 10.9 fusion.94
  817.7 8.2 fusion.312
  825.9 24.2 %fusion.141 = bf16[16,64,512]{2,1,0:T(8,128)(2,1)S(1)} fusion(bf16[512,16,64]{0,2,1:T(8,128)(2,1)S(1)} %bitcast.847, f32[16,512,512]{1,2,0:T(8,128)} %fusion.312, f32[16,512,512]{1,2,0:T(8,128)} %get-tuple-element.492, f32[16,512]{1,0:T(8,128)S(1)} %copy-done.110, pred[512,512]{0,1:T(8,128)(4,1)S(1)} %copy-done.65), kind=kOutput, calls=%fused_computation.240 | convolution fusion | flops 583541248 | bytes 35946496 | tf_op jit(solution)/shard_map/bnhqk,bnqhe->bnkhe/dot_general | solution.py:201
  851.4 10.3 convert_reduce_fusion.3
  867.5 9.6 collective-permute-done.43
  900.0 24.6 %fusion.138 = bf16[16,64,512]{2,1,0:T(8,128)(2,1)} fusion(bf16[512,16,64]{0,2,1:T(8,128)(2,1)} %bitcast.893, f32[16,512,512]{1,2,0:T(8,128)} %fusion.312, f32[16,512,512]{1,2,0:T(8,128)} %get-tuple-element.492, f32[16,512]{1,0:T(8,128)S(1)} %copy-done.110, pred[512,512]{0,1:T(8,128)(4,1)S(1)} %copy-done.65), kind=kOutput, calls=%fused_computation.239 | convolution fusion | flops 583541248 | bytes 35946496 | tf_op jit(solution)/shard_map/bnhqk,bnkhe->bnqhe/dot_general | solution.py:197
  924.6 21.2 %collective-permute-done.46 = f32[2,2,2,336,128]{4,3,2,1,0:T(8,128)} collective-permute-done((f32[2,2,2,336,128]{4,3,2,1,0:T(8,128)}, f32[2,2,2,336,128]{4,3,2,1,0:T(8,128)}, u32[]{:S(2)}, u32[]{:S(2)}) %collective-permute-start.46) | collective-permute-done | bytes 1376288 | tf_op jit(solution)/shard_map/ppermute | solution.py:338
  971.7 20.4 %collective-permute-done.49 = f32[2,2,336,128]{3,2,1,0:T(8,128)S(1)} collective-permute-done((f32[2,2,336,128]{3,2,1,0:T(8,128)S(1)}, f32[2,2,336,128]{3,2,1,0:T(8,128)S(1)}, u32[]{:S(2)}, u32[]{:S(2)}) %collective-permute-start.49) | collective-permute-done | bytes 688160 | tf_op jit(solution)/shard_map/ppermute | solution.py:338
  1013.7 10.7 shard_map.313
  1096.7 28.5 %collective-permute-done.78 = f32[2,2,2,1,336,128]{5,4,2,1,0,3:T(8,128)} collective-permute-done((f32[2,2,2,1,336,128]{5,4,2,1,0,3:T(8,128)}, f32[2,2,2,1,336,128]{5,4,2,1,0,3:T(8,128)}, u32[]{:S(2)}, u32[]{:S(2)}) %collective-permute-start.78) | collective-permute-done | bytes 1376288 | tf_op jit(solution)/shard_map/ppermute | solution.py:338
  1135.7 79.9 %collective-permute-done.79 = f32[2,2,1,336,128]{4,3,1,0,2:T(8,128)S(1)} collective-permute-done((f32[2,2,1,336,128]{4,3,1,0,2:T(8,128)S(1)}, f32[2,2,1,336,128]{4,3,1,0,2:T(8,128)S(1)}, u32[]{:S(2)}, u32[]{:S(2)}) %collective-permute-start.79) | collective-permute-done | bytes 688160 | tf_op jit(solution)/shard_map/ppermute | solution.py:338
  1236.3 12.7 collective-permute-done.84
  1249.3 7.9 collective-permute-done.85
  1266.9 8.8 fusion.135
  1303.3 8.9 divide_subtract_fusion
  1316.0 8.5 collective-permute-done.94
  1375.9 10.7 collective-permute-done.102
  1390.4 21.4 %collective-permute-done.107 = bf16[4,336,256]{2,1,0:T(8,128)(2,1)S(1)} collective-permute-done((bf16[4,336,256]{2,1,0:T(8,128)(2,1)S(1)}, bf16[4,336,256]{2,1,0:T(8,128)(2,1)S(1)}, u32[]{:S(2)}, u32[]{:S(2)}) %collective-permute-start.107) | collective-permute-done | bytes 688160 | tf_op jit(solution)/shard_map/ppermute | solution.py:338
  1421.0 23.0 %collective-permute-done.108 = bf16[8,336,256]{2,1,0:T(8,128)(2,1)S(1)} collective-permute-done((bf16[8,336,256]{2,1,0:T(8,128)(2,1)S(1)}, bf16[8,336,256]{2,1,0:T(8,128)(2,1)S(1)}, u32[]{:S(2)}, u32[]{:S(2)}) %collective-permute-start.108) | collective-permute-done | bytes 1376288 | tf_op jit(solution)/shard_map/ppermute | solution.py:338
  1446.3 12.0 fusion.53
  (988 shorter events, 663.3 us)
Async XLA Ops:
  7.2 161.3 %all-gather.5.cloned.1.call-start = ((), (), s32[]{:S(2)}) async-start(), calls=%async_computation.11 | async-start | bytes 11083776 | tf_op jit(solution)/shard_map/all_gather | solution.py:727
  10.9 251.8 %all-gather.7.cloned.1.call-start = ((), (), s32[]{:S(2)}) async-start(), calls=%async_computation.12 | async-start | bytes 17301504 | tf_op jit(solution)/shard_map/all_gather | solution.py:735
  38.5 90.2 %all-to-all-start.5 = ((bf16[32,32,1024]{2,1,0:T(8,128)(2,1)}), bf16[32,32,1024]{2,1,0:T(8,128)(2,1)S(1)}, u32[]{:S(2)}, u32[]{:S(2)}) async-start(bf16[32,32,1024]{2,1,0:T(8,128)(2,1)} %bitcast.874), calls=%async_computation.5 | async-start | bytes 4194304 | tf_op jit(solution)/shard_map/all_to_all | solution.py:311
  333.0 182.1 %all-to-all-start.6 = ((bf16[32,80,992]{2,1,0:T(8,128)(2,1)}), bf16[32,80,992]{2,1,0:T(8,128)(2,1)}, u32[]{:S(2)}, u32[]{:S(2)}) async-start(bf16[32,80,992]{2,1,0:T(8,128)(2,1)} %bitcast.796), calls=%async_computation.6 | async-start | bytes 10485760 | tf_op jit(solution)/shard_map/all_to_all | solution.py:311
  343.1 32.7 %collective-permute-start.16 = (bf16[1,80,384]{2,1,0:T(8,128)(2,1)S(1)}, bf16[1,80,384]{2,1,0:T(8,128)(2,1)S(1)}, u32[]{:S(2)}, u32[]{:S(2)}) collective-permute-start(bf16[1,80,384]{2,1,0:T(8,128)(2,1)S(1)} %get-tuple-element.443), channel_id=1, source_target_pairs={{0,2},{2,0},{1,3},{3,1},{4,6},{6,4},{5,7},{7,5},{8,10},{10,8},{9,1... | collective-permute-start | bytes 184328 | tf_op jit(solution)/shard_map/ppermute | solution.py:338
  344.6 114.8 %collective-permute-start.12 = (bf16[1,80,384]{2,1,0:T(8,128)(2,1)S(1)}, bf16[1,80,384]{2,1,0:T(8,128)(2,1)S(1)}, u32[]{:S(2)}, u32[]{:S(2)}) collective-permute-start(bf16[1,80,384]{2,1,0:T(8,128)(2,1)S(1)} %get-tuple-element.442), channel_id=1, source_target_pairs={{0,16},{4,20},{8,24},{12,28},{16,0},{20,4},{24,8},{28,12},{1,17},{... | collective-permute-start | bytes 184328 | tf_op jit(solution)/shard_map/ppermute | solution.py:338
  359.1 100.5 %collective-permute-start.21 = (bf16[2,80,256]{2,1,0:T(8,128)(2,1)S(1)}, bf16[2,80,256]{2,1,0:T(8,128)(2,1)S(1)}, u32[]{:S(2)}, u32[]{:S(2)}) collective-permute-start(bf16[2,80,256]{2,1,0:T(8,128)(2,1)S(1)} %pad_maximum_fusion.52), channel_id=1, source_target_pairs={{0,2},{2,0},{1,3},{3,1},{4,6},{6,4},{5,7},{7,5},{8,10},{10,8},{9,1... | collective-permute-start | bytes 245768 | tf_op jit(solution)/shard_map/ppermute | solution.py:338
  375.8 85.7 %collective-permute-start.17 = (bf16[2,80,384]{2,1,0:T(8,128)(2,1)S(1)}, bf16[2,80,384]{2,1,0:T(8,128)(2,1)S(1)}, u32[]{:S(2)}, u32[]{:S(2)}) collective-permute-start(bf16[2,80,384]{2,1,0:T(8,128)(2,1)S(1)} %pad_maximum_fusion.49), channel_id=1, source_target_pairs={{0,16},{4,20},{8,24},{12,28},{16,0},{20,4},{24,8},{28,12},{1,17},{... | collective-permute-start | bytes 368648 | tf_op jit(solution)/shard_map/ppermute | solution.py:338
  578.5 146.5 %collective-permute-start.38 = (bf16[1024,512]{0,1:T(8,128)(2,1)}, bf16[1024,512]{0,1:T(8,128)(2,1)}, u32[]{:S(2)}, u32[]{:S(2)}) collective-permute-start(bf16[1024,512]{0,1:T(8,128)(2,1)} %fusion.282), channel_id=1, source_target_pairs={{0,1},{1,0},{2,3},{3,2},{4,5},{5,4},{6,7},{7,6},{8,9},{9,8},{10,11... | collective-permute-start | bytes 3145736 | tf_op jit(solution)/shard_map/ppermute | solution.py:338
  580.2 151.8 %collective-permute-start.66 = (bf16[1024,512]{0,1:T(8,128)(2,1)}, bf16[1024,512]{0,1:T(8,128)(2,1)}, u32[]{:S(2)}, u32[]{:S(2)}) collective-permute-start(bf16[1024,512]{0,1:T(8,128)(2,1)} %fusion.387), channel_id=1, source_target_pairs={{0,1},{1,0},{2,3},{3,2},{4,5},{5,4},{6,7},{7,6},{8,9},{9,8},{10,11... | collective-permute-start | bytes 3145736 | tf_op jit(solution)/shard_map/ppermute | solution.py:338
  582.4 157.2 %collective-permute-start.67 = (bf16[1024,512]{0,1:T(8,128)(2,1)}, bf16[1024,512]{0,1:T(8,128)(2,1)}, u32[]{:S(2)}, u32[]{:S(2)}) collective-permute-start(bf16[1024,512]{0,1:T(8,128)(2,1)} %get-tuple-element.407), channel_id=1, source_target_pairs={{0,1},{1,0},{2,3},{3,2},{4,5},{5,4},{6,7},{7,6},{8,9},{9,8},{10,11... | collective-permute-start | bytes 3145736 | tf_op jit(solution)/shard_map/ppermute | solution.py:338
  591.6 33.2 %collective-permute-start.30 = (f32[2,2,2,80,384]{4,3,2,0,1:T(8,128)S(1)}, f32[2,2,2,80,384]{4,3,2,0,1:T(8,128)S(1)}, u32[]{:S(2)}, u32[]{:S(2)}) collective-permute-start(f32[2,2,2,80,384]{4,3,2,0,1:T(8,128)S(1)} %bitcast.894), channel_id=1, source_target_pairs={{0,4},{4,0},{8,12},{12,8},{16,20},{20,16},{24,28},{28,24},{1,5},{5... | collective-permute-start | bytes 2949128 | tf_op jit(solution)/shard_map/ppermute | solution.py:338
  624.8 26.4 %collective-permute-start.36 = (f32[2,80,256]{2,1,0:T(8,128)S(1)}, f32[2,80,256]{2,1,0:T(8,128)S(1)}, u32[]{:S(2)}, u32[]{:S(2)}) collective-permute-start(f32[2,80,256]{2,1,0:T(8,128)S(1)} %slice_bitcast_fusion.49), channel_id=1, source_target_pairs={{0,2},{2,0},{1,3},{3,1},{4,6},{6,4},{5,7},{7,5},{8,10},{10,8},{9,1... | collective-permute-start | bytes 491528 | tf_op jit(solution)/shard_map/ppermute | solution.py:338
  655.8 90.5 %collective-permute-start.41 = (bf16[512,2048]{1,0:T(8,128)(2,1)}, bf16[512,2048]{1,0:T(8,128)(2,1)}, u32[]{:S(2)}, u32[]{:S(2)}) collective-permute-start(bf16[512,2048]{1,0:T(8,128)(2,1)} %get-tuple-element.398), channel_id=1, source_target_pairs={{0,1},{1,0},{2,3},{3,2},{4,5},{5,4},{6,7},{7,6},{8,9},{9,8},{10,11... | collective-permute-start | bytes 6291464 | tf_op jit(solution)/shard_map/ppermute | solution.py:338
  724.4 43.4 %collective-permute-start.40 = (bf16[512,2048]{1,0:T(8,128)(2,1)}, bf16[512,2048]{1,0:T(8,128)(2,1)}, u32[]{:S(2)}, u32[]{:S(2)}) collective-permute-start(bf16[512,2048]{1,0:T(8,128)(2,1)} %get-tuple-element.400), channel_id=1, source_target_pairs={{0,1},{1,0},{2,3},{3,2},{4,5},{5,4},{6,7},{7,6},{8,9},{9,8},{10,11... | collective-permute-start | bytes 6291464 | tf_op jit(solution)/shard_map/ppermute | solution.py:338
  811.4 71.9 %collective-permute-start.42 = (f32[2,2,2,2,352,128]{5,4,3,2,1,0:T(8,128)}, f32[2,2,2,2,352,128]{5,4,3,2,1,0:T(8,128)}, u32[]{:S(2)}, u32[]{:S(2)}) collective-permute-start(f32[2,2,2,2,352,128]{5,4,3,2,1,0:T(8,128)} %slice_bitcast_fusion), channel_id=1, source_target_pairs={{0,2},{2,0},{1,3},{3,1},{4,6},{6,4},{5,7},{7,5},{8,10},{10,8},{9,1... | collective-permute-start | bytes 8650760 | tf_op jit(solution)/shard_map/ppermute | solution.py:338
  815.5 61.6 %collective-permute-start.43 = (f32[2,2,2,2,336,128]{5,4,3,2,1,0:T(8,128)}, f32[2,2,2,2,336,128]{5,4,3,2,1,0:T(8,128)}, u32[]{:S(2)}, u32[]{:S(2)}) collective-permute-start(f32[2,2,2,2,336,128]{5,4,3,2,1,0:T(8,128)} %slice_bitcast_fusion.2), channel_id=1, source_target_pairs={{0,4},{4,0},{8,12},{12,8},{16,20},{20,16},{24,28},{28,24},{1,5},{5... | collective-permute-start | bytes 8257544 | tf_op jit(solution)/shard_map/ppermute | solution.py:338
  817.7 62.5 %collective-permute-start.44 = (f32[2,2,2,2,336,128]{5,4,3,2,1,0:T(8,128)}, f32[2,2,2,2,336,128]{5,4,3,2,1,0:T(8,128)}, u32[]{:S(2)}, u32[]{:S(2)}) collective-permute-start(f32[2,2,2,2,336,128]{5,4,3,2,1,0:T(8,128)} %slice_bitcast_fusion.1), channel_id=1, source_target_pairs={{0,8},{4,12},{8,0},{12,4},{16,24},{20,28},{24,16},{28,20},{1,9},{5... | collective-permute-start | bytes 8257544 | tf_op jit(solution)/shard_map/ppermute | solution.py:338
  866.8 28.2 %collective-permute-start.69 = (bf16[512,1024]{1,0:T(8,128)(2,1)}, bf16[512,1024]{1,0:T(8,128)(2,1)}, u32[]{:S(2)}, u32[]{:S(2)}) collective-permute-start(bf16[512,1024]{1,0:T(8,128)(2,1)} %get-tuple-element.403), channel_id=1, source_target_pairs={{0,1},{1,0},{2,3},{3,2},{4,5},{5,4},{6,7},{7,6},{8,9},{9,8},{10,11... | collective-permute-start | bytes 3145736 | tf_op jit(solution)/shard_map/ppermute | solution.py:338
  887.6 58.3 %collective-permute-start.46 = (f32[2,2,2,336,128]{4,3,2,1,0:T(8,128)}, f32[2,2,2,336,128]{4,3,2,1,0:T(8,128)}, u32[]{:S(2)}, u32[]{:S(2)}) collective-permute-start(f32[2,2,2,336,128]{4,3,2,1,0:T(8,128)} %slice_bitcast_fusion.11), channel_id=1, source_target_pairs={{0,8},{4,12},{8,0},{12,4},{16,24},{20,28},{24,16},{28,20},{1,9},{5... | collective-permute-start | bytes 4128776 | tf_op jit(solution)/shard_map/ppermute | solution.py:338
  888.9 61.7 %collective-permute-start.47 = (f32[2,2,2,336,128]{4,3,2,1,0:T(8,128)}, f32[2,2,2,336,128]{4,3,2,1,0:T(8,128)}, u32[]{:S(2)}, u32[]{:S(2)}) collective-permute-start(f32[2,2,2,336,128]{4,3,2,1,0:T(8,128)} %slice_bitcast_fusion.10), channel_id=1, source_target_pairs={{0,16},{4,20},{8,24},{12,28},{16,0},{20,4},{24,8},{28,12},{1,17},{... | collective-permute-start | bytes 4128776 | tf_op jit(solution)/shard_map/ppermute | solution.py:338
  891.9 61.3 %collective-permute-start.45 = (f32[2,2,2,352,128]{4,3,2,1,0:T(8,128)}, f32[2,2,2,352,128]{4,3,2,1,0:T(8,128)}, u32[]{:S(2)}, u32[]{:S(2)}) collective-permute-start(f32[2,2,2,352,128]{4,3,2,1,0:T(8,128)} %slice_bitcast_fusion.5), channel_id=1, source_target_pairs={{0,4},{4,0},{8,12},{12,8},{16,20},{20,16},{24,28},{28,24},{1,5},{5... | collective-permute-start | bytes 4325384 | tf_op jit(solution)/shard_map/ppermute | solution.py:338
  960.9 31.5 %collective-permute-start.48 = (f32[2,2,352,128]{3,2,1,0:T(8,128)S(1)}, f32[2,2,352,128]{3,2,1,0:T(8,128)S(1)}, u32[]{:S(2)}, u32[]{:S(2)}) collective-permute-start(f32[2,2,352,128]{3,2,1,0:T(8,128)S(1)} %slice_bitcast_fusion.14), channel_id=1, source_target_pairs={{0,8},{4,12},{8,0},{12,4},{16,24},{20,28},{24,16},{28,20},{1,9},{5... | collective-permute-start | bytes 2162696 | tf_op jit(solution)/shard_map/ppermute | solution.py:338
  961.0 31.1 %collective-permute-start.49 = (f32[2,2,336,128]{3,2,1,0:T(8,128)S(1)}, f32[2,2,336,128]{3,2,1,0:T(8,128)S(1)}, u32[]{:S(2)}, u32[]{:S(2)}) collective-permute-start(f32[2,2,336,128]{3,2,1,0:T(8,128)S(1)} %slice_bitcast_fusion.20), channel_id=1, source_target_pairs={{0,16},{4,20},{8,24},{12,28},{16,0},{20,4},{24,8},{28,12},{1,17},{... | collective-permute-start | bytes 2064392 | tf_op jit(solution)/shard_map/ppermute | solution.py:338
  964.4 27.9 %collective-permute-start.50 = (f32[2,2,336,128]{3,2,1,0:T(8,128)S(1)}, f32[2,2,336,128]{3,2,1,0:T(8,128)S(1)}, u32[]{:S(2)}, u32[]{:S(2)}) collective-permute-start(f32[2,2,336,128]{3,2,1,0:T(8,128)S(1)} %slice_bitcast_fusion.19), channel_id=1, source_target_pairs={{0,2},{2,0},{1,3},{3,1},{4,6},{6,4},{5,7},{7,5},{8,10},{10,8},{9,1... | collective-permute-start | bytes 2064392 | tf_op jit(solution)/shard_map/ppermute | solution.py:338
  967.5 43.2 %collective-permute-start.68 = (bf16[512,1024]{1,0:T(8,128)(2,1)}, bf16[512,1024]{1,0:T(8,128)(2,1)}, u32[]{:S(2)}, u32[]{:S(2)}) collective-permute-start(bf16[512,1024]{1,0:T(8,128)(2,1)} %get-tuple-element.405), channel_id=1, source_target_pairs={{0,1},{1,0},{2,3},{3,2},{4,5},{5,4},{6,7},{7,6},{8,9},{9,8},{10,11... | collective-permute-start | bytes 3145736 | tf_op jit(solution)/shard_map/ppermute | solution.py:338
  994.3 33.8 %collective-permute-start.51 = (f32[2,352,128]{2,1,0:T(8,128)}, f32[2,352,128]{2,1,0:T(8,128)}, u32[]{:S(2)}, u32[]{:S(2)}) collective-permute-start(f32[2,352,128]{2,1,0:T(8,128)} %slice_bitcast_fusion.27), channel_id=1, source_target_pairs={{0,16},{4,20},{8,24},{12,28},{16,0},{20,4},{24,8},{28,12},{1,17},{... | collective-permute-start | bytes 1081352 | tf_op jit(solution)/shard_map/ppermute | solution.py:338
  995.8 28.6 %collective-permute-start.52 = (f32[2,336,128]{2,1,0:T(8,128)}, f32[2,336,128]{2,1,0:T(8,128)}, u32[]{:S(2)}, u32[]{:S(2)}) collective-permute-start(f32[2,336,128]{2,1,0:T(8,128)} %slice_bitcast_fusion.33), channel_id=1, source_target_pairs={{0,2},{2,0},{1,3},{3,1},{4,6},{6,4},{5,7},{7,5},{8,10},{10,8},{9,1... | collective-permute-start | bytes 1032200 | tf_op jit(solution)/shard_map/ppermute | solution.py:338
  998.1 28.1 %collective-permute-start.53 = (f32[2,336,128]{2,1,0:T(8,128)}, f32[2,336,128]{2,1,0:T(8,128)}, u32[]{:S(2)}, u32[]{:S(2)}) collective-permute-start(f32[2,336,128]{2,1,0:T(8,128)} %slice_bitcast_fusion.32), channel_id=1, source_target_pairs={{0,4},{4,0},{8,12},{12,8},{16,20},{20,16},{24,28},{28,24},{1,5},{5... | collective-permute-start | bytes 1032200 | tf_op jit(solution)/shard_map/ppermute | solution.py:338
  1009.7 82.2 %collective-permute-start.82 = (f32[2,2,2,2,288,128]{5,4,3,2,1,0:T(8,128)}, f32[2,2,2,2,288,128]{5,4,3,2,1,0:T(8,128)}, u32[]{:S(2)}, u32[]{:S(2)}) collective-permute-start(f32[2,2,2,2,288,128]{5,4,3,2,1,0:T(8,128)} %dynamic-slice_bitcast_fusion), channel_id=1, source_target_pairs={{0,1},{1,0},{2,3},{3,2},{4,5},{5,4},{6,7},{7,6},{8,9},{9,8},{10,11... | collective-permute-start | bytes 7077896 | tf_op jit(solution)/shard_map/ppermute | solution.py:338
  1076.7 48.5 %collective-permute-start.78 = (f32[2,2,2,1,336,128]{5,4,2,1,0,3:T(8,128)}, f32[2,2,2,1,336,128]{5,4,2,1,0,3:T(8,128)}, u32[]{:S(2)}, u32[]{:S(2)}) collective-permute-start(f32[2,2,2,1,336,128]{5,4,2,1,0,3:T(8,128)} %slice_bitcast_fusion.8), channel_id=1, source_target_pairs={{0,8},{4,12},{8,0},{12,4},{16,24},{20,28},{24,16},{28,20},{1,9},{5... | collective-permute-start | bytes 4128776 | tf_op jit(solution)/shard_map/ppermute | solution.py:338
  1078.0 51.4 %collective-permute-start.74 = (f32[2,2,2,1,336,128]{5,4,2,1,0,3:T(8,128)}, f32[2,2,2,1,336,128]{5,4,2,1,0,3:T(8,128)}, u32[]{:S(2)}, u32[]{:S(2)}) collective-permute-start(f32[2,2,2,1,336,128]{5,4,2,1,0,3:T(8,128)} %slice_bitcast_fusion.9), channel_id=1, source_target_pairs={{0,4},{4,0},{8,12},{12,8},{16,20},{20,16},{24,28},{28,24},{1,5},{5... | collective-permute-start | bytes 4128776 | tf_op jit(solution)/shard_map/ppermute | solution.py:338
  1079.5 54.4 %collective-permute-start.70 = (f32[2,2,2,1,352,128]{5,4,2,1,0,3:T(8,128)}, f32[2,2,2,1,352,128]{5,4,2,1,0,3:T(8,128)}, u32[]{:S(2)}, u32[]{:S(2)}) collective-permute-start(f32[2,2,2,1,352,128]{5,4,2,1,0,3:T(8,128)} %slice_bitcast_fusion.4), channel_id=1, source_target_pairs={{0,2},{2,0},{1,3},{3,1},{4,6},{6,4},{5,7},{7,5},{8,10},{10,8},{9,1... | collective-permute-start | bytes 4325384 | tf_op jit(solution)/shard_map/ppermute | solution.py:338
  1086.1 180.7 %all-to-all-start.9 = ((f32[32,32,1024]{2,1,0:T(8,128)}), f32[32,32,1024]{2,1,0:T(8,128)}, u32[]{:S(2)}, u32[]{:S(2)}) async-start(f32[32,32,1024]{2,1,0:T(8,128)} %bitcast.801), calls=%async_computation.9 | async-start | bytes 8388608 | tf_op jit(solution)/shard_map/all_to_all | solution.py:311
  1094.8 138.8 %collective-permute-start.83 = (f32[2,2,2,288,128]{4,3,2,1,0:T(8,128)S(1)}, f32[2,2,2,288,128]{4,3,2,1,0:T(8,128)S(1)}, u32[]{:S(2)}, u32[]{:S(2)}) collective-permute-start(f32[2,2,2,288,128]{4,3,2,1,0:T(8,128)S(1)} %dynamic-slice_bitcast_fusion.1), channel_id=1, source_target_pairs={{0,2},{2,0},{1,3},{3,1},{4,6},{6,4},{5,7},{7,5},{8,10},{10,8},{9,1... | collective-permute-start | bytes 3538952 | tf_op jit(solution)/shard_map/ppermute | solution.py:338
  1126.8 88.7 %collective-permute-start.79 = (f32[2,2,1,336,128]{4,3,1,0,2:T(8,128)S(1)}, f32[2,2,1,336,128]{4,3,1,0,2:T(8,128)S(1)}, u32[]{:S(2)}, u32[]{:S(2)}) collective-permute-start(f32[2,2,1,336,128]{4,3,1,0,2:T(8,128)S(1)} %slice_bitcast_fusion.15), channel_id=1, source_target_pairs={{0,16},{4,20},{8,24},{12,28},{16,0},{20,4},{24,8},{28,12},{1,17},{... | collective-permute-start | bytes 2064392 | tf_op jit(solution)/shard_map/ppermute | solution.py:338
  1130.9 85.6 %collective-permute-start.75 = (f32[2,2,1,336,128]{4,3,1,0,2:T(8,128)S(1)}, f32[2,2,1,336,128]{4,3,1,0,2:T(8,128)S(1)}, u32[]{:S(2)}, u32[]{:S(2)}) collective-permute-start(f32[2,2,1,336,128]{4,3,1,0,2:T(8,128)S(1)} %slice_bitcast_fusion.17), channel_id=1, source_target_pairs={{0,8},{4,12},{8,0},{12,4},{16,24},{20,28},{24,16},{28,20},{1,9},{5... | collective-permute-start | bytes 2064392 | tf_op jit(solution)/shard_map/ppermute | solution.py:338
  1135.6 81.1 %collective-permute-start.71 = (f32[2,2,1,352,128]{4,3,1,0,2:T(8,128)S(1)}, f32[2,2,1,352,128]{4,3,1,0,2:T(8,128)S(1)}, u32[]{:S(2)}, u32[]{:S(2)}) collective-permute-start(f32[2,2,1,352,128]{4,3,1,0,2:T(8,128)S(1)} %slice_bitcast_fusion.12), channel_id=1, source_target_pairs={{0,4},{4,0},{8,12},{12,8},{16,20},{20,16},{24,28},{28,24},{1,5},{5... | collective-permute-start | bytes 2162696 | tf_op jit(solution)/shard_map/ppermute | solution.py:338
  1303.2 26.8 %collective-permute-start.96 = (f32[1024,128]{1,0:T(8,128)S(1)}, f32[1024,128]{1,0:T(8,128)S(1)}, u32[]{:S(2)}, u32[]{:S(2)}) collective-permute-start(f32[1024,128]{1,0:T(8,128)S(1)} %get-tuple-element.419), channel_id=1, source_target_pairs={{0,1},{1,0},{2,3},{3,2},{4,5},{5,4},{6,7},{7,6},{8,9},{9,8},{10,11... | collective-permute-start | bytes 1572872 | tf_op jit(solution)/shard_map/ppermute | solution.py:338
  1331.5 33.9 %collective-permute-start.105 = (bf16[1,336,256]{2,1,0:T(8,128)(2,1)S(1)}, bf16[1,336,256]{2,1,0:T(8,128)(2,1)S(1)}, u32[]{:S(2)}, u32[]{:S(2)}) collective-permute-start(bf16[1,336,256]{2,1,0:T(8,128)(2,1)S(1)} %get-tuple-element.423), channel_id=1, source_target_pairs={{0,4},{4,0},{8,12},{12,8},{16,20},{20,16},{24,28},{28,24},{1,5},{5... | collective-permute-start | bytes 516104 | tf_op jit(solution)/shard_map/ppermute | solution.py:338
  1332.1 33.9 %collective-permute-start.101 = (bf16[1,336,256]{2,1,0:T(8,128)(2,1)S(1)}, bf16[1,336,256]{2,1,0:T(8,128)(2,1)S(1)}, u32[]{:S(2)}, u32[]{:S(2)}) collective-permute-start(bf16[1,336,256]{2,1,0:T(8,128)(2,1)S(1)} %get-tuple-element.422), channel_id=1, source_target_pairs={{0,2},{2,0},{1,3},{3,1},{4,6},{6,4},{5,7},{7,5},{8,10},{10,8},{9,1... | collective-permute-start | bytes 516104 | tf_op jit(solution)/shard_map/ppermute | solution.py:338
  1335.1 32.1 %collective-permute-start.97 = (bf16[1,352,256]{2,1,0:T(8,128)(2,1)S(1)}, bf16[1,352,256]{2,1,0:T(8,128)(2,1)S(1)}, u32[]{:S(2)}, u32[]{:S(2)}) collective-permute-start(bf16[1,352,256]{2,1,0:T(8,128)(2,1)S(1)} %slice_bitcast_fusion.40), channel_id=1, source_target_pairs={{0,16},{4,20},{8,24},{12,28},{16,0},{20,4},{24,8},{28,12},{1,17},{... | collective-permute-start | bytes 540680 | tf_op jit(solution)/shard_map/ppermute | solution.py:338
  1373.5 38.3 %collective-permute-start.107 = (bf16[4,336,256]{2,1,0:T(8,128)(2,1)S(1)}, bf16[4,336,256]{2,1,0:T(8,128)(2,1)S(1)}, u32[]{:S(2)}, u32[]{:S(2)}) collective-permute-start(bf16[4,336,256]{2,1,0:T(8,128)(2,1)S(1)} %pad_maximum_fusion.19), channel_id=1, source_target_pairs={{0,16},{4,20},{8,24},{12,28},{16,0},{20,4},{24,8},{28,12},{1,17},{... | collective-permute-start | bytes 2064392 | tf_op jit(solution)/shard_map/ppermute | solution.py:338
  1386.6 28.7 %collective-permute-start.103 = (bf16[4,336,256]{2,1,0:T(8,128)(2,1)S(1)}, bf16[4,336,256]{2,1,0:T(8,128)(2,1)S(1)}, u32[]{:S(2)}, u32[]{:S(2)}) collective-permute-start(bf16[4,336,256]{2,1,0:T(8,128)(2,1)S(1)} %pad_maximum_fusion.18), channel_id=1, source_target_pairs={{0,8},{4,12},{8,0},{12,4},{16,24},{20,28},{24,16},{28,20},{1,9},{5... | collective-permute-start | bytes 2064392 | tf_op jit(solution)/shard_map/ppermute | solution.py:338
  1386.8 29.9 %collective-permute-start.99 = (bf16[4,352,256]{2,1,0:T(8,128)(2,1)S(1)}, bf16[4,352,256]{2,1,0:T(8,128)(2,1)S(1)}, u32[]{:S(2)}, u32[]{:S(2)}) collective-permute-start(bf16[4,352,256]{2,1,0:T(8,128)(2,1)S(1)} %pad_maximum_fusion.15), channel_id=1, source_target_pairs={{0,4},{4,0},{8,12},{12,8},{16,20},{20,16},{24,28},{28,24},{1,5},{5... | collective-permute-start | bytes 2162696 | tf_op jit(solution)/shard_map/ppermute | solution.py:338
  1411.9 32.1 %collective-permute-start.108 = (bf16[8,336,256]{2,1,0:T(8,128)(2,1)S(1)}, bf16[8,336,256]{2,1,0:T(8,128)(2,1)S(1)}, u32[]{:S(2)}, u32[]{:S(2)}) collective-permute-start(bf16[8,336,256]{2,1,0:T(8,128)(2,1)S(1)} %pad_maximum_fusion.12), channel_id=1, source_target_pairs={{0,8},{4,12},{8,0},{12,4},{16,24},{20,28},{24,16},{28,20},{1,9},{5... | collective-permute-start | bytes 4128776 | tf_op jit(solution)/shard_map/ppermute | solution.py:338
  1415.5 28.8 %collective-permute-start.104 = (bf16[8,336,256]{2,1,0:T(8,128)(2,1)S(1)}, bf16[8,336,256]{2,1,0:T(8,128)(2,1)S(1)}, u32[]{:S(2)}, u32[]{:S(2)}) collective-permute-start(bf16[8,336,256]{2,1,0:T(8,128)(2,1)S(1)} %pad_maximum_fusion.11), channel_id=1, source_target_pairs={{0,4},{4,0},{8,12},{12,8},{16,20},{20,16},{24,28},{28,24},{1,5},{5... | collective-permute-start | bytes 4128776 | tf_op jit(solution)/shard_map/ppermute | solution.py:338
  1416.9 29.1 %collective-permute-start.100 = (bf16[8,352,256]{2,1,0:T(8,128)(2,1)S(1)}, bf16[8,352,256]{2,1,0:T(8,128)(2,1)S(1)}, u32[]{:S(2)}, u32[]{:S(2)}) collective-permute-start(bf16[8,352,256]{2,1,0:T(8,128)(2,1)S(1)} %pad_maximum_fusion.10), channel_id=1, source_target_pairs={{0,2},{2,0},{1,3},{3,1},{4,6},{6,4},{5,7},{7,5},{8,10},{10,8},{9,1... | collective-permute-start | bytes 4325384 | tf_op jit(solution)/shard_map/ppermute | solution.py:338
  (230 other events, 4809.9 us)
Sparse Core Ops, SparseCore 0:
  11.5 123.4 all-gather.4
  138.4 115.3 all-gather.6

commit v3 on v2

--- a/solution.py
+++ b/solution.py
@@ -138,24 +138,18 @@
         act_low,
         second_pull,
     )
-    return (output, stored)
-
-
-def layer_backward(grad_out, stored, params, allowed):
+    shared = (
+        share(middle_low[0].T, 1),
+        share_half(act_low[0]),
+        share(inputs[0].T, 1),
+        swap_pick(inputs[0].T, context[0].T, 1),
+    )
+    return (output, stored, shared)
+
+
+def layer_backward(grad_out, stored, shared, params, allowed):
     w_query, w_key, w_value, w_out, w_up, w_down, _, _ = params
-    (
-        inputs,
-        queries,
-        key_proj,
-        values,
-        log_total,
-        context,
-        first_pull,
-        middle_low,
-        gelu_pull,
-        act_low,
-        second_pull,
-    ) = stored
+    (_, queries, key_proj, values, log_total, _, first_pull, _, gelu_pull, _, second_pull) = stored
     count, length, model_width = grad_out.shape
     grad_ffn, grad_gain_two, grad_shift_two = second_pull(grad_out)
     down_low = grad_ffn.astype(jnp.bfloat16)
@@ -163,10 +157,10 @@
     up_low = grad_up.astype(jnp.bfloat16)
     wide_count = lax.axis_size("wide")
     operands = (
-        share(middle_low[0].T, 1),
+        shared[0],
         share(down_low[0].T, 1),
         share_half(up_low[0]),
-        share_half(act_low[0]),
+        shared[1],
     )
     if FF // (4 * wide_count) == lanes:
         grad_mats_ffn = ffn_weight_grads(*operands, wide_count)
@@ -214,8 +208,8 @@
     for step in range(3, len(routes(wide_count)[0])):
         parts = reduce_step(parts, wide_count, step)
     operands = (
-        share(inputs[0].T, 1),
-        swap_pick(inputs[0].T, context[0].T, 1),
+        shared[2],
+        shared[3],
         swap_pick(grad_query[0], grad_key[0], 0),
         swap_pick(grad_value[0], attn_low[0], 0),
     )
@@ -265,11 +259,6 @@
     return current
 
 
-def gather_columns(columns, with_pair):
-    wide_count = lax.axis_size("wide")
-    return gather_relative(columns[0].astype(jnp.bfloat16), wide_count, 0, tile, with_pair)
-
-
 def gram_of(found):
     return jnp.einsum("wdc,wec->de", found, found, preferred_element_type=jnp.float32)[None]
 
@@ -359,22 +348,17 @@
     return [(start, start + size) for start, size in zip(starts, sizes) if size]
 
 
-def reduce_blocks(values, wide_count, axis, unit):
-    bits = wide_bits(wide_count)[::-1] + [("pair", 1)]
-    parts = []
-    for route, (start, stop) in zip(routes(wide_count), cuts(values.shape[2 + axis], unit)):
-        part = lax.slice_in_dim(values, start, stop, axis=2 + axis)
-        part = part.reshape((2,) * len(bits) + part.shape[2:])
-        left = list(bits)
-        for bit in route:
-            part = halve(part, bit, left.index(bit))
-            left.remove(bit)
-        parts.append(part)
-    return jnp.concatenate(parts, axis=axis)
-
-
 def here16():
     return lax.axis_index("wide") * 2 + lax.axis_index("pair")
+
+
+def lockstep(*groups):
+    flat = lax.optimization_barrier(sum((list(group) for group in groups), []))
+    found = []
+    for group in groups:
+        found.append(flat[: len(group)])
+        flat = flat[len(group) :]
+    return found
 
 
 def reduce_step(parts, wide_count, step):
@@ -389,38 +373,66 @@
     return value, parts
 
 
-def reduce_relative(parts, wide_count):
-    done = []
+def static_step(part, left, bit):
+    dim = left.index(bit)
+    keep = lax.index_in_dim(part, 0, dim, keepdims=False)
+    return keep + exchange(lax.index_in_dim(part, 1, dim, keepdims=False), bit)
+
+
+def route_parts(values, wide_count):
+    bits = wide_bits(wide_count)[::-1] + [("pair", 1)]
+    return [
+        values[..., start:stop].reshape((2,) * len(bits) + (values.shape[1], stop - start))
+        for start, stop in cuts(values.shape[-1], lanes)
+    ]
+
+
+def route_step(parts, wide_count, step, static):
+    bits = wide_bits(wide_count)[::-1] + [("pair", 1)]
+    found = []
     for part, route in zip(parts, routes(wide_count)):
-        for bit in route:
-            part = part[0] + exchange(part[1], bit)
-        done.append(part)
-    return done
+        left = [bit for bit in bits if bit not in route[:step]]
+        if static:
+            found.append(static_step(part, left, route[step]))
+        else:
+            found.append(halve(part, route[step], left.index(route[step])))
+    return found
 
 
 def reduce_rows(values, wide_count):
-    bits = wide_bits(wide_count)[::-1] + [("pair", 1)]
-    parts = []
-    for route, (start, stop) in zip(routes(wide_count), cuts(values.shape[-1], lanes)):
-        part = values[..., start:stop].reshape((2,) * len(bits) + (values.shape[1], stop - start))
-        left = list(bits)
-        for bit in route:
-            dim = left.index(bit)
-            left.remove(bit)
-            keep = lax.index_in_dim(part, 0, dim, keepdims=False)
-            part = keep + exchange(lax.index_in_dim(part, 1, dim, keepdims=False), bit)
-        parts.append(part)
+    parts = route_parts(values, wide_count)
+    for step in range(len(routes(wide_count)[0])):
+        (parts,) = lockstep(route_step(parts, wide_count, step, True))
     return jnp.concatenate(parts, axis=-1)
 
 
-def gather_relative(block, wide_count, axis, unit, with_pair=True):
-    parts = []
-    for route, (start, stop) in zip(routes(wide_count, with_pair), cuts(block.shape[axis], unit)):
-        part = lax.slice_in_dim(block, start, stop, axis=axis)[None]
-        for bit in route[::-1]:
-            part = jnp.concatenate([part, exchange(part, bit)])
-        parts.append(relative_order(part, route[::-1]))
-    return jnp.concatenate(parts, axis=1 + axis)
+def gather_start(block, axis, unit):
+    return [
+        lax.slice_in_dim(block, start, stop, axis=axis)[None]
+        for start, stop in cuts(block.shape[axis], unit)
+    ]
+
+
+def gather_step(parts, wide_count, step, with_pair=True):
+    return [
+        jnp.concatenate([part, exchange(part, route[::-1][step])])
+        for part, route in zip(parts, routes(wide_count, with_pair))
+    ]
+
+
+def gather_end(parts, wide_count, axis, with_pair=True):
+    ordered = [
+        relative_order(part, route[::-1])
+        for part, route in zip(parts, routes(wide_count, with_pair))
+    ]
+    return jnp.concatenate(ordered, axis=1 + axis)
+
+
+def gather_relative(block, wide_count, axis, unit):
+    parts = gather_start(block, axis, unit)
+    for step in range(len(routes(wide_count)[0])):
+        (parts,) = lockstep(gather_step(parts, wide_count, step))
+    return gather_end(parts, wide_count, axis)
 
 
 def route_shape(route, covered):
@@ -659,6 +671,47 @@
     )(blocks)
 
 
+def unpack_kernel(*refs):
+    half = len(refs) * 2 // 3
+    for place, out_ref in enumerate(refs[half:]):
+        out_ref[:, :lanes] = refs[2 * place][...].reshape(D, lanes)
+        out_ref[:, lanes:] = refs[2 * place + 1][...].reshape(D, lanes)
+
+
+def unpack_attn(merged, wide_count, narrow_count):
+    specs = [
+        pl.BlockSpec((1, D, lanes), lambda step, add=step_add, kind=kind: (
+            (2 * step + add) * narrow_count + kind, 0, 0
+        ))
+        for kind in range(narrow_count)
+        for step_add in range(2)
+    ]
+    return pl.pallas_call(
+        unpack_kernel,
+        grid=(wide_count // 2,),
+        in_specs=specs,
+        out_specs=[pl.BlockSpec((D, 2 * lanes), lambda step: (0, step))] * narrow_count,
+        out_shape=[jax.ShapeDtypeStruct((D, D), merged.dtype)] * narrow_count,
+    )(*[merged] * len(specs))
+
+
+def unpack_ffn(blocks, wide_count):
+    specs = [
+        pl.BlockSpec((1, 1, D, lanes), lambda step, kind=kind, pair=pair: (
+            step % wide_count * 4 + pair * 2 + step // wide_count, kind, 0, 0
+        ))
+        for kind in range(2)
+        for pair in range(2)
+    ]
+    return pl.pallas_call(
+        unpack_kernel,
+        grid=(2 * wide_count,),
+        in_specs=specs,
+        out_specs=[pl.BlockSpec((D, 2 * lanes), lambda step: (0, step))] * 2,
+        out_shape=[jax.ShapeDtypeStruct((D, FF), blocks.dtype)] * 2,
+    )(*[blocks] * 4)
+
+
 def split_kernel(front_ref, rest_ref, out_ref, *, starts):
     front, rows = front_ref.shape[0], out_ref.shape[1]
     total = front + rest_ref.shape[0]
@@ -674,7 +727,7 @@
             out_ref[dev, rows - left :] = jnp.zeros((left, lanes), out_ref.dtype)
 
 
-def scatter_flat(front, rest, size, device, devices):
+def scatter_flat(front, rest, size, devices):
     wide_count = lax.axis_size("wide")
     starts, rows = flat_blocks(size, devices)
     blocks = pl.pallas_call(
@@ -683,9 +736,17 @@
     )(front, rest)
     bits = wide_bits(wide_count)[::-1] + [("pair", 1), side_bit]
     part = blocks.reshape((2,) * len(bits) + blocks.shape[1:])
-    for bit in [side_bit] + routes(wide_count)[0]:
-        part = halve(part, bit, bits.index(bit))
-        bits.remove(bit)
+    return halve(part, side_bit, len(bits) - 1)
+
+
+def other_step(part, wide_count, step):
+    bits = wide_bits(wide_count)[::-1] + [("pair", 1)]
+    route = routes(wide_count)[0]
+    left = [bit for bit in bits if bit not in route[:step]]
+    return halve(part, route[step], left.index(route[step]))
+
+
+def own_share(part, size, device):
     return lax.dynamic_slice(part.reshape(-1), (device * size % (tile * lanes),), (size,))
 
 
@@ -725,13 +786,14 @@
     if col_width == lanes:
         merged = jnp.concatenate([attn_own.reshape(-1, lanes), other_own])
         merged = lax.all_gather(merged, everyone)
-        attn_all, other_all = merged[:, : kinds * D], merged[:, kinds * D :]
+        other_all = merged[:, kinds * D :]
+        attn_low = unpack_attn(merged, wide_count, narrow_count)
     else:
         attn_all = lax.all_gather(attn_own, everyone)
         other_all = lax.all_gather(other_own, everyone)
+        attn_all = attn_all.reshape(wide_count, narrow_count * kinds, D, col_width)
+        attn_low = attn_all.transpose(1, 2, 0, 3).reshape(narrow_count * kinds, D, D)
     other_flat = join_flat(other_all, size)
-    attn_all = attn_all.reshape(wide_count, narrow_count * kinds, D, col_width)
-    attn_low = attn_all.transpose(1, 2, 0, 3).reshape(narrow_count * kinds, D, D)
     ffn_all = lax.all_gather(ffn_mats.astype(jnp.bfloat16), everyone)
     bias_rows = V // lanes
     up_rows = bias_rows + L * FF // lanes
@@ -821,9 +883,11 @@
     fetched, source_cut, source_total = lax.optimization_barrier(
         (fetched, source_cut, source_total)
     )
-    ffn_all, source_cut = lax.optimization_barrier((ffn_all, source_cut))
-    ffn_low = ffn_all.reshape(devices // 2, 2, 2 * L, D, ffn_width)
-    ffn_low = ffn_low.transpose(2, 3, 1, 0, 4).reshape(2 * L, D, FF)
+    if ffn_width == lanes:
+        ffn_low = unpack_ffn(ffn_all, wide_count)
+    else:
+        ffn_low = ffn_all.reshape(devices // 2, 2, 2 * L, D, ffn_width)
+        ffn_low = ffn_low.transpose(2, 3, 1, 0, 4).reshape(2 * L, D, FF)
     source_here = swap_all(source_cut)
     token_rows = select_rows(now, fetched)
     place_part = select_rows(held, fetched).astype(jnp.bfloat16)
@@ -856,7 +920,7 @@
         up_biases[0],
         vectors[2:10],
     )
-    hidden, stored = layer_forward(hidden, params, allowed)
+    hidden, stored, shared = layer_forward(hidden, params, allowed)
     picks = mask_pos.reshape(-1)
     head_in = select_rows(picks, hidden.reshape(WINDOW, D).astype(jnp.bfloat16))
     head_in = head_in.astype(jnp.bfloat16)
@@ -871,6 +935,7 @@
     rank_of_dev = (order_rows % 2 ^ side) * group + (order_rows // 2 ^ here)
     dev_of_rank = (order_rows % group ^ here) * 2 + (order_rows // group ^ side)
     head_all = gather_relative(head_low, wide_count, 1, lanes)
+    head_all, *shared = lax.optimization_barrier((head_all, *shared))
     head_all = jnp.concatenate([head_all, exchange(head_all, side_bit)]).reshape(rows_all, D)
     labels_all = pick_rows(labels_all.reshape(devices, MPW), dev_of_rank).reshape(rows_all, 1)
     is_live = jnp.arange(MPW, dtype=jnp.int32)[None, :] < pick_rows(counts_all[:, None], dev_of_rank)
@@ -922,14 +987,13 @@
     grad_head_in = jnp.einsum("rf,df->rd", pre_low, head_weight, preferred_element_type=jnp.float32)
     grad_hidden = add_rows(picks, grad_head_in, WINDOW).reshape(win_count, WINDOW, D)
     grad_hidden, layer_mats, up_grad, vec_grads = layer_backward(
-        grad_hidden, stored, params, allowed
+        grad_hidden, stored, shared, params, allowed
     )
     grad_embed, grad_emb_gain, grad_emb_shift = embed_pull(grad_hidden)
     flat_embed = grad_embed.reshape(WINDOW, D)
 
     ffn_parts, attn_parts = layer_mats[1], layer_mats[0]
     flat_embed, ffn_parts = tied(flat_embed, ffn_parts)
-    ffn_grad = jnp.concatenate(ffn_parts, axis=1)
     dec_block = jnp.zeros((devices * owned,), jnp.float32)
     dec_block = lax.dynamic_update_slice(dec_block, grad_dec, (device * owned,))[:V]
     vector_block = jnp.concatenate(
@@ -945,16 +1009,30 @@
             vector_block.reshape(-1, lanes),
         ]
     )
-    other_grad = scatter_flat(front, grad_head_w.reshape(-1, lanes), size, device, devices)
+    other_part = scatter_flat(front, grad_head_w.reshape(-1, lanes), size, devices)
 
     place_grad = flat_embed.reshape(per_place, group, D).transpose(1, 0, 2)
-    place_grad = place_grad.reshape(wide_count, narrow_count // 2, per_place, D)
-    place_grad = reduce_blocks(place_grad, wide_count, 1, 128)
-    place_grad, attn_parts = tied(place_grad, attn_parts)
-    attn_grad = jnp.concatenate(reduce_relative(attn_parts, wide_count), axis=1)
-    sent = add_rows(now, flat_embed, devices * slots) + add_rows(held, place_grad, devices * slots)
-    arrived = swap_all(sent.reshape(devices, slots, D)).reshape(-1, D)
-    table_grad = grad_words + add_rows(asked, arrived, owned)
+    ffn_grad = jnp.concatenate(ffn_parts, axis=1)
+    sent = add_rows(now, flat_embed, devices * slots)
+    arrived = swap_all(sent.reshape(devices, slots, D))
+    place_parts = route_parts(place_grad.reshape(group, per_place, D), wide_count)
+    for step in range(len(routes(wide_count)[0])):
+        place_parts, attn_parts, (other_part,) = lockstep(
+            route_step(place_parts, wide_count, step, False),
+            reduce_step(attn_parts, wide_count, step),
+            [other_step(other_part, wide_count, step)],
+        )
+    attn_grad = jnp.concatenate(attn_parts, axis=1)
+    other_grad = own_share(other_part, size, device)
+    place_grad = jnp.concatenate(place_parts, axis=-1)
+    place_grad = gather_relative(place_grad, wide_count, 1, lanes)
+    place_grad = jnp.concatenate([place_grad, exchange(place_grad, side_bit)])
+    turn = jnp.arange(devices, dtype=jnp.int32)[:, None]
+    place_ids = (turn // group ^ side) * WINDOW + (turn % group ^ here)
+    place_ids = place_ids + jnp.arange(per_place, dtype=jnp.int32)[None, :] * group
+    place_ids = (V - device * owned + place_ids).reshape(-1)
+    table_grad = grad_words + add_rows(asked, arrived.reshape(-1, D), owned)
+    table_grad = table_grad + add_rows(place_ids, place_grad.reshape(SEQ, D), owned)
 
     def more_grads(state):
         round_idx, grads = state
@@ -981,8 +1059,16 @@
     keep = jnp.where(second, ffn_moment_new[1], ffn_moment_new[0])
     got = exchange(jnp.where(second, ffn_moment_new[0], ffn_moment_new[1]), side_bit)
     ffn_pair = jnp.concatenate([keep, got], axis=1)[None]
-    attn_found = gather_columns(attn_moment_new, False)
-    ffn_found = gather_columns(ffn_pair, True)
+    attn_parts = gather_start(attn_moment_new[0].astype(jnp.bfloat16), 0, tile)
+    ffn_parts = gather_start(ffn_pair[0].astype(jnp.bfloat16), 0, tile)
+    steps = len(routes(wide_count)[0])
+    for step in range(steps - 1):
+        attn_parts, ffn_parts = lockstep(
+            gather_step(attn_parts, wide_count, step, False),
+            gather_step(ffn_parts, wide_count, step),
+        )
+    attn_found = gather_end(attn_parts, wide_count, 0, False)
+    ffn_found = gather_end(gather_step(ffn_parts, wide_count, steps - 1), wide_count, 0)
     attn_new = muon_cols(attn_mats, attn_moment_new, gram_of(attn_found), D)
     ffn_turn = newton_cols(ffn_pair, gram_of(ffn_found))[0]
     keep, give = ffn_turn[:, :ffn_width], ffn_turn[:, ffn_width:]

time: 1510 us -> 1550 us (1.026)
  local copies, waits for them, and re-layouts: 205 us -> 152 us
  Pallas kernels: 62 us -> 88 us
  waiting for transfers between devices: 614 us -> 637 us
  starting transfers between devices: 135 us -> 157 us
  other arithmetic: 152 us -> 171 us
    slice x15 -> x10, local copies, waits for them, and re-layouts: 58.3 us -> 5.86 us  [the longest x1 3.68 us: shards(): other_all = merged[:, kinds * D:]]
    pallas_call x0 -> x2, Pallas kernels: none -> 25.4 us  [the longest x1 17.9 us: unpack_ffn(): pl.pallas_call(unpack_kernel, grid=(2 * wide_count,), in_specs=specs, out...]
    ppermute x110 -> x123, starting transfers between devices: 104 us -> 126 us  [exchange(): return lax.ppermute(values, axis, steps)]
    concatenate x29 -> x48, other arithmetic: 3.28 us -> 23.8 us  [the longest x45 17.6 us: gather_step(): jnp.concatenate([part, exchange(part, route[::-1][step])])]
    ppermute x110 -> x123, waiting for transfers between devices: 540 us -> 557 us  [exchange(): return lax.ppermute(values, axis, steps)]
  transfers between devices with their start and end apart: 119 -> 132, of which waited for: 65 -> 72; matrix products, arithmetic and copies ran while one was open for 32% -> 32% of each run, Pallas kernels for 1% -> 3%
where the time goes in v3:
time: 1550 us; the launch traced here: 1530 us
  waiting for transfers between devices  637 us (41%)
  matrix products  300 us (19%)
  other arithmetic  171 us (11%)
  starting transfers between devices  157 us (10%)
  local copies, waits for them, and re-layouts  152 us (10%)
  Pallas kernels  88 us (6%)
  between operations  30.2 us (2%)
    ppermute x123, waiting for transfers between devices, exchange(): return lax.ppermute(values, axis, steps)  557 us
    ppermute x123, starting transfers between devices, exchange(): return lax.ppermute(values, axis, steps)  126 us
    all_to_all x7, waiting for transfers between devices, swap_all(): return lax.all_to_all(blocks, axes, 0, 0, tiled=True)  73.4 us
    dot_general x6, matrix products, project(): jnp.einsum('bsd,df->bsf', inputs, weight, preferred_element_type=jnp.floa...  52.7 us
  transfers between devices with their start and end apart: 132, of which 72 were waited for; matrix products, arithmetic and copies ran while one was open for 32% of the time, Pallas kernels for 3%

profile of v3, /device:TPU:0, one launch (start us, length us, event | category | flops | bytes accessed | tf_op | source)
XLA Modules:
  0.0 1534.6 jit_solution(6552241368103352589)
XLA Ops:
  18.7 7.3 all-to-all-start.4
  50.2 10.4 reshape.1680
  60.6 7.7 copy.517
  78.1 50.6 %all-to-all-done.5 = bf16[32,32,1024]{2,1,0:T(8,128)(2,1)S(1)} async-done(((bf16[32,32,1024]{2,1,0:T(8,128)(2,1)}), bf16[32,32,1024]{2,1,0:T(8,128)(2,1)S(1)}, u32[]{:S(2)}, u32[]{:S(2)}) %all-to-all-start.5) | async-done | bytes 2097184 | tf_op jit(solution)/shard_map/all_to_all | solution.py:300
  170.7 7.4 shard_map.311
  204.5 8.7 fusion.17
  213.2 9.3 exponential_reduce_fusion
  222.5 9.4 convolution_convert_fusion.1
  246.9 6.8 all-gather.7.cloned.1.call-done
  253.7 17.9 %shard_map.312 = (bf16[1024,4096]{1,0:T(8,128)(2,1)}, bf16[1024,4096]{1,0:T(8,128)(2,1)}) custom-call(bf16[32,2,1024,128]{3,2,1,0:T(8,128)(2,1)} %bitcast.768, bf16[32,2,1024,128]{3,2,1,0:T(8,128)(2,1)} %bitcast.769, bf16[32,2,1024,128]{3,2,1,0:T(8,128)(2,1)} %bitcast.770, bf16[32,2,1024,128]{3,2,1,0:T(8,128)(2,1)} %bitcast.771), custom_call_target="tpu_custom_call" | custom-call | tf_op jit(solution)/shard_map/pallas_call | solution.py:706
  271.6 27.8 %multiply_convert_fusion.1 = (bf16[512,4096]{1,0:T(8,128)(2,1)S(1)}, f32[512,4096]{1,0:T(8,128)}, f32[512,4096]{1,0:T(8,128)}) fusion(f32[4096]{0:T(1024)S(1)} %bitcast.897, bf16[1024,4096]{1,0:T(8,128)(2,1)} %get-tuple-element.355, f32[512,1024]{1,0:T(8,128)} %copy-done.2, f32[1024]{0:T(1024)S(1)} %get-tuple-element.636, f32[1024]{0:T(1024)S(1)} %get-tuple-element.637, ...), kind=kOutput, calls=%fused_computation.50 | convolution fusion | flops 4436000768 | bytes 31485952 | tf_op jit(solution)/shard_map/bsd,df->bsf/dot_general | solution.py:60
  320.4 14.4 collective-permute-done.14
  334.9 12.8 collective-permute-done.13
  347.7 81.7 %collective-permute-done.12 = bf16[1,80,384]{2,1,0:T(8,128)(2,1)S(1)} collective-permute-done((bf16[1,80,384]{2,1,0:T(8,128)(2,1)S(1)}, bf16[1,80,384]{2,1,0:T(8,128)(2,1)S(1)}, u32[]{:S(2)}, u32[]{:S(2)}) %collective-permute-start.12) | collective-permute-done | bytes 61472 | tf_op jit(solution)/shard_map/ppermute | solution.py:327
  441.2 8.9 collective-permute-done.20
  450.1 7.9 collective-permute-done.19
  491.2 11.6 fusion.295
  513.4 7.0 all-to-all-done.7
  524.4 6.9 all-to-all-done.8
  533.4 26.1 %shard_map.313 = (bf16[2560,992]{1,0:T(8,128)(2,1)}, f32[1,992]{1,0:T(1,128)}, f32[1,992]{1,0:T(1,128)}) custom-call(s32[3]{0:T(128)} %pad_add_fusion.facts, f32[2560,992]{1,0:T(8,128)} %get-tuple-element.658.logits_ref, bf16[32,80,992]{2,1,0:T(8,128)(2,1)} %all-to-all-done.6.source_ref, f32[2560,4]{1,0:T(8,128)} %copy.426.rows_ref), custom_call_target="tpu_custom_call" | custom-call | tf_op jit(solution)/shard_map/pallas_call | solution.py:587
  565.1 8.5 collective-permute-done.29
  581.8 7.2 fusion.296
  595.7 7.5 collective-permute-done.31
  607.7 12.6 collective-permute-done.35
  628.8 7.4 collective-permute-done.37
  655.5 10.9 convert_reduce_fusion
  701.8 17.6 %shard_map.314 = (f32[2,2,2,2,2,352,128]{6,5,4,3,2,1,0:T(8,128)}, f32[2,2,2,2,2,336,128]{6,5,4,3,2,1,0:T(8,128)}, f32[2,2,2,2,2,336,128]{6,5,4,3,2,1,0:T(8,128)}) custom-call(s32[2]{0:T(128)} %pad_add_fusion.1.here, bf16[1024,1024]{1,0:T(8,128)(2,1)} %copy.433.up_rows, bf16[1024,1024]{1,0:T(8,128)(2,1)} %copy.434.down_rows, ...), custom_call_target="tpu_custom_call" | custom-call | tf_op jit(solution)/shard_map/pallas_call | solution.py:462
  730.2 8.2 fusion.95
  743.6 10.3 convert_reduce_fusion.3
  759.2 9.5 fusion.298
  768.7 24.5 %fusion.143 = bf16[16,64,512]{2,1,0:T(8,128)(2,1)} fusion(bf16[512,16,64]{0,2,1:T(8,128)(2,1)S(1)} %bitcast.810, f32[16,512,512]{1,2,0:T(8,128)} %fusion.298, f32[16,512,512]{1,2,0:T(8,128)} %get-tuple-element.650, f32[16,512]{1,0:T(8,128)S(1)} %copy-done.107, pred[512,512]{0,1:T(8,128)(4,1)S(1)} %copy-done.66), kind=kOutput, calls=%fused_computation.248 | convolution fusion | flops 583541248 | bytes 35946496 | tf_op jit(solution)/shard_map/bnhqk,bnqhe->bnkhe/dot_general | solution.py:195
  819.2 24.7 %fusion.140 = bf16[16,64,512]{2,1,0:T(8,128)(2,1)} fusion(bf16[512,16,64]{0,2,1:T(8,128)(2,1)} %bitcast.860, f32[16,512,512]{1,2,0:T(8,128)} %fusion.298, f32[16,512,512]{1,2,0:T(8,128)} %get-tuple-element.650, f32[16,512]{1,0:T(8,128)S(1)} %copy-done.107, pred[512,512]{0,1:T(8,128)(4,1)S(1)} %copy-done.66), kind=kOutput, calls=%fused_computation.247 | convolution fusion | flops 583541248 | bytes 35946496 | tf_op jit(solution)/shard_map/bnhqk,bnkhe->bnqhe/dot_general | solution.py:191
  843.9 26.2 %collective-permute-done.49 = f32[2,2,2,336,128]{4,3,2,1,0:T(8,128)} collective-permute-done((f32[2,2,2,336,128]{4,3,2,1,0:T(8,128)}, f32[2,2,2,336,128]{4,3,2,1,0:T(8,128)}, u32[]{:S(2)}, u32[]{:S(2)}) %collective-permute-start.49) | collective-permute-done | bytes 1376288 | tf_op jit(solution)/shard_map/ppermute | solution.py:327
  901.1 17.2 %collective-permute-done.51 = f32[2,2,336,128]{3,2,1,0:T(8,128)S(1)} collective-permute-done((f32[2,2,336,128]{3,2,1,0:T(8,128)S(1)}, f32[2,2,336,128]{3,2,1,0:T(8,128)S(1)}, u32[]{:S(2)}, u32[]{:S(2)}) %collective-permute-start.51) | collective-permute-done | bytes 688160 | tf_op jit(solution)/shard_map/ppermute | solution.py:327
  942.7 11.0 shard_map.315
  978.9 16.3 %collective-permute-done.58 = f32[2,2,2,32,256]{4,2,1,0,3:T(2,128)} collective-permute-done((f32[2,2,2,32,256]{4,2,1,0,3:T(2,128)}, f32[2,2,2,32,256]{4,2,1,0,3:T(2,128)}, u32[]{:S(2)}, u32[]{:S(2)}) %collective-permute-start.58) | collective-permute-done | bytes 262176 | tf_op jit(solution)/shard_map/ppermute | solution.py:327
  1011.1 18.8 %collective-permute-done.61 = f32[2,2,2,1,352,128]{5,4,2,1,0,3:T(8,128)S(1)} collective-permute-done((f32[2,2,2,1,352,128]{5,4,2,1,0,3:T(8,128)}, f32[2,2,2,1,352,128]{5,4,2,1,0,3:T(8,128)S(1)}, u32[]{:S(2)}, u32[]{:S(2)}) %collective-permute-start.61) | collective-permute-done | bytes 1441824 | tf_op jit(solution)/shard_map/ppermute | solution.py:327
  1030.0 23.8 %collective-permute-done.65 = f32[2,2,2,288,128]{4,3,2,1,0:T(8,128)S(1)} collective-permute-done((f32[2,2,2,288,128]{4,3,2,1,0:T(8,128)S(1)}, f32[2,2,2,288,128]{4,3,2,1,0:T(8,128)S(1)}, u32[]{:S(2)}, u32[]{:S(2)}) %collective-permute-start.65) | collective-permute-done | bytes 1179680 | tf_op jit(solution)/shard_map/ppermute | solution.py:327
  1061.5 30.4 %collective-permute-done.68 = f32[2,2,32,256]{3,2,0,1:T(8,128)S(1)} collective-permute-done((f32[2,2,32,256]{3,2,0,1:T(8,128)S(1)}, f32[2,2,32,256]{3,2,0,1:T(8,128)S(1)}, u32[]{:S(2)}, u32[]{:S(2)}) %collective-permute-start.68) | collective-permute-done | bytes 131104 | tf_op jit(solution)/shard_map/ppermute | solution.py:327
  1118.1 9.0 collective-permute-done.74
  1149.1 20.4 %collective-permute-done.82 = f32[32,256]{1,0:T(8,128)S(1)} collective-permute-done((f32[32,256]{1,0:T(8,128)S(1)}, f32[32,256]{1,0:T(8,128)S(1)}, u32[]{:S(2)}, u32[]{:S(2)}) %collective-permute-start.82) | collective-permute-done | bytes 32800 | tf_op jit(solution)/shard_map/ppermute | solution.py:327
  1175.5 10.9 collective-permute-done.81
  1186.5 60.9 %collective-permute-done.80 = f32[32,384]{1,0:T(8,128)S(1)} collective-permute-done((f32[32,384]{1,0:T(8,128)S(1)}, f32[32,384]{1,0:T(8,128)S(1)}, u32[]{:S(2)}, u32[]{:S(2)}) %collective-permute-start.80) | collective-permute-done | bytes 49184 | tf_op jit(solution)/shard_map/ppermute | solution.py:327
  1303.1 7.1 fusion.82
  1368.6 9.0 collective-permute-done.109
  1378.5 12.6 collective-permute-done.107
  1406.9 20.5 %collective-permute-done.114 = bf16[4,336,128]{2,1,0:T(8,128)(2,1)} collective-permute-done((bf16[4,336,128]{2,1,0:T(8,128)(2,1)}, bf16[4,336,128]{2,1,0:T(8,128)(2,1)}, u32[]{:S(2)}, u32[]{:S(2)}) %collective-permute-start.114) | collective-permute-done | bytes 344096 | tf_op jit(solution)/shard_map/ppermute | solution.py:327
  1480.0 11.7 fusion.53
  (991 shorter events, 709.0 us)
Async XLA Ops:
  7.2 159.8 %all-gather.5.cloned.1.call-start = ((), (), s32[]{:S(2)}) async-start(), calls=%async_computation.11 | async-start | bytes 11083776 | tf_op jit(solution)/shard_map/all_gather | solution.py:788
  10.9 242.7 %all-gather.7.cloned.1.call-start = ((), (), s32[]{:S(2)}) async-start(), calls=%async_computation.12 | async-start | bytes 17301504 | tf_op jit(solution)/shard_map/all_gather | solution.py:797
  38.5 90.1 %all-to-all-start.5 = ((bf16[32,32,1024]{2,1,0:T(8,128)(2,1)}), bf16[32,32,1024]{2,1,0:T(8,128)(2,1)S(1)}, u32[]{:S(2)}, u32[]{:S(2)}) async-start(bf16[32,32,1024]{2,1,0:T(8,128)(2,1)} %bitcast.846), calls=%async_computation.5 | async-start | bytes 4194304 | tf_op jit(solution)/shard_map/all_to_all | solution.py:300
  235.7 230.4 %collective-permute-start.26 = (bf16[1024,512]{0,1:T(8,128)(2,1)}, bf16[1024,512]{0,1:T(8,128)(2,1)}, u32[]{:S(2)}, u32[]{:S(2)}) collective-permute-start(bf16[1024,512]{0,1:T(8,128)(2,1)} %fusion.373), channel_id=1, source_target_pairs={{0,1},{1,0},{2,3},{3,2},{4,5},{5,4},{6,7},{7,6},{8,9},{9,8},{10,11... | collective-permute-start | bytes 3145736 | tf_op jit(solution)/shard_map/ppermute | solution.py:327
  242.2 227.4 %collective-permute-start.24 = (bf16[1024,512]{0,1:T(8,128)(2,1)}, bf16[1024,512]{0,1:T(8,128)(2,1)}, u32[]{:S(2)}, u32[]{:S(2)}) collective-permute-start(bf16[1024,512]{0,1:T(8,128)(2,1)} %fusion.270), channel_id=1, source_target_pairs={{0,1},{1,0},{2,3},{3,2},{4,5},{5,4},{6,7},{7,6},{8,9},{9,8},{10,11... | collective-permute-start | bytes 3145736 | tf_op jit(solution)/shard_map/ppermute | solution.py:327
  306.3 202.6 %all-to-all-start.6 = ((bf16[32,80,992]{2,1,0:T(8,128)(2,1)}), bf16[32,80,992]{2,1,0:T(8,128)(2,1)}, u32[]{:S(2)}, u32[]{:S(2)}) async-start(bf16[32,80,992]{2,1,0:T(8,128)(2,1)} %bitcast.776), calls=%async_computation.6 | async-start | bytes 10485760 | tf_op jit(solution)/shard_map/all_to_all | solution.py:300
  316.4 31.3 %collective-permute-start.13 = (bf16[1,80,384]{2,1,0:T(8,128)(2,1)S(1)}, bf16[1,80,384]{2,1,0:T(8,128)(2,1)S(1)}, u32[]{:S(2)}, u32[]{:S(2)}) collective-permute-start(bf16[1,80,384]{2,1,0:T(8,128)(2,1)S(1)} %get-tuple-element.610), channel_id=1, source_target_pairs={{0,2},{2,0},{1,3},{3,1},{4,6},{6,4},{5,7},{7,5},{8,10},{10,8},{9,1... | collective-permute-start | bytes 184328 | tf_op jit(solution)/shard_map/ppermute | solution.py:327
  317.9 111.5 %collective-permute-start.12 = (bf16[1,80,384]{2,1,0:T(8,128)(2,1)S(1)}, bf16[1,80,384]{2,1,0:T(8,128)(2,1)S(1)}, u32[]{:S(2)}, u32[]{:S(2)}) collective-permute-start(bf16[1,80,384]{2,1,0:T(8,128)(2,1)S(1)} %get-tuple-element.611), channel_id=1, source_target_pairs={{0,16},{4,20},{8,24},{12,28},{16,0},{20,4},{24,8},{28,12},{1,17},{... | collective-permute-start | bytes 184328 | tf_op jit(solution)/shard_map/ppermute | solution.py:327
  431.1 50.3 %collective-permute-start.25 = (bf16[512,2048]{1,0:T(8,128)(2,1)S(1)}, bf16[512,2048]{1,0:T(8,128)(2,1)S(1)}, u32[]{:S(2)}, u32[]{:S(2)}) collective-permute-start(bf16[512,2048]{1,0:T(8,128)(2,1)S(1)} %get-tuple-element.568), channel_id=1, source_target_pairs={{0,1},{1,0},{2,3},{3,2},{4,5},{5,4},{6,7},{7,6},{8,9},{9,8},{10,11... | collective-permute-start | bytes 6291464 | tf_op jit(solution)/shard_map/ppermute | solution.py:327
  441.1 33.2 %collective-permute-start.27 = (bf16[1024,512]{0,1:T(8,128)(2,1)S(1)}, bf16[1024,512]{0,1:T(8,128)(2,1)S(1)}, u32[]{:S(2)}, u32[]{:S(2)}) collective-permute-start(bf16[1024,512]{0,1:T(8,128)(2,1)S(1)} %get-tuple-element.577), channel_id=1, source_target_pairs={{0,1},{1,0},{2,3},{3,2},{4,5},{5,4},{6,7},{7,6},{8,9},{9,8},{10,11... | collective-permute-start | bytes 3145736 | tf_op jit(solution)/shard_map/ppermute | solution.py:327
  723.3 72.2 %collective-permute-start.46 = (f32[2,2,2,2,336,128]{5,4,3,2,1,0:T(8,128)}, f32[2,2,2,2,336,128]{5,4,3,2,1,0:T(8,128)}, u32[]{:S(2)}, u32[]{:S(2)}) collective-permute-start(f32[2,2,2,2,336,128]{5,4,3,2,1,0:T(8,128)} %slice_bitcast_fusion.1), channel_id=1, source_target_pairs={{0,8},{4,12},{8,0},{12,4},{16,24},{20,28},{24,16},{28,20},{1,9},{5... | collective-permute-start | bytes 8257544 | tf_op jit(solution)/shard_map/ppermute | solution.py:327
  727.0 71.6 %collective-permute-start.45 = (f32[2,2,2,2,336,128]{5,4,3,2,1,0:T(8,128)}, f32[2,2,2,2,336,128]{5,4,3,2,1,0:T(8,128)}, u32[]{:S(2)}, u32[]{:S(2)}) collective-permute-start(f32[2,2,2,2,336,128]{5,4,3,2,1,0:T(8,128)} %slice_bitcast_fusion.2), channel_id=1, source_target_pairs={{0,4},{4,0},{8,12},{12,8},{16,20},{20,16},{24,28},{28,24},{1,5},{5... | collective-permute-start | bytes 8257544 | tf_op jit(solution)/shard_map/ppermute | solution.py:327
  729.3 73.2 %collective-permute-start.44 = (f32[2,2,2,2,352,128]{5,4,3,2,1,0:T(8,128)}, f32[2,2,2,2,352,128]{5,4,3,2,1,0:T(8,128)}, u32[]{:S(2)}, u32[]{:S(2)}) collective-permute-start(f32[2,2,2,2,352,128]{5,4,3,2,1,0:T(8,128)} %slice_bitcast_fusion), channel_id=1, source_target_pairs={{0,2},{2,0},{1,3},{3,1},{4,6},{6,4},{5,7},{7,5},{8,10},{10,8},{9,1... | collective-permute-start | bytes 8650760 | tf_op jit(solution)/shard_map/ppermute | solution.py:327
  759.2 55.8 %collective-permute-start.60 = (bf16[512,1024]{1,0:T(8,128)(2,1)}, bf16[512,1024]{1,0:T(8,128)(2,1)}, u32[]{:S(2)}, u32[]{:S(2)}) collective-permute-start(bf16[512,1024]{1,0:T(8,128)(2,1)} %get-tuple-element.571), channel_id=1, source_target_pairs={{0,1},{1,0},{2,3},{3,2},{4,5},{5,4},{6,7},{7,6},{8,9},{9,8},{10,11... | collective-permute-start | bytes 3145736 | tf_op jit(solution)/shard_map/ppermute | solution.py:327
  806.8 63.3 %collective-permute-start.49 = (f32[2,2,2,336,128]{4,3,2,1,0:T(8,128)}, f32[2,2,2,336,128]{4,3,2,1,0:T(8,128)}, u32[]{:S(2)}, u32[]{:S(2)}) collective-permute-start(f32[2,2,2,336,128]{4,3,2,1,0:T(8,128)} %slice_bitcast_fusion.10), channel_id=1, source_target_pairs={{0,16},{4,20},{8,24},{12,28},{16,0},{20,4},{24,8},{28,12},{1,17},{... | collective-permute-start | bytes 4128776 | tf_op jit(solution)/shard_map/ppermute | solution.py:327
  810.0 63.2 %collective-permute-start.48 = (f32[2,2,2,336,128]{4,3,2,1,0:T(8,128)}, f32[2,2,2,336,128]{4,3,2,1,0:T(8,128)}, u32[]{:S(2)}, u32[]{:S(2)}) collective-permute-start(f32[2,2,2,336,128]{4,3,2,1,0:T(8,128)} %slice_bitcast_fusion.11), channel_id=1, source_target_pairs={{0,8},{4,12},{8,0},{12,4},{16,24},{20,28},{24,16},{28,20},{1,9},{5... | collective-permute-start | bytes 4128776 | tf_op jit(solution)/shard_map/ppermute | solution.py:327
  811.3 65.0 %collective-permute-start.47 = (f32[2,2,2,352,128]{4,3,2,1,0:T(8,128)}, f32[2,2,2,352,128]{4,3,2,1,0:T(8,128)}, u32[]{:S(2)}, u32[]{:S(2)}) collective-permute-start(f32[2,2,2,352,128]{4,3,2,1,0:T(8,128)} %slice_bitcast_fusion.5), channel_id=1, source_target_pairs={{0,4},{4,0},{8,12},{12,8},{16,20},{20,16},{24,28},{28,24},{1,5},{5... | collective-permute-start | bytes 4325384 | tf_op jit(solution)/shard_map/ppermute | solution.py:327
  886.5 31.9 %collective-permute-start.51 = (f32[2,2,336,128]{3,2,1,0:T(8,128)S(1)}, f32[2,2,336,128]{3,2,1,0:T(8,128)S(1)}, u32[]{:S(2)}, u32[]{:S(2)}) collective-permute-start(f32[2,2,336,128]{3,2,1,0:T(8,128)S(1)} %slice_bitcast_fusion.20), channel_id=1, source_target_pairs={{0,16},{4,20},{8,24},{12,28},{16,0},{20,4},{24,8},{28,12},{1,17},{... | collective-permute-start | bytes 2064392 | tf_op jit(solution)/shard_map/ppermute | solution.py:327
  886.6 32.7 %collective-permute-start.50 = (f32[2,2,352,128]{3,2,1,0:T(8,128)S(1)}, f32[2,2,352,128]{3,2,1,0:T(8,128)S(1)}, u32[]{:S(2)}, u32[]{:S(2)}) collective-permute-start(f32[2,2,352,128]{3,2,1,0:T(8,128)S(1)} %slice_bitcast_fusion.14), channel_id=1, source_target_pairs={{0,8},{4,12},{8,0},{12,4},{16,24},{20,28},{24,16},{28,20},{1,9},{5... | collective-permute-start | bytes 2162696 | tf_op jit(solution)/shard_map/ppermute | solution.py:327
  890.4 49.2 %collective-permute-start.59 = (bf16[512,1024]{1,0:T(8,128)(2,1)}, bf16[512,1024]{1,0:T(8,128)(2,1)}, u32[]{:S(2)}, u32[]{:S(2)}) collective-permute-start(bf16[512,1024]{1,0:T(8,128)(2,1)} %get-tuple-element.573), channel_id=1, source_target_pairs={{0,1},{1,0},{2,3},{3,2},{4,5},{5,4},{6,7},{7,6},{8,9},{9,8},{10,11... | collective-permute-start | bytes 3145736 | tf_op jit(solution)/shard_map/ppermute | solution.py:327
  920.2 42.3 %collective-permute-start.55 = (f32[2,336,128]{2,1,0:T(8,128)}, f32[2,336,128]{2,1,0:T(8,128)S(1)}, u32[]{:S(2)}, u32[]{:S(2)}) collective-permute-start(f32[2,336,128]{2,1,0:T(8,128)} %slice_bitcast_fusion.30), channel_id=1, source_target_pairs={{0,4},{4,0},{8,12},{12,8},{16,20},{20,16},{24,28},{28,24},{1,5},{5... | collective-permute-start | bytes 1032200 | tf_op jit(solution)/shard_map/ppermute | solution.py:327
  922.3 41.5 %collective-permute-start.54 = (f32[2,336,128]{2,1,0:T(8,128)}, f32[2,336,128]{2,1,0:T(8,128)S(1)}, u32[]{:S(2)}, u32[]{:S(2)}) collective-permute-start(f32[2,336,128]{2,1,0:T(8,128)} %slice_bitcast_fusion.31), channel_id=1, source_target_pairs={{0,2},{2,0},{1,3},{3,1},{4,6},{6,4},{5,7},{7,5},{8,10},{10,8},{9,1... | collective-permute-start | bytes 1032200 | tf_op jit(solution)/shard_map/ppermute | solution.py:327
  923.6 41.0 %collective-permute-start.53 = (f32[2,352,128]{2,1,0:T(8,128)S(1)}, f32[2,352,128]{2,1,0:T(8,128)S(1)}, u32[]{:S(2)}, u32[]{:S(2)}) collective-permute-start(f32[2,352,128]{2,1,0:T(8,128)S(1)} %slice_bitcast_fusion.25), channel_id=1, source_target_pairs={{0,16},{4,20},{8,24},{12,28},{16,0},{20,4},{24,8},{28,12},{1,17},{... | collective-permute-start | bytes 1081352 | tf_op jit(solution)/shard_map/ppermute | solution.py:327
  938.7 60.5 %collective-permute-start.64 = (f32[2,2,2,2,288,128]{5,4,3,2,1,0:T(8,128)}, f32[2,2,2,2,288,128]{5,4,3,2,1,0:T(8,128)}, u32[]{:S(2)}, u32[]{:S(2)}) collective-permute-start(f32[2,2,2,2,288,128]{5,4,3,2,1,0:T(8,128)} %dynamic-slice_bitcast_fusion), channel_id=1, source_target_pairs={{0,1},{1,0},{2,3},{3,2},{4,5},{5,4},{6,7},{7,6},{8,9},{9,8},{10,11... | collective-permute-start | bytes 7077896 | tf_op jit(solution)/shard_map/ppermute | solution.py:327
  956.4 51.3 %collective-permute-start.63 = (f32[2,2,2,1,336,128]{5,4,2,1,0,3:T(8,128)}, f32[2,2,2,1,336,128]{5,4,2,1,0,3:T(8,128)}, u32[]{:S(2)}, u32[]{:S(2)}) collective-permute-start(f32[2,2,2,1,336,128]{5,4,2,1,0,3:T(8,128)} %slice_bitcast_fusion.8), channel_id=1, source_target_pairs={{0,8},{4,12},{8,0},{12,4},{16,24},{20,28},{24,16},{28,20},{1,9},{5... | collective-permute-start | bytes 4128776 | tf_op jit(solution)/shard_map/ppermute | solution.py:327
  962.5 47.0 %collective-permute-start.62 = (f32[2,2,2,1,336,128]{5,4,2,1,0,3:T(8,128)}, f32[2,2,2,1,336,128]{5,4,2,1,0,3:T(8,128)}, u32[]{:S(2)}, u32[]{:S(2)}) collective-permute-start(f32[2,2,2,1,336,128]{5,4,2,1,0,3:T(8,128)} %slice_bitcast_fusion.9), channel_id=1, source_target_pairs={{0,4},{4,0},{8,12},{12,8},{16,20},{20,16},{24,28},{28,24},{1,5},{5... | collective-permute-start | bytes 4128776 | tf_op jit(solution)/shard_map/ppermute | solution.py:327
  995.2 34.7 %collective-permute-start.61 = (f32[2,2,2,1,352,128]{5,4,2,1,0,3:T(8,128)}, f32[2,2,2,1,352,128]{5,4,2,1,0,3:T(8,128)S(1)}, u32[]{:S(2)}, u32[]{:S(2)}) collective-permute-start(f32[2,2,2,1,352,128]{5,4,2,1,0,3:T(8,128)} %slice_bitcast_fusion.4), channel_id=1, source_target_pairs={{0,2},{2,0},{1,3},{3,1},{4,6},{6,4},{5,7},{7,5},{8,10},{10,8},{9,1... | collective-permute-start | bytes 4325384 | tf_op jit(solution)/shard_map/ppermute | solution.py:327
  1002.1 51.7 %collective-permute-start.65 = (f32[2,2,2,288,128]{4,3,2,1,0:T(8,128)S(1)}, f32[2,2,2,288,128]{4,3,2,1,0:T(8,128)S(1)}, u32[]{:S(2)}, u32[]{:S(2)}) collective-permute-start(f32[2,2,2,288,128]{4,3,2,1,0:T(8,128)S(1)} %dynamic-slice_bitcast_fusion.1), channel_id=1, source_target_pairs={{0,2},{2,0},{1,3},{3,1},{4,6},{6,4},{5,7},{7,5},{8,10},{10,8},{9,1... | collective-permute-start | bytes 3538952 | tf_op jit(solution)/shard_map/ppermute | solution.py:327
  1054.0 49.8 %collective-permute-start.72 = (f32[2,2,288,128]{3,2,1,0:T(8,128)S(1)}, f32[2,2,288,128]{3,2,1,0:T(8,128)S(1)}, u32[]{:S(2)}, u32[]{:S(2)}) collective-permute-start(f32[2,2,288,128]{3,2,1,0:T(8,128)S(1)} %dynamic-slice_bitcast_fusion.2), channel_id=1, source_target_pairs={{0,4},{4,0},{8,12},{12,8},{16,20},{20,16},{24,28},{28,24},{1,5},{5... | collective-permute-start | bytes 1769480 | tf_op jit(solution)/shard_map/ppermute | solution.py:327
  1054.7 49.2 %collective-permute-start.71 = (f32[2,2,1,336,128]{4,3,1,0,2:T(8,128)S(1)}, f32[2,2,1,336,128]{4,3,1,0,2:T(8,128)S(1)}, u32[]{:S(2)}, u32[]{:S(2)}) collective-permute-start(f32[2,2,1,336,128]{4,3,1,0,2:T(8,128)S(1)} %slice_bitcast_fusion.17), channel_id=1, source_target_pairs={{0,16},{4,20},{8,24},{12,28},{16,0},{20,4},{24,8},{28,12},{1,17},{... | collective-permute-start | bytes 2064392 | tf_op jit(solution)/shard_map/ppermute | solution.py:327
  1056.7 47.4 %collective-permute-start.70 = (f32[2,2,1,336,128]{4,3,1,0,2:T(8,128)S(1)}, f32[2,2,1,336,128]{4,3,1,0,2:T(8,128)S(1)}, u32[]{:S(2)}, u32[]{:S(2)}) collective-permute-start(f32[2,2,1,336,128]{4,3,1,0,2:T(8,128)S(1)} %slice_bitcast_fusion.18), channel_id=1, source_target_pairs={{0,8},{4,12},{8,0},{12,4},{16,24},{20,28},{24,16},{28,20},{1,9},{5... | collective-permute-start | bytes 2064392 | tf_op jit(solution)/shard_map/ppermute | solution.py:327
  1057.3 46.8 %collective-permute-start.69 = (f32[2,2,1,352,128]{4,3,1,0,2:T(8,128)S(1)}, f32[2,2,1,352,128]{4,3,1,0,2:T(8,128)S(1)}, u32[]{:S(2)}, u32[]{:S(2)}) collective-permute-start(f32[2,2,1,352,128]{4,3,1,0,2:T(8,128)S(1)} %slice_bitcast_fusion.13), channel_id=1, source_target_pairs={{0,4},{4,0},{8,12},{12,8},{16,20},{20,16},{24,28},{28,24},{1,5},{5... | collective-permute-start | bytes 2162696 | tf_op jit(solution)/shard_map/ppermute | solution.py:327
  1059.0 32.9 %collective-permute-start.68 = (f32[2,2,32,256]{3,2,0,1:T(8,128)S(1)}, f32[2,2,32,256]{3,2,0,1:T(8,128)S(1)}, u32[]{:S(2)}, u32[]{:S(2)}) collective-permute-start(f32[2,2,32,256]{3,2,0,1:T(8,128)S(1)} %bitcast.882), channel_id=1, source_target_pairs={{0,16},{4,20},{8,24},{12,28},{16,0},{20,4},{24,8},{28,12},{1,17},{... | collective-permute-start | bytes 393224 | tf_op jit(solution)/shard_map/ppermute | solution.py:327
  1105.1 32.5 %collective-permute-start.79 = (f32[2,288,128]{2,1,0:T(8,128)}, f32[2,288,128]{2,1,0:T(8,128)}, u32[]{:S(2)}, u32[]{:S(2)}) collective-permute-start(f32[2,288,128]{2,1,0:T(8,128)} %dynamic-slice_bitcast_fusion.4), channel_id=1, source_target_pairs={{0,8},{4,12},{8,0},{12,4},{16,24},{20,28},{24,16},{28,20},{1,9},{5... | collective-permute-start | bytes 884744 | tf_op jit(solution)/shard_map/ppermute | solution.py:327
  1106.1 32.6 %collective-permute-start.78 = (f32[2,1,336,128]{3,2,0,1:T(8,128)}, f32[2,1,336,128]{3,2,0,1:T(8,128)}, u32[]{:S(2)}, u32[]{:S(2)}) collective-permute-start(f32[2,1,336,128]{3,2,0,1:T(8,128)} %slice_bitcast_fusion.28), channel_id=1, source_target_pairs={{0,2},{2,0},{1,3},{3,1},{4,6},{6,4},{5,7},{7,5},{8,10},{10,8},{9,1... | collective-permute-start | bytes 1032200 | tf_op jit(solution)/shard_map/ppermute | solution.py:327
  1107.7 32.0 %collective-permute-start.77 = (f32[2,1,336,128]{3,2,0,1:T(8,128)}, f32[2,1,336,128]{3,2,0,1:T(8,128)}, u32[]{:S(2)}, u32[]{:S(2)}) collective-permute-start(f32[2,1,336,128]{3,2,0,1:T(8,128)} %slice_bitcast_fusion.29), channel_id=1, source_target_pairs={{0,16},{4,20},{8,24},{12,28},{16,0},{20,4},{24,8},{28,12},{1,17},{... | collective-permute-start | bytes 1032200 | tf_op jit(solution)/shard_map/ppermute | solution.py:327
  1133.2 169.9 %all-to-all-start.9 = ((f32[32,32,1024]{2,1,0:T(8,128)}), f32[32,32,1024]{2,1,0:T(8,128)}, u32[]{:S(2)}, u32[]{:S(2)}) async-start(f32[32,32,1024]{2,1,0:T(8,128)} %bitcast.818), calls=%async_computation.9 | async-start | bytes 8388608 | tf_op jit(solution)/shard_map/all_to_all | solution.py:300
  1141.9 105.5 %collective-permute-start.86 = (f32[288,128]{1,0:T(8,128)S(1)}, f32[288,128]{1,0:T(8,128)S(1)}, u32[]{:S(2)}, u32[]{:S(2)}) collective-permute-start(f32[288,128]{1,0:T(8,128)S(1)} %dynamic-slice_bitcast_fusion.6), channel_id=1, source_target_pairs={{0,16},{4,20},{8,24},{12,28},{16,0},{20,4},{24,8},{28,12},{1,17},{... | collective-permute-start | bytes 442376 | tf_op jit(solution)/shard_map/ppermute | solution.py:327
  1144.8 102.6 %collective-permute-start.85 = (f32[1,336,128]{2,1,0:T(8,128)S(1)}, f32[1,336,128]{2,1,0:T(8,128)S(1)}, u32[]{:S(2)}, u32[]{:S(2)}) collective-permute-start(f32[1,336,128]{2,1,0:T(8,128)S(1)} %slice_bitcast_fusion.42), channel_id=1, source_target_pairs={{0,4},{4,0},{8,12},{12,8},{16,20},{20,16},{24,28},{28,24},{1,5},{5... | collective-permute-start | bytes 516104 | tf_op jit(solution)/shard_map/ppermute | solution.py:327
  1146.4 101.8 %collective-permute-start.84 = (f32[1,336,128]{2,1,0:T(8,128)S(1)}, f32[1,336,128]{2,1,0:T(8,128)S(1)}, u32[]{:S(2)}, u32[]{:S(2)}) collective-permute-start(f32[1,336,128]{2,1,0:T(8,128)S(1)} %slice_bitcast_fusion.43), channel_id=1, source_target_pairs={{0,2},{2,0},{1,3},{3,1},{4,6},{6,4},{5,7},{7,5},{8,10},{10,8},{9,1... | collective-permute-start | bytes 516104 | tf_op jit(solution)/shard_map/ppermute | solution.py:327
  1147.9 100.9 %collective-permute-start.83 = (f32[1,352,128]{2,1,0:T(8,128)S(1)}, f32[1,352,128]{2,1,0:T(8,128)S(1)}, u32[]{:S(2)}, u32[]{:S(2)}) collective-permute-start(f32[1,352,128]{2,1,0:T(8,128)S(1)} %slice_bitcast_fusion.37), channel_id=1, source_target_pairs={{0,16},{4,20},{8,24},{12,28},{16,0},{20,4},{24,8},{28,12},{1,17},{... | collective-permute-start | bytes 540680 | tf_op jit(solution)/shard_map/ppermute | solution.py:327
  1186.5 60.9 %collective-permute-start.80 = (f32[32,384]{1,0:T(8,128)S(1)}, f32[32,384]{1,0:T(8,128)S(1)}, u32[]{:S(2)}, u32[]{:S(2)}) collective-permute-start(f32[32,384]{1,0:T(8,128)S(1)} %dynamic-slice_bitcast_fusion.11), channel_id=1, source_target_pairs={{0,16},{4,20},{8,24},{12,28},{16,0},{20,4},{24,8},{28,12},{1,17},{... | collective-permute-start | bytes 147464 | tf_op jit(solution)/shard_map/ppermute | solution.py:327
  1398.3 35.6 %collective-permute-start.118 = (bf16[4,336,256]{2,1,0:T(8,128)(2,1)S(1)}, bf16[4,336,256]{2,1,0:T(8,128)(2,1)}, u32[]{:S(2)}, u32[]{:S(2)}) collective-permute-start(bf16[4,336,256]{2,1,0:T(8,128)(2,1)S(1)} %pad_maximum_fusion.26), channel_id=1, source_target_pairs={{0,16},{4,20},{8,24},{12,28},{16,0},{20,4},{24,8},{28,12},{1,17},{... | collective-permute-start | bytes 2064392 | tf_op jit(solution)/shard_map/ppermute | solution.py:327
  1400.9 35.4 %collective-permute-start.117 = (bf16[4,336,256]{2,1,0:T(8,128)(2,1)S(1)}, bf16[4,336,256]{2,1,0:T(8,128)(2,1)}, u32[]{:S(2)}, u32[]{:S(2)}) collective-permute-start(bf16[4,336,256]{2,1,0:T(8,128)(2,1)S(1)} %pad_maximum_fusion.25), channel_id=1, source_target_pairs={{0,8},{4,12},{8,0},{12,4},{16,24},{20,28},{24,16},{28,20},{1,9},{5... | collective-permute-start | bytes 2064392 | tf_op jit(solution)/shard_map/ppermute | solution.py:327
  1400.9 37.6 %collective-permute-start.116 = (bf16[4,352,256]{2,1,0:T(8,128)(2,1)S(1)}, bf16[4,352,256]{2,1,0:T(8,128)(2,1)}, u32[]{:S(2)}, u32[]{:S(2)}) collective-permute-start(bf16[4,352,256]{2,1,0:T(8,128)(2,1)S(1)} %pad_maximum_fusion.23), channel_id=1, source_target_pairs={{0,4},{4,0},{8,12},{12,8},{16,20},{20,16},{24,28},{28,24},{1,5},{5... | collective-permute-start | bytes 2162696 | tf_op jit(solution)/shard_map/ppermute | solution.py:327
  1439.8 38.4 %collective-permute-start.119 = (bf16[8,352,256]{2,1,0:T(8,128)(2,1)S(1)}, bf16[8,352,256]{2,1,0:T(8,128)(2,1)}, u32[]{:S(2)}, u32[]{:S(2)}) collective-permute-start(bf16[8,352,256]{2,1,0:T(8,128)(2,1)S(1)} %pad_maximum_fusion.15), channel_id=1, source_target_pairs={{0,2},{2,0},{1,3},{3,1},{4,6},{6,4},{5,7},{7,5},{8,10},{10,8},{9,1... | collective-permute-start | bytes 4325384 | tf_op jit(solution)/shard_map/ppermute | solution.py:327
  1440.9 32.9 %collective-permute-start.120 = (bf16[8,336,256]{2,1,0:T(8,128)(2,1)}, bf16[8,336,256]{2,1,0:T(8,128)(2,1)}, u32[]{:S(2)}, u32[]{:S(2)}) collective-permute-start(bf16[8,336,256]{2,1,0:T(8,128)(2,1)} %pad_maximum_fusion.16), channel_id=1, source_target_pairs={{0,4},{4,0},{8,12},{12,8},{16,20},{20,16},{24,28},{28,24},{1,5},{5... | collective-permute-start | bytes 4128776 | tf_op jit(solution)/shard_map/ppermute | solution.py:327
  1441.4 34.6 %collective-permute-start.121 = (bf16[8,336,256]{2,1,0:T(8,128)(2,1)}, bf16[8,336,256]{2,1,0:T(8,128)(2,1)}, u32[]{:S(2)}, u32[]{:S(2)}) collective-permute-start(bf16[8,336,256]{2,1,0:T(8,128)(2,1)} %pad_maximum_fusion.17), channel_id=1, source_target_pairs={{0,8},{4,12},{8,0},{12,4},{16,24},{20,28},{24,16},{28,20},{1,9},{5... | collective-permute-start | bytes 4128776 | tf_op jit(solution)/shard_map/ppermute | solution.py:327
  (235 other events, 4558.0 us)
Sparse Core Ops, SparseCore 0:
  11.5 124.2 all-gather.4
  139.2 114.4 all-gather.6

commit v4 on v3

--- a/solution.py
+++ b/solution.py
@@ -198,15 +198,6 @@
     grad_key = grad_key.reshape(count, length, model_width).astype(jnp.bfloat16)
     grad_query, parts = tied(grad_query, parts)
     parts = reduce_step(parts, wide_count, 2)
-    grad_hidden = (
-        grad_attn
-        + project_back(grad_query, w_query)
-        + project_back(grad_key, w_key)
-        + project_back(grad_value, w_value)
-    )
-    grad_hidden, parts = tied(grad_hidden, parts)
-    for step in range(3, len(routes(wide_count)[0])):
-        parts = reduce_step(parts, wide_count, step)
     operands = (
         shared[2],
         shared[3],
@@ -214,13 +205,24 @@
         swap_pick(grad_value[0], attn_low[0], 0),
     )
     if D // wide_count == lanes:
-        grad_mats_attn = attn_weight_grads(*operands, wide_count)
+        attn_parts = attn_weight_grads(*operands, wide_count)
     else:
         blocks = jnp.stack([jnp.dot(*operands[::2], preferred_element_type=jnp.float32),
                             jnp.dot(*operands[1::2], preferred_element_type=jnp.float32)])
         blocks = blocks.reshape(2, 1, D, wide_count, -1).transpose(3, 0, 1, 2, 4)
-        grad_mats_attn = in_routes(blocks, wide_count)
-    matrices = (grad_mats_attn, parts)
+        attn_parts = in_routes(blocks, wide_count)
+    last_query, attn_parts = tied(grad_query, attn_parts)
+    attn_parts = reduce_step(attn_parts, wide_count, 0)
+    grad_hidden = (
+        grad_attn
+        + project_back(last_query, w_query)
+        + project_back(grad_key, w_key)
+        + project_back(grad_value, w_value)
+    )
+    grad_hidden, parts = tied(grad_hidden, parts)
+    for step in range(3, len(routes(wide_count)[0])):
+        parts = reduce_step(parts, wide_count, step)
+    matrices = (attn_parts, parts)
     vector_grads = jnp.stack(
         [
             grad_gain_one,
@@ -313,7 +315,8 @@
 def routes(wide_count, with_pair=True):
     bits = wide_bits(wide_count)
     near, far, across = bits[:1], bits[1:], [("pair", 1)] if with_pair else []
-    return [across + near + far, near + far + across, far + across + near]
+    last = far[1:]
+    return [across + near + far, near + far[:1] + across + last, far[:1] + across + near + last]
 
 
 def my_bit(bit):
@@ -615,21 +618,6 @@
     return jnp.dot(
         hits.astype(rows.dtype), rows, precision=high, preferred_element_type=jnp.float32
     )
-
-
-def position_plan(devices, owned):
-    group = devices // 2
-    place = np.arange(SEQ)
-    owner = (V + place) // owned
-    target = 2 * (place % WINDOW % group) + place // WINDOW
-    rank = np.zeros(SEQ, np.int64)
-    seen = {}
-    for p in range(SEQ):
-        pair = (owner[p], target[p])
-        rank[p] = seen.get(pair, 0)
-        seen[pair] = rank[p] + 1
-    assert rank.max() < slots
-    return owner, target, rank
 
 
 def flat_blocks(size, devices):
@@ -809,8 +797,6 @@
     assert win_count == 1 and SEQ == 2 * WINDOW
     group = devices // 2
     per_place = WINDOW // group
-    half = device % 2
-    owner_of, target_of, rank_of = position_plan(devices, owned)
     tokens = token_ids.reshape(-1)
     token_owner = tokens // owned
     token_local = tokens - token_owner * owned
@@ -820,12 +806,7 @@
     is_first = ~jnp.any(same & earlier, axis=1)
     same_owner = token_owner[:, None] == token_owner[None, :]
     rank = jnp.sum((same_owner & earlier & is_first[None, :]).astype(jnp.int32), axis=1)
-    taken = np.zeros((devices, devices), np.int32)
-    np.add.at(taken, (target_of, owner_of), 1)
-    taken_here = lax.dynamic_index_in_dim(jnp.asarray(taken), device, 0, keepdims=False)
-    owners = jnp.arange(devices, dtype=jnp.int32)
-    offset = jnp.sum(jnp.where(token_owner[:, None] == owners[None, :], taken_here[None], 0), 1)
-    first_slot = jnp.where(is_first, offset + rank, 0)
+    first_slot = jnp.where(is_first, rank, 0)
     slot = jnp.sum(jnp.where(same & is_first[None, :], first_slot[None, :], 0), axis=1)
 
     def address(round_idx):
@@ -854,17 +835,15 @@
     counts_all = message[:, slots + 1]
     labels_all = message[:, labels_at : labels_at + MPW].reshape(-1)
     masked_total = jnp.sum(counts_all).astype(jnp.float32)
-    place = np.arange(SEQ)
-    cell_of = jnp.asarray(target_of * slots + rank_of, jnp.int32)
-    local_of = jnp.asarray(V + place - owner_of * owned + 1, jnp.int32)
-    mine = jnp.asarray(owner_of, jnp.int32) == device
-    cells = jnp.arange(devices * slots, dtype=jnp.int32)
-    place_hits = (cells[:, None] == cell_of[None, :]) & mine[None, :]
-    place_rows = jnp.sum(jnp.where(place_hits, local_of[None, :], 0), axis=1)
-    asked = message[:, :slots].reshape(-1) + place_rows - 1
-    held = (owner_of * slots + rank_of).reshape(2, per_place, group).transpose(0, 2, 1)
-    held = jnp.asarray(held.reshape(devices, per_place), jnp.int32)
-    held = lax.dynamic_index_in_dim(held, half * group + device // 2, 0, keepdims=False)
+    asked = message[:, :slots].reshape(-1) - 1
+    place_rows = V - device * owned + jnp.arange(SEQ, dtype=jnp.int32)
+    place_rows = select_rows(place_rows, table_low).astype(jnp.bfloat16)
+    place_rows = halve(place_rows.reshape(2, group, per_place, D), side_bit, 0)
+    place_parts = route_parts(place_rows, wide_count)
+    for step in range(len(routes(wide_count)[0])):
+        (place_parts,) = lockstep(route_step(place_parts, wide_count, step, False))
+    place_own = jnp.concatenate(place_parts, axis=-1)
+    place_all = gather_blocks(place_own, wide_count, 1, lanes).reshape(WINDOW, D)
 
     def fetch(asked_rows):
         rows = select_rows(asked_rows, table_low).astype(jnp.bfloat16)
@@ -880,8 +859,8 @@
     source_total = source_max + jnp.log(source_sum)
     source_cut = jnp.pad(source_own, ((0, 0), (0, devices * owned - V)))
     source_cut = source_cut.reshape(MPW, devices, owned).transpose(1, 0, 2)
-    fetched, source_cut, source_total = lax.optimization_barrier(
-        (fetched, source_cut, source_total)
+    fetched, source_cut, source_total, place_all = lax.optimization_barrier(
+        (fetched, source_cut, source_total, place_all)
     )
     if ffn_width == lanes:
         ffn_low = unpack_ffn(ffn_all, wide_count)
@@ -890,9 +869,6 @@
         ffn_low = ffn_low.transpose(2, 3, 1, 0, 4).reshape(2 * L, D, FF)
     source_here = swap_all(source_cut)
     token_rows = select_rows(now, fetched)
-    place_part = select_rows(held, fetched).astype(jnp.bfloat16)
-    place_all = gather_blocks(place_part, wide_count, 1, 128).reshape(group, per_place, D)
-    place_all = place_all.transpose(1, 0, 2).reshape(WINDOW, D).astype(jnp.float32)
 
     def more_rows(state):
         round_idx, rows = state
@@ -908,7 +884,7 @@
     bucket_ids = buckets.reshape(win_count, 1, WINDOW)
     same_bucket = bucket_ids[:, :, None, :, None] == bucket_ids[:, :, None, None, :]
     allowed = same_bucket & key_ok | jnp.eye(WINDOW, dtype=bool)
-    embedded = (token_rows + place_all).reshape(win_count, WINDOW, D)
+    embedded = (token_rows + place_all.astype(jnp.float32)).reshape(win_count, WINDOW, D)
     hidden, embed_pull = jax.vjp(layer_norm, embedded, vectors[0], vectors[1])
     params = (
         attn_low[0],
@@ -993,7 +969,7 @@
     flat_embed = grad_embed.reshape(WINDOW, D)
 
     ffn_parts, attn_parts = layer_mats[1], layer_mats[0]
-    flat_embed, ffn_parts = tied(flat_embed, ffn_parts)
+    (flat_embed,), ffn_parts, attn_parts = lockstep([flat_embed], ffn_parts, attn_parts)
     dec_block = jnp.zeros((devices * owned,), jnp.float32)
     dec_block = lax.dynamic_update_slice(dec_block, grad_dec, (device * owned,))[:V]
     vector_block = jnp.concatenate(
@@ -1011,15 +987,16 @@
     )
     other_part = scatter_flat(front, grad_head_w.reshape(-1, lanes), size, devices)
 
-    place_grad = flat_embed.reshape(per_place, group, D).transpose(1, 0, 2)
+    place_grad = flat_embed.reshape(group, per_place, D)
     ffn_grad = jnp.concatenate(ffn_parts, axis=1)
     sent = add_rows(now, flat_embed, devices * slots)
     arrived = swap_all(sent.reshape(devices, slots, D))
     place_parts = route_parts(place_grad.reshape(group, per_place, D), wide_count)
-    for step in range(len(routes(wide_count)[0])):
+    steps = len(routes(wide_count)[0])
+    for step in range(steps):
         place_parts, attn_parts, (other_part,) = lockstep(
             route_step(place_parts, wide_count, step, False),
-            reduce_step(attn_parts, wide_count, step),
+            reduce_step(attn_parts, wide_count, step + 1) if step + 1 < steps else attn_parts,
             [other_step(other_part, wide_count, step)],
         )
     attn_grad = jnp.concatenate(attn_parts, axis=1)
@@ -1028,8 +1005,8 @@
     place_grad = gather_relative(place_grad, wide_count, 1, lanes)
     place_grad = jnp.concatenate([place_grad, exchange(place_grad, side_bit)])
     turn = jnp.arange(devices, dtype=jnp.int32)[:, None]
-    place_ids = (turn // group ^ side) * WINDOW + (turn % group ^ here)
-    place_ids = place_ids + jnp.arange(per_place, dtype=jnp.int32)[None, :] * group
+    place_ids = (turn // group ^ side) * WINDOW + (turn % group ^ here) * per_place
+    place_ids = place_ids + jnp.arange(per_place, dtype=jnp.int32)[None, :]
     place_ids = (V - device * owned + place_ids).reshape(-1)
     table_grad = grad_words + add_rows(asked, arrived.reshape(-1, D), owned)
     table_grad = table_grad + add_rows(place_ids, place_grad.reshape(SEQ, D), owned)
@@ -1062,14 +1039,17 @@
     attn_parts = gather_start(attn_moment_new[0].astype(jnp.bfloat16), 0, tile)
     ffn_parts = gather_start(ffn_pair[0].astype(jnp.bfloat16), 0, tile)
     steps = len(routes(wide_count)[0])
-    for step in range(steps - 1):
+    for step in range(steps - 2):
         attn_parts, ffn_parts = lockstep(
             gather_step(attn_parts, wide_count, step, False),
             gather_step(ffn_parts, wide_count, step),
         )
-    attn_found = gather_end(attn_parts, wide_count, 0, False)
+    (attn_parts,) = lockstep(gather_step(attn_parts, wide_count, steps - 2, False))
+    attn_gram = gram_of(gather_end(attn_parts, wide_count, 0, False))
+    ffn_parts = gather_step(ffn_parts, wide_count, steps - 2)
+    attn_gram, ffn_parts = tied(attn_gram, ffn_parts)
     ffn_found = gather_end(gather_step(ffn_parts, wide_count, steps - 1), wide_count, 0)
-    attn_new = muon_cols(attn_mats, attn_moment_new, gram_of(attn_found), D)
+    attn_new = muon_cols(attn_mats, attn_moment_new, attn_gram, D)
     ffn_turn = newton_cols(ffn_pair, gram_of(ffn_found))[0]
     keep, give = ffn_turn[:, :ffn_width], ffn_turn[:, ffn_width:]
     got = exchange(give, side_bit)

time: 1550 us -> 1520 us (0.981)
  local copies, waits for them, and re-layouts: 152 us -> 128 us
  starting transfers between devices: 157 us -> 175 us
    all_to_all x7, waiting for transfers between devices: 73.4 us -> 24.5 us  [swap_all(): return lax.all_to_all(blocks, axes, 0, 0, tiled=True)]
    ppermute x123 -> x136, waiting for transfers between devices: 557 us -> 598 us  [exchange(): return lax.ppermute(values, axis, steps)]
    ppermute x123 -> x136, starting transfers between devices: 126 us -> 145 us  [exchange(): return lax.ppermute(values, axis, steps)]
  transfers between devices with their start and end apart: 132 -> 145, of which waited for: 72 -> 91; matrix products, arithmetic and copies ran while one was open for 32% -> 30% of each run, Pallas kernels for 3% -> 2%
where the time goes in v4:
time: 1520 us; the launch traced here: 1510 us
  waiting for transfers between devices  622 us (41%)
  matrix products  294 us (19%)
  starting transfers between devices  175 us (12%)
  other arithmetic  167 us (11%)
  local copies, waits for them, and re-layouts  128 us (8%)
  Pallas kernels  88.6 us (6%)
  between operations  30.3 us (2%)
    ppermute x136, waiting for transfers between devices, exchange(): return lax.ppermute(values, axis, steps)  598 us
    ppermute x136, starting transfers between devices, exchange(): return lax.ppermute(values, axis, steps)  145 us
    dot_general x6, matrix products, project(): jnp.einsum('bsd,df->bsf', inputs, weight, preferred_element_type=jnp.floa...  52.8 us
  transfers between devices with their start and end apart: 145, of which 91 were waited for; matrix products, arithmetic and copies ran while one was open for 30% of the time, Pallas kernels for 2%

profile of v4, /device:TPU:0, one launch (start us, length us, event | category | flops | bytes accessed | tf_op | source)
XLA Modules:
  0.0 1505.1 jit_solution(13444463741919265897)
XLA Ops:
  34.3 7.0 all-to-all-start.4
  46.9 10.1 reshape.1670
  57.0 7.7 copy.521
  77.2 8.9 collective-permute-done.3
  134.8 46.5 %collective-permute-done.14 = bf16[2,32,384]{2,1,0:T(8,128)(2,1)S(1)} collective-permute-done((bf16[2,32,384]{2,1,0:T(8,128)(2,1)S(1)}, bf16[2,32,384]{2,1,0:T(8,128)(2,1)S(1)}, u32[]{:S(2)}, u32[]{:S(2)}) %collective-permute-start.14) | collective-permute-done | bytes 49184 | tf_op jit(solution)/shard_map/ppermute | solution.py:330
  211.2 7.6 shard_map.266
  245.0 8.9 fusion.17
  253.9 9.4 exponential_reduce_fusion
  263.3 9.2 convolution_convert_fusion.1
  287.6 18.1 %shard_map.267 = (bf16[1024,4096]{1,0:T(8,128)(2,1)}, bf16[1024,4096]{1,0:T(8,128)(2,1)}) custom-call(bf16[32,2,1024,128]{3,2,1,0:T(8,128)(2,1)} %bitcast.908, bf16[32,2,1024,128]{3,2,1,0:T(8,128)(2,1)} %bitcast.909, bf16[32,2,1024,128]{3,2,1,0:T(8,128)(2,1)} %bitcast.910, bf16[32,2,1024,128]{3,2,1,0:T(8,128)(2,1)} %bitcast.911), custom_call_target="tpu_custom_call" | custom-call | tf_op jit(solution)/shard_map/pallas_call | solution.py:694
  305.7 27.8 %multiply_convert_fusion.1 = (bf16[512,4096]{1,0:T(8,128)(2,1)S(1)}, f32[512,4096]{1,0:T(8,128)}, f32[512,4096]{1,0:T(8,128)}) fusion(f32[4096]{0:T(1024)S(1)} %bitcast.1055, bf16[1024,4096]{1,0:T(8,128)(2,1)} %get-tuple-element.389, f32[512,1024]{1,0:T(8,128)} %copy-done.3, f32[1024]{0:T(1024)S(1)} %get-tuple-element.668, ...), kind=kOutput, calls=%fused_computation.50 | convolution fusion | flops 4436000768 | bytes 31485952 | tf_op jit(solution)/shard_map/bsd,df->bsf/dot_general | solution.py:60
  354.9 111.2 %collective-permute-done.27 = bf16[1,80,256]{2,1,0:T(8,128)(2,1)S(1)} collective-permute-done((bf16[1,80,256]{2,1,0:T(8,128)(2,1)S(1)}, bf16[1,80,256]{2,1,0:T(8,128)(2,1)S(1)}, u32[]{:S(2)}, u32[]{:S(2)}) %collective-permute-start.27) | collective-permute-done | bytes 40992 | tf_op jit(solution)/shard_map/ppermute | solution.py:330
  490.5 6.9 collective-permute-done.31
  521.7 8.9 fusion.321
  541.7 7.0 all-to-all-done.7
  552.7 6.9 all-to-all-done.8
  561.7 26.2 %shard_map.268 = (bf16[2560,992]{1,0:T(8,128)(2,1)}, f32[1,992]{1,0:T(1,128)}, f32[1,992]{1,0:T(1,128)}) custom-call(s32[3]{0:T(128)} %pad_add_fusion.facts, f32[2560,992]{1,0:T(8,128)} %get-tuple-element.696.logits_ref, bf16[32,80,992]{2,1,0:T(8,128)(2,1)} %all-to-all-done.6.source_ref, f32[2560,4]{1,0:T(8,128)} %copy.434.rows_ref), custom_call_target="tpu_custom_call" | custom-call | tf_op jit(solution)/shard_map/pallas_call | solution.py:590
  592.9 8.5 collective-permute-done.42
  608.1 7.2 fusion.330
  615.2 6.6 collective-permute-done.45
  622.0 7.5 collective-permute-done.44
  675.2 10.9 convert_reduce_fusion
  720.5 17.7 %shard_map.269 = (f32[2,2,2,2,2,352,128]{6,5,4,3,2,1,0:T(8,128)}, f32[2,2,2,2,2,336,128]{6,5,4,3,2,1,0:T(8,128)}, f32[2,2,2,2,2,336,128]{6,5,4,3,2,1,0:T(8,128)}) custom-call(s32[2]{0:T(128)} %pad_add_fusion.1.here, bf16[1024,1024]{1,0:T(8,128)(2,1)} %copy.441.up_rows, bf16[1024,1024]{1,0:T(8,128)(2,1)} %copy.442.down_rows, ...), custom_call_target="tpu_custom_call" | custom-call | tf_op jit(solution)/shard_map/pallas_call | solution.py:465
  738.3 10.3 fusion.114
  761.6 8.1 convert_reduce_fusion.3
  774.5 8.1 fusion.332
  782.7 30.3 %collective-permute-done.59 = f32[2,2,2,2,336,128]{5,4,3,2,1,0:T(8,128)} collective-permute-done((f32[2,2,2,2,336,128]{5,4,3,2,1,0:T(8,128)}, f32[2,2,2,2,336,128]{5,4,3,2,1,0:T(8,128)}, u32[]{:S(2)}, u32[]{:S(2)}) %collective-permute-start.59) | collective-permute-done | bytes 2752544 | tf_op jit(solution)/shard_map/ppermute | solution.py:330
  833.4 24.7 %fusion.162 = bf16[16,64,512]{2,1,0:T(8,128)(2,1)} fusion(bf16[512,16,64]{0,2,1:T(8,128)(2,1)} %bitcast.954, f32[16,512,512]{1,2,0:T(8,128)} %fusion.332, f32[16,512,512]{1,2,0:T(8,128)} %get-tuple-element.688, f32[16,512]{1,0:T(8,128)S(1)} %copy-done.95, pred[512,512]{0,1:T(8,128)(4,1)S(1)} %copy-done.57), kind=kOutput, calls=%fused_computation.246 | convolution fusion | flops 583541248 | bytes 35946496 | tf_op jit(solution)/shard_map/bnhqk,bnqhe->bnkhe/dot_general | solution.py:195
  867.3 24.5 %fusion.159 = bf16[16,64,512]{2,1,0:T(8,128)(2,1)} fusion(bf16[512,16,64]{0,2,1:T(8,128)(2,1)} %bitcast.1015, f32[16,512,512]{1,2,0:T(8,128)} %fusion.332, f32[16,512,512]{1,2,0:T(8,128)} %get-tuple-element.688, f32[16,512]{1,0:T(8,128)S(1)} %copy-done.95, pred[512,512]{0,1:T(8,128)(4,1)S(1)} %copy-done.57), kind=kOutput, calls=%fused_computation.245 | convolution fusion | flops 583541248 | bytes 35946496 | tf_op jit(solution)/shard_map/bnhqk,bnkhe->bnqhe/dot_general | solution.py:191
  911.9 10.5 collective-permute-done.67
  927.0 11.0 shard_map.270
  968.4 12.3 collective-permute-done.70
  989.8 13.3 collective-permute-done.68
  1018.0 14.4 collective-permute-done.76
  1044.3 24.4 %collective-permute-done.81 = f32[2,2,2,288,128]{4,3,2,1,0:T(8,128)S(1)} collective-permute-done((f32[2,2,2,288,128]{4,3,2,1,0:T(8,128)S(1)}, f32[2,2,2,288,128]{4,3,2,1,0:T(8,128)S(1)}, u32[]{:S(2)}, u32[]{:S(2)}) %collective-permute-start.81) | collective-permute-done | bytes 1179680 | tf_op jit(solution)/shard_map/ppermute | solution.py:330
  1074.1 7.0 collective-permute-done.84
  1110.9 16.6 %collective-permute-done.91 = f32[2,32,256]{2,1,0:T(8,128)S(1)} collective-permute-done((f32[2,32,256]{2,1,0:T(8,128)S(1)}, f32[2,32,256]{2,1,0:T(8,128)S(1)}, u32[]{:S(2)}, u32[]{:S(2)}) %collective-permute-start.91) | collective-permute-done | bytes 65568 | tf_op jit(solution)/shard_map/ppermute | solution.py:330
  1127.5 8.8 collective-permute-start.90
  1140.6 41.2 %collective-permute-done.89 = f32[2,32,384]{2,1,0:T(8,128)S(1)} collective-permute-done((f32[2,32,384]{2,1,0:T(8,128)S(1)}, f32[2,32,384]{2,1,0:T(8,128)S(1)}, u32[]{:S(2)}, u32[]{:S(2)}) %collective-permute-start.89) | collective-permute-done | bytes 98336 | tf_op jit(solution)/shard_map/ppermute | solution.py:330
  1184.3 24.9 %collective-permute-done.93 = f32[1,336,128]{2,1,0:T(8,128)S(1)} collective-permute-done((f32[1,336,128]{2,1,0:T(8,128)S(1)}, f32[1,336,128]{2,1,0:T(8,128)S(1)}, u32[]{:S(2)}, u32[]{:S(2)}) %collective-permute-start.93) | collective-permute-done | bytes 172064 | tf_op jit(solution)/shard_map/ppermute | solution.py:330
  1220.2 7.1 collective-permute-done.98
  1282.5 7.1 fusion.93
  1320.5 8.0 collective-permute-done.115
  1335.5 13.0 collective-permute-done.119
  1356.6 7.6 divide_subtract_fusion
  1369.1 10.5 collective-permute-done.120
  1417.9 7.3 bitcast_add_fusion.5
  1450.5 11.5 fusion.53
  (1025 shorter events, 725.3 us)
Async XLA Ops:
  7.2 200.4 %all-gather.5.cloned.1.call-start = ((), (), s32[]{:S(2)}) async-start(), calls=%async_computation.11 | async-start | bytes 11083776 | tf_op jit(solution)/shard_map/all_gather | solution.py:776
  10.9 276.7 %all-gather.7.cloned.1.call-start = ((), (), s32[]{:S(2)}) async-start(), calls=%async_computation.12 | async-start | bytes 17301504 | tf_op jit(solution)/shard_map/all_gather | solution.py:785
  20.9 49.7 %collective-permute-start = (bf16[16,32,1024]{2,1,0:T(8,128)(2,1)S(1)}, bf16[16,32,1024]{2,1,0:T(8,128)(2,1)}, u32[]{:S(2)}, u32[]{:S(2)}) collective-permute-start(bf16[16,32,1024]{2,1,0:T(8,128)(2,1)S(1)} %dynamic-slice_bitcast_fusion.2), channel_id=1, source_target_pairs={{0,1},{1,0},{2,3},{3,2},{4,5},{5,4},{6,7},{7,6},{8,9},{9,8},{10,11... | collective-permute-start | bytes 3145736 | tf_op jit(solution)/shard_map/ppermute | solution.py:330
  34.3 30.4 %all-to-all-start.4 = ((s32[32,1,128]{2,1,0:T(1,128)}), s32[32,1,128]{2,1,0:T(1,128)S(1)}, u32[]{:S(2)}, u32[]{:S(2)}) async-start(s32[32,1,128]{2,1,0:T(1,128)} %bitcast.15), calls=%async_computation.4 | async-start | bytes 32768 | tf_op jit(solution)/shard_map/all_to_all | solution.py:302
  118.4 83.8 %all-to-all-start.5 = ((bf16[32,32,1024]{2,1,0:T(8,128)(2,1)}), bf16[32,32,1024]{2,1,0:T(8,128)(2,1)S(1)}, u32[]{:S(2)}, u32[]{:S(2)}) async-start(bf16[32,32,1024]{2,1,0:T(8,128)(2,1)} %bitcast.17), calls=%async_computation.5 | async-start | bytes 4194304 | tf_op jit(solution)/shard_map/all_to_all | solution.py:302
  125.1 56.2 %collective-permute-start.14 = (bf16[2,32,384]{2,1,0:T(8,128)(2,1)S(1)}, bf16[2,32,384]{2,1,0:T(8,128)(2,1)S(1)}, u32[]{:S(2)}, u32[]{:S(2)}) collective-permute-start(bf16[2,32,384]{2,1,0:T(8,128)(2,1)S(1)} %pad_maximum_fusion.73), channel_id=1, source_target_pairs={{0,8},{4,12},{8,0},{12,4},{16,24},{20,28},{24,16},{28,20},{1,9},{5... | collective-permute-start | bytes 147464 | tf_op jit(solution)/shard_map/ppermute | solution.py:330
  126.7 56.0 %collective-permute-start.18 = (bf16[2,32,384]{2,1,0:T(8,128)(2,1)S(1)}, bf16[2,32,384]{2,1,0:T(8,128)(2,1)S(1)}, u32[]{:S(2)}, u32[]{:S(2)}) collective-permute-start(bf16[2,32,384]{2,1,0:T(8,128)(2,1)S(1)} %pad_maximum_fusion.74), channel_id=1, source_target_pairs={{0,2},{2,0},{1,3},{3,1},{4,6},{6,4},{5,7},{7,5},{8,10},{10,8},{9,1... | collective-permute-start | bytes 147464 | tf_op jit(solution)/shard_map/ppermute | solution.py:330
  134.2 51.0 %collective-permute-start.23 = (bf16[2,2,32,256]{3,2,1,0:T(8,128)(2,1)S(1)}, bf16[2,2,32,256]{3,2,1,0:T(8,128)(2,1)S(1)}, u32[]{:S(2)}, u32[]{:S(2)}) collective-permute-start(bf16[2,2,32,256]{3,2,1,0:T(8,128)(2,1)S(1)} %pad_maximum_fusion.71), channel_id=1, source_target_pairs={{0,2},{2,0},{1,3},{3,1},{4,6},{6,4},{5,7},{7,5},{8,10},{10,8},{9,1... | collective-permute-start | bytes 196616 | tf_op jit(solution)/shard_map/ppermute | solution.py:330
  276.3 222.1 %collective-permute-start.39 = (bf16[1024,512]{0,1:T(8,128)(2,1)}, bf16[1024,512]{0,1:T(8,128)(2,1)}, u32[]{:S(2)}, u32[]{:S(2)}) collective-permute-start(bf16[1024,512]{0,1:T(8,128)(2,1)} %fusion.403), channel_id=1, source_target_pairs={{0,1},{1,0},{2,3},{3,2},{4,5},{5,4},{6,7},{7,6},{8,9},{9,8},{10,11... | collective-permute-start | bytes 3145736 | tf_op jit(solution)/shard_map/ppermute | solution.py:330
  282.9 218.6 %collective-permute-start.37 = (bf16[1024,512]{0,1:T(8,128)(2,1)}, bf16[1024,512]{0,1:T(8,128)(2,1)}, u32[]{:S(2)}, u32[]{:S(2)}) collective-permute-start(bf16[1024,512]{0,1:T(8,128)(2,1)} %fusion.292), channel_id=1, source_target_pairs={{0,1},{1,0},{2,3},{3,2},{4,5},{5,4},{6,7},{7,6},{8,9},{9,8},{10,11... | collective-permute-start | bytes 3145736 | tf_op jit(solution)/shard_map/ppermute | solution.py:330
  340.4 196.3 %all-to-all-start.6 = ((bf16[32,80,992]{2,1,0:T(8,128)(2,1)}), bf16[32,80,992]{2,1,0:T(8,128)(2,1)}, u32[]{:S(2)}, u32[]{:S(2)}) async-start(bf16[32,80,992]{2,1,0:T(8,128)(2,1)} %bitcast.916), calls=%async_computation.6 | async-start | bytes 10485760 | tf_op jit(solution)/shard_map/all_to_all | solution.py:302
  349.1 117.1 %collective-permute-start.27 = (bf16[1,80,256]{2,1,0:T(8,128)(2,1)S(1)}, bf16[1,80,256]{2,1,0:T(8,128)(2,1)S(1)}, u32[]{:S(2)}, u32[]{:S(2)}) collective-permute-start(bf16[1,80,256]{2,1,0:T(8,128)(2,1)S(1)} %slice_bitcast_fusion.51), channel_id=1, source_target_pairs={{0,16},{4,20},{8,24},{12,28},{16,0},{20,4},{24,8},{28,12},{1,17},{... | collective-permute-start | bytes 122888 | tf_op jit(solution)/shard_map/ppermute | solution.py:330
  351.9 115.6 %collective-permute-start.26 = (bf16[1,80,384]{2,1,0:T(8,128)(2,1)S(1)}, bf16[1,80,384]{2,1,0:T(8,128)(2,1)S(1)}, u32[]{:S(2)}, u32[]{:S(2)}) collective-permute-start(bf16[1,80,384]{2,1,0:T(8,128)(2,1)S(1)} %get-tuple-element.652), channel_id=1, source_target_pairs={{0,16},{4,20},{8,24},{12,28},{16,0},{20,4},{24,8},{28,12},{1,17},{... | collective-permute-start | bytes 184328 | tf_op jit(solution)/shard_map/ppermute | solution.py:330
  352.2 116.1 %collective-permute-start.25 = (bf16[1,80,384]{2,1,0:T(8,128)(2,1)S(1)}, bf16[1,80,384]{2,1,0:T(8,128)(2,1)S(1)}, u32[]{:S(2)}, u32[]{:S(2)}) collective-permute-start(bf16[1,80,384]{2,1,0:T(8,128)(2,1)S(1)} %get-tuple-element.653), channel_id=1, source_target_pairs={{0,16},{4,20},{8,24},{12,28},{16,0},{20,4},{24,8},{28,12},{1,17},{... | collective-permute-start | bytes 184328 | tf_op jit(solution)/shard_map/ppermute | solution.py:330
  471.9 40.0 %collective-permute-start.38 = (bf16[512,2048]{1,0:T(8,128)(2,1)S(1)}, bf16[512,2048]{1,0:T(8,128)(2,1)S(1)}, u32[]{:S(2)}, u32[]{:S(2)}) collective-permute-start(bf16[512,2048]{1,0:T(8,128)(2,1)S(1)} %get-tuple-element.610), channel_id=1, source_target_pairs={{0,1},{1,0},{2,3},{3,2},{4,5},{5,4},{6,7},{7,6},{8,9},{9,8},{10,11... | collective-permute-start | bytes 6291464 | tf_op jit(solution)/shard_map/ppermute | solution.py:330
  479.6 27.7 %collective-permute-start.40 = (bf16[1024,512]{0,1:T(8,128)(2,1)S(1)}, bf16[1024,512]{0,1:T(8,128)(2,1)S(1)}, u32[]{:S(2)}, u32[]{:S(2)}) collective-permute-start(bf16[1024,512]{0,1:T(8,128)(2,1)S(1)} %get-tuple-element.619), channel_id=1, source_target_pairs={{0,1},{1,0},{2,3},{3,2},{4,5},{5,4},{6,7},{7,6},{8,9},{9,8},{10,11... | collective-permute-start | bytes 3145736 | tf_op jit(solution)/shard_map/ppermute | solution.py:330
  605.9 23.6 %collective-permute-start.44 = (f32[2,2,2,80,384]{4,3,0,2,1:T(8,128)S(1)}, f32[2,2,2,80,384]{4,3,0,2,1:T(8,128)S(1)}, u32[]{:S(2)}, u32[]{:S(2)}) collective-permute-start(f32[2,2,2,80,384]{4,3,0,2,1:T(8,128)S(1)} %bitcast.1019), channel_id=1, source_target_pairs={{0,4},{4,0},{8,12},{12,8},{16,20},{20,16},{24,28},{28,24},{1,5},{5... | collective-permute-start | bytes 2949128 | tf_op jit(solution)/shard_map/ppermute | solution.py:330
  606.7 23.3 %collective-permute-start.43 = (f32[2,2,2,80,384]{4,3,0,1,2:T(8,128)S(1)}, f32[2,2,2,80,384]{4,3,0,1,2:T(8,128)S(1)}, u32[]{:S(2)}, u32[]{:S(2)}) collective-permute-start(f32[2,2,2,80,384]{4,3,0,1,2:T(8,128)S(1)} %bitcast.1020), channel_id=1, source_target_pairs={{0,2},{2,0},{1,3},{3,1},{4,6},{6,4},{5,7},{7,5},{8,10},{10,8},{9,1... | collective-permute-start | bytes 2949128 | tf_op jit(solution)/shard_map/ppermute | solution.py:330
  689.3 27.1 %collective-permute-start.56 = (bf16[512,2048]{1,0:T(8,128)(2,1)}, bf16[512,2048]{1,0:T(8,128)(2,1)}, u32[]{:S(2)}, u32[]{:S(2)}) collective-permute-start(bf16[512,2048]{1,0:T(8,128)(2,1)} %get-tuple-element.608), channel_id=1, source_target_pairs={{0,1},{1,0},{2,3},{3,2},{4,5},{5,4},{6,7},{7,6},{8,9},{9,8},{10,11... | collective-permute-start | bytes 6291464 | tf_op jit(solution)/shard_map/ppermute | solution.py:330
  751.1 61.9 %collective-permute-start.59 = (f32[2,2,2,2,336,128]{5,4,3,2,1,0:T(8,128)}, f32[2,2,2,2,336,128]{5,4,3,2,1,0:T(8,128)}, u32[]{:S(2)}, u32[]{:S(2)}) collective-permute-start(f32[2,2,2,2,336,128]{5,4,3,2,1,0:T(8,128)} %slice_bitcast_fusion.1), channel_id=1, source_target_pairs={{0,8},{4,12},{8,0},{12,4},{16,24},{20,28},{24,16},{28,20},{1,9},{5... | collective-permute-start | bytes 8257544 | tf_op jit(solution)/shard_map/ppermute | solution.py:330
  755.8 61.9 %collective-permute-start.58 = (f32[2,2,2,2,336,128]{5,4,3,2,1,0:T(8,128)}, f32[2,2,2,2,336,128]{5,4,3,2,1,0:T(8,128)}, u32[]{:S(2)}, u32[]{:S(2)}) collective-permute-start(f32[2,2,2,2,336,128]{5,4,3,2,1,0:T(8,128)} %slice_bitcast_fusion.2), channel_id=1, source_target_pairs={{0,4},{4,0},{8,12},{12,8},{16,20},{20,16},{24,28},{28,24},{1,5},{5... | collective-permute-start | bytes 8257544 | tf_op jit(solution)/shard_map/ppermute | solution.py:330
  761.2 64.5 %collective-permute-start.57 = (f32[2,2,2,2,352,128]{5,4,3,2,1,0:T(8,128)}, f32[2,2,2,2,352,128]{5,4,3,2,1,0:T(8,128)}, u32[]{:S(2)}, u32[]{:S(2)}) collective-permute-start(f32[2,2,2,2,352,128]{5,4,3,2,1,0:T(8,128)} %slice_bitcast_fusion), channel_id=1, source_target_pairs={{0,2},{2,0},{1,3},{3,1},{4,6},{6,4},{5,7},{7,5},{8,10},{10,8},{9,1... | collective-permute-start | bytes 8650760 | tf_op jit(solution)/shard_map/ppermute | solution.py:330
  774.5 134.5 %collective-permute-start.64 = (bf16[512,1024]{1,0:T(8,128)(2,1)}, bf16[512,1024]{1,0:T(8,128)(2,1)}, u32[]{:S(2)}, u32[]{:S(2)}) collective-permute-start(bf16[512,1024]{1,0:T(8,128)(2,1)} %get-tuple-element.615), channel_id=1, source_target_pairs={{0,1},{1,0},{2,3},{3,2},{4,5},{5,4},{6,7},{7,6},{8,9},{9,8},{10,11... | collective-permute-start | bytes 3145736 | tf_op jit(solution)/shard_map/ppermute | solution.py:330
  829.0 62.7 %collective-permute-start.62 = (f32[2,2,2,336,128]{4,3,2,1,0:T(8,128)}, f32[2,2,2,336,128]{4,3,2,1,0:T(8,128)}, u32[]{:S(2)}, u32[]{:S(2)}) collective-permute-start(f32[2,2,2,336,128]{4,3,2,1,0:T(8,128)} %slice_bitcast_fusion.10), channel_id=1, source_target_pairs={{0,2},{2,0},{1,3},{3,1},{4,6},{6,4},{5,7},{7,5},{8,10},{10,8},{9,1... | collective-permute-start | bytes 4128776 | tf_op jit(solution)/shard_map/ppermute | solution.py:330
  830.5 64.4 %collective-permute-start.61 = (f32[2,2,2,336,128]{4,3,2,1,0:T(8,128)}, f32[2,2,2,336,128]{4,3,2,1,0:T(8,128)}, u32[]{:S(2)}, u32[]{:S(2)}) collective-permute-start(f32[2,2,2,336,128]{4,3,2,1,0:T(8,128)} %slice_bitcast_fusion.11), channel_id=1, source_target_pairs={{0,8},{4,12},{8,0},{12,4},{16,24},{20,28},{24,16},{28,20},{1,9},{5... | collective-permute-start | bytes 4128776 | tf_op jit(solution)/shard_map/ppermute | solution.py:330
  831.7 65.8 %collective-permute-start.60 = (f32[2,2,2,352,128]{4,3,2,1,0:T(8,128)}, f32[2,2,2,352,128]{4,3,2,1,0:T(8,128)}, u32[]{:S(2)}, u32[]{:S(2)}) collective-permute-start(f32[2,2,2,352,128]{4,3,2,1,0:T(8,128)} %slice_bitcast_fusion.5), channel_id=1, source_target_pairs={{0,4},{4,0},{8,12},{12,8},{16,20},{20,16},{24,28},{28,24},{1,5},{5... | collective-permute-start | bytes 4325384 | tf_op jit(solution)/shard_map/ppermute | solution.py:330
  940.6 63.3 %collective-permute-start.73 = (f32[2,2,2,1,336,128]{5,4,2,1,0,3:T(8,128)}, f32[2,2,2,1,336,128]{5,4,2,1,0,3:T(8,128)}, u32[]{:S(2)}, u32[]{:S(2)}) collective-permute-start(f32[2,2,2,1,336,128]{5,4,2,1,0,3:T(8,128)} %slice_bitcast_fusion.8), channel_id=1, source_target_pairs={{0,8},{4,12},{8,0},{12,4},{16,24},{20,28},{24,16},{28,20},{1,9},{5... | collective-permute-start | bytes 4128776 | tf_op jit(solution)/shard_map/ppermute | solution.py:330
  944.9 60.7 %collective-permute-start.72 = (f32[2,2,2,1,336,128]{5,4,2,1,0,3:T(8,128)}, f32[2,2,2,1,336,128]{5,4,2,1,0,3:T(8,128)}, u32[]{:S(2)}, u32[]{:S(2)}) collective-permute-start(f32[2,2,2,1,336,128]{5,4,2,1,0,3:T(8,128)} %slice_bitcast_fusion.9), channel_id=1, source_target_pairs={{0,4},{4,0},{8,12},{12,8},{16,20},{20,16},{24,28},{28,24},{1,5},{5... | collective-permute-start | bytes 4128776 | tf_op jit(solution)/shard_map/ppermute | solution.py:330
  947.6 59.6 %collective-permute-start.71 = (f32[2,2,2,1,352,128]{5,4,2,1,0,3:T(8,128)}, f32[2,2,2,1,352,128]{5,4,2,1,0,3:T(8,128)}, u32[]{:S(2)}, u32[]{:S(2)}) collective-permute-start(f32[2,2,2,1,352,128]{5,4,2,1,0,3:T(8,128)} %slice_bitcast_fusion.4), channel_id=1, source_target_pairs={{0,2},{2,0},{1,3},{3,1},{4,6},{6,4},{5,7},{7,5},{8,10},{10,8},{9,1... | collective-permute-start | bytes 4325384 | tf_op jit(solution)/shard_map/ppermute | solution.py:330
  953.1 27.5 %collective-permute-start.70 = (f32[2,336,128]{2,1,0:T(8,128)}, f32[2,336,128]{2,1,0:T(8,128)}, u32[]{:S(2)}, u32[]{:S(2)}) collective-permute-start(f32[2,336,128]{2,1,0:T(8,128)} %slice_bitcast_fusion.30), channel_id=1, source_target_pairs={{0,16},{4,20},{8,24},{12,28},{16,0},{20,4},{24,8},{28,12},{1,17},{... | collective-permute-start | bytes 1032200 | tf_op jit(solution)/shard_map/ppermute | solution.py:330
  954.0 34.1 %collective-permute-start.69 = (f32[2,336,128]{2,1,0:T(8,128)}, f32[2,336,128]{2,1,0:T(8,128)}, u32[]{:S(2)}, u32[]{:S(2)}) collective-permute-start(f32[2,336,128]{2,1,0:T(8,128)} %slice_bitcast_fusion.31), channel_id=1, source_target_pairs={{0,16},{4,20},{8,24},{12,28},{16,0},{20,4},{24,8},{28,12},{1,17},{... | collective-permute-start | bytes 1032200 | tf_op jit(solution)/shard_map/ppermute | solution.py:330
  988.0 45.7 %collective-permute-start.80 = (f32[2,2,2,2,288,128]{5,4,3,2,1,0:T(8,128)S(1)}, f32[2,2,2,2,288,128]{5,4,3,2,1,0:T(8,128)S(1)}, u32[]{:S(2)}, u32[]{:S(2)}) collective-permute-start(f32[2,2,2,2,288,128]{5,4,3,2,1,0:T(8,128)S(1)} %dynamic-slice_bitcast_fusion), channel_id=1, source_target_pairs={{0,1},{1,0},{2,3},{3,2},{4,5},{5,4},{6,7},{7,6},{8,9},{9,8},{10,11... | collective-permute-start | bytes 7077896 | tf_op jit(solution)/shard_map/ppermute | solution.py:330
  1008.9 35.1 %collective-permute-start.79 = (f32[2,2,1,336,128]{4,3,1,0,2:T(8,128)S(1)}, f32[2,2,1,336,128]{4,3,1,0,2:T(8,128)S(1)}, u32[]{:S(2)}, u32[]{:S(2)}) collective-permute-start(f32[2,2,1,336,128]{4,3,1,0,2:T(8,128)S(1)} %slice_bitcast_fusion.17), channel_id=1, source_target_pairs={{0,2},{2,0},{1,3},{3,1},{4,6},{6,4},{5,7},{7,5},{8,10},{10,8},{9,1... | collective-permute-start | bytes 2064392 | tf_op jit(solution)/shard_map/ppermute | solution.py:330
  1009.6 34.5 %collective-permute-start.78 = (f32[2,2,1,336,128]{4,3,1,0,2:T(8,128)S(1)}, f32[2,2,1,336,128]{4,3,1,0,2:T(8,128)S(1)}, u32[]{:S(2)}, u32[]{:S(2)}) collective-permute-start(f32[2,2,1,336,128]{4,3,1,0,2:T(8,128)S(1)} %slice_bitcast_fusion.18), channel_id=1, source_target_pairs={{0,8},{4,12},{8,0},{12,4},{16,24},{20,28},{24,16},{28,20},{1,9},{5... | collective-permute-start | bytes 2064392 | tf_op jit(solution)/shard_map/ppermute | solution.py:330
  1009.8 34.4 %collective-permute-start.77 = (f32[2,2,1,352,128]{4,3,1,0,2:T(8,128)S(1)}, f32[2,2,1,352,128]{4,3,1,0,2:T(8,128)S(1)}, u32[]{:S(2)}, u32[]{:S(2)}) collective-permute-start(f32[2,2,1,352,128]{4,3,1,0,2:T(8,128)S(1)} %slice_bitcast_fusion.13), channel_id=1, source_target_pairs={{0,4},{4,0},{8,12},{12,8},{16,20},{20,16},{24,28},{28,24},{1,5},{5... | collective-permute-start | bytes 2162696 | tf_op jit(solution)/shard_map/ppermute | solution.py:330
  1042.3 26.4 %collective-permute-start.81 = (f32[2,2,2,288,128]{4,3,2,1,0:T(8,128)S(1)}, f32[2,2,2,288,128]{4,3,2,1,0:T(8,128)S(1)}, u32[]{:S(2)}, u32[]{:S(2)}) collective-permute-start(f32[2,2,2,288,128]{4,3,2,1,0:T(8,128)S(1)} %dynamic-slice_bitcast_fusion.1), channel_id=1, source_target_pairs={{0,2},{2,0},{1,3},{3,1},{4,6},{6,4},{5,7},{7,5},{8,10},{10,8},{9,1... | collective-permute-start | bytes 3538952 | tf_op jit(solution)/shard_map/ppermute | solution.py:330
  1068.9 26.3 %collective-permute-start.88 = (f32[2,2,288,128]{3,2,1,0:T(8,128)S(1)}, f32[2,2,288,128]{3,2,1,0:T(8,128)S(1)}, u32[]{:S(2)}, u32[]{:S(2)}) collective-permute-start(f32[2,2,288,128]{3,2,1,0:T(8,128)S(1)} %dynamic-slice_bitcast_fusion.3), channel_id=1, source_target_pairs={{0,4},{4,0},{8,12},{12,8},{16,20},{20,16},{24,28},{28,24},{1,5},{5... | collective-permute-start | bytes 1769480 | tf_op jit(solution)/shard_map/ppermute | solution.py:330
  1069.8 24.4 %collective-permute-start.87 = (f32[2,1,336,128]{3,2,0,1:T(8,128)S(1)}, f32[2,1,336,128]{3,2,0,1:T(8,128)S(1)}, u32[]{:S(2)}, u32[]{:S(2)}) collective-permute-start(f32[2,1,336,128]{3,2,0,1:T(8,128)S(1)} %slice_bitcast_fusion.28), channel_id=1, source_target_pairs={{0,4},{4,0},{8,12},{12,8},{16,20},{20,16},{24,28},{28,24},{1,5},{5... | collective-permute-start | bytes 1032200 | tf_op jit(solution)/shard_map/ppermute | solution.py:330
  1071.1 23.3 %collective-permute-start.86 = (f32[2,1,336,128]{3,2,0,1:T(8,128)S(1)}, f32[2,1,336,128]{3,2,0,1:T(8,128)S(1)}, u32[]{:S(2)}, u32[]{:S(2)}) collective-permute-start(f32[2,1,336,128]{3,2,0,1:T(8,128)S(1)} %slice_bitcast_fusion.29), channel_id=1, source_target_pairs={{0,2},{2,0},{1,3},{3,1},{4,6},{6,4},{5,7},{7,5},{8,10},{10,8},{9,1... | collective-permute-start | bytes 1032200 | tf_op jit(solution)/shard_map/ppermute | solution.py:330
  1096.1 117.1 %collective-permute-start.95 = (f32[2,288,128]{2,1,0:T(8,128)}, f32[2,288,128]{2,1,0:T(8,128)}, u32[]{:S(2)}, u32[]{:S(2)}) collective-permute-start(f32[2,288,128]{2,1,0:T(8,128)} %dynamic-slice_bitcast_fusion.6), channel_id=1, source_target_pairs={{0,8},{4,12},{8,0},{12,4},{16,24},{20,28},{24,16},{28,20},{1,9},{5... | collective-permute-start | bytes 884744 | tf_op jit(solution)/shard_map/ppermute | solution.py:330
  1097.3 85.4 %collective-permute-start.94 = (f32[1,336,128]{2,1,0:T(8,128)}, f32[1,336,128]{2,1,0:T(8,128)}, u32[]{:S(2)}, u32[]{:S(2)}) collective-permute-start(f32[1,336,128]{2,1,0:T(8,128)} %slice_bitcast_fusion.42), channel_id=1, source_target_pairs={{0,16},{4,20},{8,24},{12,28},{16,0},{20,4},{24,8},{28,12},{1,17},{... | collective-permute-start | bytes 516104 | tf_op jit(solution)/shard_map/ppermute | solution.py:330
  1100.0 182.5 %all-to-all-start.9 = ((f32[32,32,1024]{2,1,0:T(8,128)}), f32[32,32,1024]{2,1,0:T(8,128)}, u32[]{:S(2)}, u32[]{:S(2)}) async-start(f32[32,32,1024]{2,1,0:T(8,128)} %bitcast.962), calls=%async_computation.9 | async-start | bytes 8388608 | tf_op jit(solution)/shard_map/all_to_all | solution.py:302
  1104.5 104.7 %collective-permute-start.93 = (f32[1,336,128]{2,1,0:T(8,128)S(1)}, f32[1,336,128]{2,1,0:T(8,128)S(1)}, u32[]{:S(2)}, u32[]{:S(2)}) collective-permute-start(f32[1,336,128]{2,1,0:T(8,128)S(1)} %slice_bitcast_fusion.43), channel_id=1, source_target_pairs={{0,16},{4,20},{8,24},{12,28},{16,0},{20,4},{24,8},{28,12},{1,17},{... | collective-permute-start | bytes 516104 | tf_op jit(solution)/shard_map/ppermute | solution.py:330
  1107.1 105.4 %collective-permute-start.92 = (f32[1,352,128]{2,1,0:T(8,128)S(1)}, f32[1,352,128]{2,1,0:T(8,128)S(1)}, u32[]{:S(2)}, u32[]{:S(2)}) collective-permute-start(f32[1,352,128]{2,1,0:T(8,128)S(1)} %slice_bitcast_fusion.37), channel_id=1, source_target_pairs={{0,16},{4,20},{8,24},{12,28},{16,0},{20,4},{24,8},{28,12},{1,17},{... | collective-permute-start | bytes 540680 | tf_op jit(solution)/shard_map/ppermute | solution.py:330
  1139.7 42.1 %collective-permute-start.89 = (f32[2,32,384]{2,1,0:T(8,128)S(1)}, f32[2,32,384]{2,1,0:T(8,128)S(1)}, u32[]{:S(2)}, u32[]{:S(2)}) collective-permute-start(f32[2,32,384]{2,1,0:T(8,128)S(1)} %dynamic-slice_bitcast_fusion.13), channel_id=1, source_target_pairs={{0,8},{4,12},{8,0},{12,4},{16,24},{20,28},{24,16},{28,20},{1,9},{5... | collective-permute-start | bytes 294920 | tf_op jit(solution)/shard_map/ppermute | solution.py:330
  1413.7 35.0 %collective-permute-start.132 = (bf16[8,352,256]{2,1,0:T(8,128)(2,1)S(1)}, bf16[8,352,256]{2,1,0:T(8,128)(2,1)}, u32[]{:S(2)}, u32[]{:S(2)}) collective-permute-start(bf16[8,352,256]{2,1,0:T(8,128)(2,1)S(1)} %pad_maximum_fusion.15), channel_id=1, source_target_pairs={{0,2},{2,0},{1,3},{3,1},{4,6},{6,4},{5,7},{7,5},{8,10},{10,8},{9,1... | collective-permute-start | bytes 4325384 | tf_op jit(solution)/shard_map/ppermute | solution.py:330
  1415.3 29.0 %collective-permute-start.133 = (bf16[8,336,256]{2,1,0:T(8,128)(2,1)}, bf16[8,336,256]{2,1,0:T(8,128)(2,1)}, u32[]{:S(2)}, u32[]{:S(2)}) collective-permute-start(bf16[8,336,256]{2,1,0:T(8,128)(2,1)} %pad_maximum_fusion.16), channel_id=1, source_target_pairs={{0,4},{4,0},{8,12},{12,8},{16,20},{20,16},{24,28},{28,24},{1,5},{5... | collective-permute-start | bytes 4128776 | tf_op jit(solution)/shard_map/ppermute | solution.py:330
  1415.8 30.7 %collective-permute-start.134 = (bf16[8,336,256]{2,1,0:T(8,128)(2,1)}, bf16[8,336,256]{2,1,0:T(8,128)(2,1)}, u32[]{:S(2)}, u32[]{:S(2)}) collective-permute-start(bf16[8,336,256]{2,1,0:T(8,128)(2,1)} %pad_maximum_fusion.17), channel_id=1, source_target_pairs={{0,8},{4,12},{8,0},{12,4},{16,24},{20,28},{24,16},{28,20},{1,9},{5... | collective-permute-start | bytes 4128776 | tf_op jit(solution)/shard_map/ppermute | solution.py:330
  (242 other events, 4635.0 us)
Sparse Core Ops, SparseCore 0:
  11.4 96.7 all-gather.4
  111.7 144.2 all-gather.6

commit v5 on v4

--- a/solution.py
+++ b/solution.py
@@ -68,22 +68,6 @@
     return jnp.sum(inputs.astype(jnp.float32), axis=(0, 1))
 
 
-def to_heads(inputs):
-    return inputs.reshape(
-        inputs.shape[0], inputs.shape[1] // WINDOW, WINDOW, HEADS, inputs.shape[2] // HEADS
-    )
-
-
-def attn_scores(queries, key_proj, allowed):
-    raw_scores = jnp.einsum(
-        "bnqhe,bnkhe->bnhqk",
-        to_heads(queries),
-        to_heads(key_proj),
-        preferred_element_type=jnp.float32,
-    )
-    return jnp.where(allowed, raw_scores * (queries.shape[2] // HEADS) ** (-0.5), masked_fill)
-
-
 def share(values, axis):
     return jnp.concatenate([values, exchange(values, side_bit)], axis=axis)
 
@@ -103,20 +87,90 @@
     return jnp.concatenate([keep, got])
 
 
+def head_scores(q_ref, k_ref, allow_ref, cols):
+    scores = lax.dot_general(
+        q_ref[:, cols], k_ref[:, cols], (((1,), (1,)), ((), ())), preferred_element_type=jnp.float32
+    )
+    return jnp.where(allow_ref[...] > 0.0, scores * (D // HEADS) ** (-0.5), masked_fill)
+
+
+def attend_kernel(q_ref, k_ref, v_ref, allow_ref, out_ref, total_ref):
+    width = D // HEADS
+    for head in range(q_ref.shape[1] // width):
+        cols = slice(head * width, (head + 1) * width)
+        scores = head_scores(q_ref, k_ref, allow_ref, cols)
+        top = jnp.max(scores, axis=1, keepdims=True)
+        total = top + jnp.log(jnp.sum(jnp.exp(scores - top), axis=1, keepdims=True))
+        probs = jnp.exp(scores - total).astype(jnp.bfloat16)
+        found = jnp.dot(probs, v_ref[:, cols], preferred_element_type=jnp.float32)
+        out_ref[:, cols] = found.astype(jnp.bfloat16)
+        total_ref[head] = total
+
+
+def attend_back_kernel(
+    q_ref, k_ref, v_ref, allow_ref, total_ref, grad_ref, q_out, k_out, v_out
+):
+    width = D // HEADS
+    rows = (((0,), (0,)), ((), ()))
+    for head in range(q_ref.shape[1] // width):
+        cols = slice(head * width, (head + 1) * width)
+        grads = grad_ref[:, cols]
+        probs = jnp.exp(head_scores(q_ref, k_ref, allow_ref, cols) - total_ref[head])
+        grad_probs = lax.dot_general(
+            grads, v_ref[:, cols], (((1,), (1,)), ((), ())), preferred_element_type=jnp.float32
+        )
+        grad_value = lax.dot_general(
+            probs.astype(jnp.bfloat16), grads, rows, preferred_element_type=jnp.float32
+        )
+        inner = jnp.sum(grad_probs * probs, axis=1, keepdims=True)
+        raw = (probs * (grad_probs - inner) * width ** (-0.5)).astype(jnp.bfloat16)
+        grad_query = jnp.dot(raw, k_ref[:, cols], preferred_element_type=jnp.float32)
+        grad_key = lax.dot_general(
+            raw, q_ref[:, cols], rows, preferred_element_type=jnp.float32
+        )
+        q_out[:, cols] = grad_query.astype(jnp.bfloat16)
+        k_out[:, cols] = grad_key.astype(jnp.bfloat16)
+        v_out[:, cols] = grad_value.astype(jnp.bfloat16)
+
+
+def attend(queries, key_proj, values, allow):
+    pair = lanes * HEADS // D
+    cols = pl.BlockSpec((WINDOW, lanes), lambda step: (0, step))
+    whole = pl.BlockSpec((WINDOW, WINDOW), lambda step: (0, 0))
+    return pl.pallas_call(
+        attend_kernel,
+        grid=(D // lanes,),
+        in_specs=[cols, cols, cols, whole],
+        out_specs=[cols, pl.BlockSpec((pair, WINDOW, 1), lambda step: (step, 0, 0))],
+        out_shape=[
+            jax.ShapeDtypeStruct((WINDOW, D), jnp.bfloat16),
+            jax.ShapeDtypeStruct((HEADS, WINDOW, 1), jnp.float32),
+        ],
+    )(queries, key_proj, values, allow)
+
+
+def attend_back(queries, key_proj, values, allow, totals, grads):
+    pair = lanes * HEADS // D
+    cols = pl.BlockSpec((WINDOW, lanes), lambda step: (0, step))
+    whole = pl.BlockSpec((WINDOW, WINDOW), lambda step: (0, 0))
+    total = pl.BlockSpec((pair, WINDOW, 1), lambda step: (step, 0, 0))
+    return pl.pallas_call(
+        attend_back_kernel,
+        grid=(D // lanes,),
+        in_specs=[cols, cols, cols, whole, total, cols],
+        out_specs=[cols] * 3,
+        out_shape=[jax.ShapeDtypeStruct((WINDOW, D), jnp.bfloat16)] * 3,
+    )(queries, key_proj, values, allow, totals, grads)
+
+
 def layer_forward(hidden, params, allowed):
     w_query, w_key, w_value, w_out, w_up, w_down, up_bias, vectors = params
-    count, length, model_width = hidden.shape
     inputs = hidden.astype(jnp.bfloat16)
     queries = (project(inputs, w_query) + vectors[4]).astype(jnp.bfloat16)
     key_proj = project(inputs, w_key).astype(jnp.bfloat16)
     values = (project(inputs, w_value) + vectors[5]).astype(jnp.bfloat16)
-    scores = attn_scores(queries, key_proj, allowed)
-    log_total = jax.nn.logsumexp(scores, axis=-1, keepdims=True)
-    prob_low = jnp.exp(scores - log_total).astype(jnp.bfloat16)
-    context = jnp.einsum(
-        "bnhqk,bnkhe->bnqhe", prob_low, to_heads(values), preferred_element_type=jnp.float32
-    )
-    context = context.reshape(count, length, model_width).astype(jnp.bfloat16)
+    context, log_total = attend(queries[0], key_proj[0], values[0], allowed)
+    context = context[None]
     attn_sum = hidden + (project(context, w_out) + vectors[6])
     middle, first_pull = jax.vjp(layer_norm, attn_sum, vectors[0], vectors[1])
     middle_low = middle.astype(jnp.bfloat16)
@@ -150,7 +204,6 @@
 def layer_backward(grad_out, stored, shared, params, allowed):
     w_query, w_key, w_value, w_out, w_up, w_down, _, _ = params
     (_, queries, key_proj, values, log_total, _, first_pull, _, gelu_pull, _, second_pull) = stored
-    count, length, model_width = grad_out.shape
     grad_ffn, grad_gain_two, grad_shift_two = second_pull(grad_out)
     down_low = grad_ffn.astype(jnp.bfloat16)
     (grad_up,) = gelu_pull(project(down_low, w_down))
@@ -174,30 +227,11 @@
     grad_middle = grad_ffn + project_back(up_low, w_up)
     grad_attn, grad_gain_one, grad_shift_one = first_pull(grad_middle)
     attn_low = grad_attn.astype(jnp.bfloat16)
-    grad_context = to_heads(project_back(attn_low, w_out).astype(jnp.bfloat16))
-    attn_prob = jnp.exp(attn_scores(queries, key_proj, allowed) - log_total)
-    prob_low = attn_prob.astype(jnp.bfloat16)
-    grad_prob = jnp.einsum(
-        "bnqhe,bnkhe->bnhqk", grad_context, to_heads(values), preferred_element_type=jnp.float32
-    )
-    grad_value = jnp.einsum(
-        "bnhqk,bnqhe->bnkhe", prob_low, grad_context, preferred_element_type=jnp.float32
-    )
-    grad_value = grad_value.reshape(count, length, model_width).astype(jnp.bfloat16)
-    grad_scores = attn_prob * (grad_prob - jnp.sum(grad_prob * attn_prob, -1, keepdims=True))
-    grad_raw = (grad_scores * (model_width // HEADS) ** (-0.5)).astype(jnp.bfloat16)
-    late_keys, parts = tied(key_proj, parts)
+    grad_context = project_back(attn_low, w_out).astype(jnp.bfloat16)
+    grads = attend_back(queries[0], key_proj[0], values[0], allowed, log_total, grad_context[0])
+    grad_query, grad_key, grad_value = (found[None] for found in grads)
+    grad_query, parts = tied(grad_query, parts)
     parts = reduce_step(parts, wide_count, 1)
-    grad_query = jnp.einsum(
-        "bnhqk,bnkhe->bnqhe", grad_raw, to_heads(late_keys), preferred_element_type=jnp.float32
-    )
-    grad_query = grad_query.reshape(count, length, model_width).astype(jnp.bfloat16)
-    grad_key = jnp.einsum(
-        "bnhqk,bnqhe->bnkhe", grad_raw, to_heads(queries), preferred_element_type=jnp.float32
-    )
-    grad_key = grad_key.reshape(count, length, model_width).astype(jnp.bfloat16)
-    grad_query, parts = tied(grad_query, parts)
-    parts = reduce_step(parts, wide_count, 2)
     operands = (
         shared[2],
         shared[3],
@@ -211,17 +245,14 @@
                             jnp.dot(*operands[1::2], preferred_element_type=jnp.float32)])
         blocks = blocks.reshape(2, 1, D, wide_count, -1).transpose(3, 0, 1, 2, 4)
         attn_parts = in_routes(blocks, wide_count)
-    last_query, attn_parts = tied(grad_query, attn_parts)
-    attn_parts = reduce_step(attn_parts, wide_count, 0)
     grad_hidden = (
         grad_attn
-        + project_back(last_query, w_query)
+        + project_back(grad_query, w_query)
         + project_back(grad_key, w_key)
         + project_back(grad_value, w_value)
     )
     grad_hidden, parts = tied(grad_hidden, parts)
-    for step in range(3, len(routes(wide_count)[0])):
-        parts = reduce_step(parts, wide_count, step)
+    parts = reduce_step(parts, wide_count, 2)
     matrices = (attn_parts, parts)
     vector_grads = jnp.stack(
         [
@@ -841,7 +872,13 @@
     place_rows = halve(place_rows.reshape(2, group, per_place, D), side_bit, 0)
     place_parts = route_parts(place_rows, wide_count)
     for step in range(len(routes(wide_count)[0])):
-        (place_parts,) = lockstep(route_step(place_parts, wide_count, step, False))
+        place_parts = route_step(place_parts, wide_count, step, False)
+        if step == 0:
+            place_parts, (source_own,) = lockstep(
+                place_parts, [source_logits.reshape(MPW, V)]
+            )
+        else:
+            (place_parts,) = lockstep(place_parts)
     place_own = jnp.concatenate(place_parts, axis=-1)
     place_all = gather_blocks(place_own, wide_count, 1, lanes).reshape(WINDOW, D)
 
@@ -853,7 +890,6 @@
         return swap_all(requests(addresses).reshape(devices, slots)).reshape(-1) - 1
 
     fetched = fetch(asked)
-    source_own = source_logits.reshape(MPW, V)
     source_max = jnp.max(source_own, axis=1).astype(jnp.float32)
     source_sum = jnp.sum(jnp.exp(source_own.astype(jnp.float32) - source_max[:, None]), axis=1)
     source_total = source_max + jnp.log(source_sum)
@@ -880,10 +916,9 @@
     )
 
     is_valid = (order[None, :] < live_lengths[:, None]) & (key_keep == 1)
-    key_ok = is_valid.reshape(win_count, 1, 1, 1, WINDOW)
-    bucket_ids = buckets.reshape(win_count, 1, WINDOW)
-    same_bucket = bucket_ids[:, :, None, :, None] == bucket_ids[:, :, None, None, :]
-    allowed = same_bucket & key_ok | jnp.eye(WINDOW, dtype=bool)
+    same_bucket = buckets.reshape(WINDOW, 1) == buckets.reshape(1, WINDOW)
+    allowed = same_bucket & is_valid.reshape(1, WINDOW) | jnp.eye(WINDOW, dtype=bool)
+    allowed = allowed.astype(jnp.float32)
     embedded = (token_rows + place_all.astype(jnp.float32)).reshape(win_count, WINDOW, D)
     hidden, embed_pull = jax.vjp(layer_norm, embedded, vectors[0], vectors[1])
     params = (
@@ -969,7 +1004,7 @@
     flat_embed = grad_embed.reshape(WINDOW, D)
 
     ffn_parts, attn_parts = layer_mats[1], layer_mats[0]
-    (flat_embed,), ffn_parts, attn_parts = lockstep([flat_embed], ffn_parts, attn_parts)
+    flat_embed, ffn_parts = tied(flat_embed, ffn_parts)
     dec_block = jnp.zeros((devices * owned,), jnp.float32)
     dec_block = lax.dynamic_update_slice(dec_block, grad_dec, (device * owned,))[:V]
     vector_block = jnp.concatenate(
@@ -988,21 +1023,32 @@
     other_part = scatter_flat(front, grad_head_w.reshape(-1, lanes), size, devices)
 
     place_grad = flat_embed.reshape(group, per_place, D)
-    ffn_grad = jnp.concatenate(ffn_parts, axis=1)
     sent = add_rows(now, flat_embed, devices * slots)
     arrived = swap_all(sent.reshape(devices, slots, D))
     place_parts = route_parts(place_grad.reshape(group, per_place, D), wide_count)
     steps = len(routes(wide_count)[0])
+
+    def place_step(parts, turn):
+        if turn < steps:
+            parts = route_step(parts, wide_count, turn, False)
+            if turn + 1 == steps:
+                parts = gather_start(jnp.concatenate(parts, axis=-1), 1, lanes)
+            return parts
+        return gather_step(parts, wide_count, turn - steps)
+
     for step in range(steps):
-        place_parts, attn_parts, (other_part,) = lockstep(
-            route_step(place_parts, wide_count, step, False),
-            reduce_step(attn_parts, wide_count, step + 1) if step + 1 < steps else attn_parts,
-            [other_step(other_part, wide_count, step)],
+        if step + 3 < steps:
+            ffn_parts = reduce_step(ffn_parts, wide_count, step + 3)
+        attn_parts = reduce_step(attn_parts, wide_count, step)
+        other_part = other_step(other_part, wide_count, step)
+        (place_parts,) = lockstep(place_step(place_parts, 2 * step))
+        place_parts, attn_parts, ffn_parts, (other_part,) = lockstep(
+            place_step(place_parts, 2 * step + 1), attn_parts, ffn_parts, [other_part]
         )
+    ffn_grad = jnp.concatenate(ffn_parts, axis=1)
     attn_grad = jnp.concatenate(attn_parts, axis=1)
     other_grad = own_share(other_part, size, device)
-    place_grad = jnp.concatenate(place_parts, axis=-1)
-    place_grad = gather_relative(place_grad, wide_count, 1, lanes)
+    place_grad = gather_end(place_parts, wide_count, 1)
     place_grad = jnp.concatenate([place_grad, exchange(place_grad, side_bit)])
     turn = jnp.arange(devices, dtype=jnp.int32)[:, None]
     place_ids = (turn // group ^ side) * WINDOW + (turn % group ^ here) * per_place

time: 1520 us -> 1420 us (0.934)
  matrix products: 294 us -> 205 us
  Pallas kernels: 88.6 us -> 124 us
  starting transfers between devices: 175 us -> 156 us
    dot_general x6 -> x0, matrix products: 83.7 us -> none  [the longest x1 24.7 us: layer_backward(): jnp.einsum('bnhqk,bnqhe->bnkhe', grad_raw, to_heads(queries), preferred_e...]
    pallas_call x0 -> x2, Pallas kernels: none -> 36.4 us  [the longest x1 19.6 us: attend_back(): pl.pallas_call(attend_back_kernel, grid=(D // lanes,), in_specs=[cols, co...]
    ppermute x136, starting transfers between devices: 145 us -> 125 us  [exchange(): return lax.ppermute(values, axis, steps)]
  transfers between devices with their start and end apart: 145 -> 145, of which waited for: 91 -> 86; matrix products, arithmetic and copies ran while one was open for 30% -> 26% of each run, Pallas kernels for 2% -> 6%
where the time goes in v5:
time: 1420 us; the launch traced here: 1410 us
  waiting for transfers between devices  626 us (44%)
  matrix products  205 us (14%)
  other arithmetic  157 us (11%)
  starting transfers between devices  156 us (11%)
  Pallas kernels  124 us (9%)
  local copies, waits for them, and re-layouts  116 us (8%)
  between operations  29.9 us (2%)
    ppermute x136, waiting for transfers between devices, exchange(): return lax.ppermute(values, axis, steps)  596 us
    ppermute x136, starting transfers between devices, exchange(): return lax.ppermute(values, axis, steps)  125 us
    dot_general x6, matrix products, project(): jnp.einsum('bsd,df->bsf', inputs, weight, preferred_element_type=jnp.floa...  49.1 us
    all_to_all x7, starting transfers between devices, swap_all(): return lax.all_to_all(blocks, axes, 0, 0, tiled=True)  31.5 us
    all_to_all x7, waiting for transfers between devices, swap_all(): return lax.all_to_all(blocks, axes, 0, 0, tiled=True)  29.6 us
    add x24, other arithmetic, reduce_step(): part[0] + exchange(part[1], route[step])  29.4 us
  transfers between devices with their start and end apart: 145, of which 86 were waited for; matrix products, arithmetic and copies ran while one was open for 26% of the time, Pallas kernels for 6%

profile of v5, /device:TPU:0, one launch (start us, length us, event | category | flops | bytes accessed | tf_op | source)
XLA Modules:
  0.0 1414.3 jit_solution(6516443509222811383)
XLA Ops:
  26.9 7.2 all-to-all-start.4
  35.4 5.9 all-to-all-done.4
  53.7 8.7 collective-permute-done.3
  97.5 10.7 reshape.1467
  108.3 7.8 copy.411
  134.3 45.2 %collective-permute-done.14 = bf16[2,32,384]{2,1,0:T(8,128)(2,1)S(1)} collective-permute-done((bf16[2,32,384]{2,1,0:T(8,128)(2,1)S(1)}, bf16[2,32,384]{2,1,0:T(8,128)(2,1)S(1)}, u32[]{:S(2)}, u32[]{:S(2)}) %collective-permute-start.14) | collective-permute-done | bytes 49184 | tf_op jit(solution)/shard_map/ppermute | solution.py:361
  207.5 7.6 shard_map.266
  231.6 16.8 %shard_map.267 = (bf16[512,1024]{1,0:T(8,128)(2,1)}, f32[16,512,1]{2,1,0:T(8,128)}) custom-call(bf16[512,1024]{1,0:T(8,128)(2,1)} %add_convert_fusion.3.q_ref, bf16[512,1024]{1,0:T(8,128)(2,1)} %convolution_convert_fusion.1.k_ref, bf16[512,1024]{1,0:T(8,128)(2,1)} %add_convert_fusion.2.v_ref, f32[512,512]{1,0:T(8,128)} %fusion.178.allow_ref), custom_call_target="tpu_custom_call" | custom-call | tf_op jit(solution)/shard_map/pallas_call | solution.py:140
  258.9 17.9 %shard_map.268 = (bf16[1024,4096]{1,0:T(8,128)(2,1)}, bf16[1024,4096]{1,0:T(8,128)(2,1)}) custom-call(bf16[32,2,1024,128]{3,2,1,0:T(8,128)(2,1)} %bitcast.883, bf16[32,2,1024,128]{3,2,1,0:T(8,128)(2,1)} %bitcast.884, bf16[32,2,1024,128]{3,2,1,0:T(8,128)(2,1)} %bitcast.885, bf16[32,2,1024,128]{3,2,1,0:T(8,128)(2,1)} %bitcast.886), custom_call_target="tpu_custom_call" | custom-call | tf_op jit(solution)/shard_map/pallas_call | solution.py:725
  276.9 28.0 %multiply_convert_fusion = (bf16[512,4096]{1,0:T(8,128)(2,1)S(1)}, f32[512,4096]{1,0:T(8,128)}, f32[512,4096]{1,0:T(8,128)}) fusion(f32[4096]{0:T(1024)S(1)} %bitcast.1010, bf16[1024,4096]{1,0:T(8,128)(2,1)} %get-tuple-element.398, f32[512,1024]{1,0:T(8,128)} %copy-done.2, f32[1024]{0:T(1024)S(1)} %get-tuple-element.682, f32[1024]{0:T(1024)S(1)} %get-tuple-element.683, ...), kind=kOutput, calls=%fused_computation.39 | convolution fusion | flops 4436000768 | bytes 31485952 | tf_op jit(solution)/shard_map/bsd,df->bsf/dot_general | solution.py:60
  327.1 111.3 %collective-permute-done.27 = bf16[1,80,256]{2,1,0:T(8,128)(2,1)S(1)} collective-permute-done((bf16[1,80,256]{2,1,0:T(8,128)(2,1)S(1)}, bf16[1,80,256]{2,1,0:T(8,128)(2,1)S(1)}, u32[]{:S(2)}, u32[]{:S(2)}) %collective-permute-start.27) | collective-permute-done | bytes 40992 | tf_op jit(solution)/shard_map/ppermute | solution.py:361
  455.6 5.9 collective-permute-done.32
  462.7 6.9 collective-permute-done.31
  493.9 8.8 fusion.275
  502.8 5.8 exponential_reduce_fusion
  513.8 7.0 all-to-all-done.7
  524.8 6.9 all-to-all-done.8
  533.8 26.2 %shard_map.269 = (bf16[2560,992]{1,0:T(8,128)(2,1)}, f32[1,992]{1,0:T(1,128)}, f32[1,992]{1,0:T(1,128)}) custom-call(s32[3]{0:T(128)} %pad_add_fusion.facts, f32[2560,992]{1,0:T(8,128)} %get-tuple-element.708.logits_ref, bf16[32,80,992]{2,1,0:T(8,128)(2,1)} %all-to-all-done.6.source_ref, f32[2560,4]{1,0:T(8,128)} %copy.338.rows_ref), custom_call_target="tpu_custom_call" | custom-call | tf_op jit(solution)/shard_map/pallas_call | solution.py:621
  565.0 8.5 collective-permute-done.42
  580.2 7.2 fusion.284
  587.4 6.6 collective-permute-done.45
  594.1 7.5 collective-permute-done.44
  629.6 6.0 collective-permute-done.54
  646.9 11.0 convert_reduce_fusion
  683.9 17.5 %shard_map.270 = (f32[2,2,2,2,2,352,128]{6,5,4,3,2,1,0:T(8,128)}, f32[2,2,2,2,2,336,128]{6,5,4,3,2,1,0:T(8,128)}, f32[2,2,2,2,2,336,128]{6,5,4,3,2,1,0:T(8,128)}) custom-call(s32[2]{0:T(128)} %pad_add_fusion.1.here, bf16[1024,1024]{1,0:T(8,128)(2,1)} %copy.345.up_rows, bf16[1024,1024]{1,0:T(8,128)(2,1)} %copy.346.down_rows, ...), custom_call_target="tpu_custom_call" | custom-call | tf_op jit(solution)/shard_map/pallas_call | solution.py:496
  712.1 8.2 fusion.86
  724.2 19.6 %shard_map.271 = (bf16[512,1024]{1,0:T(8,128)(2,1)}, bf16[512,1024]{1,0:T(8,128)(2,1)}, bf16[512,1024]{1,0:T(8,128)(2,1)}) custom-call(bf16[512,1024]{1,0:T(8,128)(2,1)} %add_convert_fusion.3.q_ref, bf16[512,1024]{1,0:T(8,128)(2,1)} %convolution_convert_fusion.1.k_ref, bf16[512,1024]{1,0:T(8,128)(2,1)} %add_convert_fusion.2.v_ref, ...), custom_call_target="tpu_custom_call" | custom-call | tf_op jit(solution)/shard_map/pallas_call | solution.py:157
  791.9 10.7 shard_map.272
  845.4 14.1 collective-permute-done.65
  870.4 8.0 collective-permute-done.68
  892.0 19.5 %collective-permute-done.79 = f32[2,336,128]{2,1,0:T(8,128)S(1)} collective-permute-done((f32[2,336,128]{2,1,0:T(8,128)S(1)}, f32[2,336,128]{2,1,0:T(8,128)S(1)}, u32[]{:S(2)}, u32[]{:S(2)}) %collective-permute-start.79) | collective-permute-done | bytes 344096 | tf_op jit(solution)/shard_map/ppermute | solution.py:361
  912.6 6.3 collective-permute-done.78
  919.6 6.8 collective-permute-done.77
  931.7 26.8 %collective-permute-done.71 = f32[2,2,32,256]{3,2,0,1:T(8,128)S(1)} collective-permute-done((f32[2,2,32,256]{3,2,0,1:T(8,128)S(1)}, f32[2,2,32,256]{3,2,0,1:T(8,128)S(1)}, u32[]{:S(2)}, u32[]{:S(2)}) %collective-permute-start.71) | collective-permute-done | bytes 131104 | tf_op jit(solution)/shard_map/ppermute | solution.py:361
  965.5 24.5 %collective-permute-done.84 = f32[2,32,256]{2,1,0:T(8,128)S(1)} collective-permute-done((f32[2,32,256]{2,1,0:T(8,128)S(1)}, f32[2,32,256]{2,1,0:T(8,128)S(1)}, u32[]{:S(2)}, u32[]{:S(2)}) %collective-permute-start.84) | collective-permute-done | bytes 65568 | tf_op jit(solution)/shard_map/ppermute | solution.py:361
  1032.2 84.8 %collective-permute-done.94 = f32[1,32,256]{2,1,0:T(8,128)S(1)} collective-permute-done((f32[1,32,256]{2,1,0:T(8,128)S(1)}, f32[1,32,256]{2,1,0:T(8,128)S(1)}, u32[]{:S(2)}, u32[]{:S(2)}) %collective-permute-start.94) | collective-permute-done | bytes 32800 | tf_op jit(solution)/shard_map/ppermute | solution.py:361
  1146.1 8.3 collective-permute-done.111
  1190.9 7.1 fusion.65
  1198.1 6.3 add_add_fusion
  1217.4 6.4 all-to-all-done.10
  1230.1 8.0 collective-permute-done.115
  1245.1 13.0 collective-permute-done.119
  1266.1 7.3 divide_subtract_fusion
  1278.4 10.5 collective-permute-done.120
  1304.2 6.6 collective-permute-done.126
  1327.2 7.3 bitcast_add_fusion.5
  1359.8 11.5 fusion.25
  1372.1 6.3 fusion.69
  (982 shorter events, 657.3 us)
Async XLA Ops:
  7.2 196.7 %all-gather.5.cloned.1.call-start = ((), (), s32[]{:S(2)}) async-start(), calls=%async_computation.11 | async-start | bytes 11083776 | tf_op jit(solution)/shard_map/all_gather | solution.py:807
  10.9 248.1 %all-gather.7.cloned.1.call-start = ((), (), s32[]{:S(2)}) async-start(), calls=%async_computation.12 | async-start | bytes 17301504 | tf_op jit(solution)/shard_map/all_gather | solution.py:816
  20.9 29.2 %collective-permute-start = (bf16[16,32,1024]{2,1,0:T(8,128)(2,1)S(1)}, bf16[16,32,1024]{2,1,0:T(8,128)(2,1)}, u32[]{:S(2)}, u32[]{:S(2)}) collective-permute-start(bf16[16,32,1024]{2,1,0:T(8,128)(2,1)S(1)} %dynamic-slice_bitcast_fusion.2), channel_id=1, source_target_pairs={{0,1},{1,0},{2,3},{3,2},{4,5},{5,4},{6,7},{7,6},{8,9},{9,8},{10,11... | collective-permute-start | bytes 3145736 | tf_op jit(solution)/shard_map/ppermute | solution.py:361
  119.0 80.0 %all-to-all-start.5 = ((bf16[32,32,1024]{2,1,0:T(8,128)(2,1)}), bf16[32,32,1024]{2,1,0:T(8,128)(2,1)S(1)}, u32[]{:S(2)}, u32[]{:S(2)}) async-start(bf16[32,32,1024]{2,1,0:T(8,128)(2,1)} %bitcast.17), calls=%async_computation.5 | async-start | bytes 4194304 | tf_op jit(solution)/shard_map/all_to_all | solution.py:333
  124.7 54.8 %collective-permute-start.14 = (bf16[2,32,384]{2,1,0:T(8,128)(2,1)S(1)}, bf16[2,32,384]{2,1,0:T(8,128)(2,1)S(1)}, u32[]{:S(2)}, u32[]{:S(2)}) collective-permute-start(bf16[2,32,384]{2,1,0:T(8,128)(2,1)S(1)} %pad_maximum_fusion.73), channel_id=1, source_target_pairs={{0,8},{4,12},{8,0},{12,4},{16,24},{20,28},{24,16},{28,20},{1,9},{5... | collective-permute-start | bytes 147464 | tf_op jit(solution)/shard_map/ppermute | solution.py:361
  126.3 54.5 %collective-permute-start.18 = (bf16[2,32,384]{2,1,0:T(8,128)(2,1)S(1)}, bf16[2,32,384]{2,1,0:T(8,128)(2,1)S(1)}, u32[]{:S(2)}, u32[]{:S(2)}) collective-permute-start(bf16[2,32,384]{2,1,0:T(8,128)(2,1)S(1)} %pad_maximum_fusion.74), channel_id=1, source_target_pairs={{0,2},{2,0},{1,3},{3,1},{4,6},{6,4},{5,7},{7,5},{8,10},{10,8},{9,1... | collective-permute-start | bytes 147464 | tf_op jit(solution)/shard_map/ppermute | solution.py:361
  133.6 49.8 %collective-permute-start.23 = (bf16[2,2,32,256]{3,2,1,0:T(8,128)(2,1)S(1)}, bf16[2,2,32,256]{3,2,1,0:T(8,128)(2,1)S(1)}, u32[]{:S(2)}, u32[]{:S(2)}) collective-permute-start(bf16[2,2,32,256]{3,2,1,0:T(8,128)(2,1)S(1)} %pad_maximum_fusion.71), channel_id=1, source_target_pairs={{0,2},{2,0},{1,3},{3,1},{4,6},{6,4},{5,7},{7,5},{8,10},{10,8},{9,1... | collective-permute-start | bytes 196616 | tf_op jit(solution)/shard_map/ppermute | solution.py:361
  223.7 246.9 %collective-permute-start.39 = (bf16[1024,512]{0,1:T(8,128)(2,1)}, bf16[1024,512]{0,1:T(8,128)(2,1)}, u32[]{:S(2)}, u32[]{:S(2)}) collective-permute-start(bf16[1024,512]{0,1:T(8,128)(2,1)} %fusion.348), channel_id=1, source_target_pairs={{0,1},{1,0},{2,3},{3,2},{4,5},{5,4},{6,7},{7,6},{8,9},{9,8},{10,11... | collective-permute-start | bytes 3145736 | tf_op jit(solution)/shard_map/ppermute | solution.py:361
  254.6 219.1 %collective-permute-start.37 = (bf16[1024,512]{0,1:T(8,128)(2,1)}, bf16[1024,512]{0,1:T(8,128)(2,1)}, u32[]{:S(2)}, u32[]{:S(2)}) collective-permute-start(bf16[1024,512]{0,1:T(8,128)(2,1)} %fusion.246), channel_id=1, source_target_pairs={{0,1},{1,0},{2,3},{3,2},{4,5},{5,4},{6,7},{7,6},{8,9},{9,8},{10,11... | collective-permute-start | bytes 3145736 | tf_op jit(solution)/shard_map/ppermute | solution.py:361
  311.7 197.1 %all-to-all-start.6 = ((bf16[32,80,992]{2,1,0:T(8,128)(2,1)}), bf16[32,80,992]{2,1,0:T(8,128)(2,1)}, u32[]{:S(2)}, u32[]{:S(2)}) async-start(bf16[32,80,992]{2,1,0:T(8,128)(2,1)} %bitcast.893), calls=%async_computation.6 | async-start | bytes 10485760 | tf_op jit(solution)/shard_map/all_to_all | solution.py:333
  321.2 117.1 %collective-permute-start.27 = (bf16[1,80,256]{2,1,0:T(8,128)(2,1)S(1)}, bf16[1,80,256]{2,1,0:T(8,128)(2,1)S(1)}, u32[]{:S(2)}, u32[]{:S(2)}) collective-permute-start(bf16[1,80,256]{2,1,0:T(8,128)(2,1)S(1)} %slice_bitcast_fusion.51), channel_id=1, source_target_pairs={{0,16},{4,20},{8,24},{12,28},{16,0},{20,4},{24,8},{28,12},{1,17},{... | collective-permute-start | bytes 122888 | tf_op jit(solution)/shard_map/ppermute | solution.py:361
  324.1 115.6 %collective-permute-start.26 = (bf16[1,80,384]{2,1,0:T(8,128)(2,1)S(1)}, bf16[1,80,384]{2,1,0:T(8,128)(2,1)S(1)}, u32[]{:S(2)}, u32[]{:S(2)}) collective-permute-start(bf16[1,80,384]{2,1,0:T(8,128)(2,1)S(1)} %get-tuple-element.666), channel_id=1, source_target_pairs={{0,16},{4,20},{8,24},{12,28},{16,0},{20,4},{24,8},{28,12},{1,17},{... | collective-permute-start | bytes 184328 | tf_op jit(solution)/shard_map/ppermute | solution.py:361
  324.3 116.1 %collective-permute-start.25 = (bf16[1,80,384]{2,1,0:T(8,128)(2,1)S(1)}, bf16[1,80,384]{2,1,0:T(8,128)(2,1)S(1)}, u32[]{:S(2)}, u32[]{:S(2)}) collective-permute-start(bf16[1,80,384]{2,1,0:T(8,128)(2,1)S(1)} %get-tuple-element.667), channel_id=1, source_target_pairs={{0,16},{4,20},{8,24},{12,28},{16,0},{20,4},{24,8},{28,12},{1,17},{... | collective-permute-start | bytes 184328 | tf_op jit(solution)/shard_map/ppermute | solution.py:361
  444.1 40.0 %collective-permute-start.38 = (bf16[512,2048]{1,0:T(8,128)(2,1)S(1)}, bf16[512,2048]{1,0:T(8,128)(2,1)S(1)}, u32[]{:S(2)}, u32[]{:S(2)}) collective-permute-start(bf16[512,2048]{1,0:T(8,128)(2,1)S(1)} %get-tuple-element.624), channel_id=1, source_target_pairs={{0,1},{1,0},{2,3},{3,2},{4,5},{5,4},{6,7},{7,6},{8,9},{9,8},{10,11... | collective-permute-start | bytes 6291464 | tf_op jit(solution)/shard_map/ppermute | solution.py:361
  705.1 61.9 %collective-permute-start.59 = (f32[2,2,2,2,336,128]{5,4,3,2,1,0:T(8,128)}, f32[2,2,2,2,336,128]{5,4,3,2,1,0:T(8,128)}, u32[]{:S(2)}, u32[]{:S(2)}) collective-permute-start(f32[2,2,2,2,336,128]{5,4,3,2,1,0:T(8,128)} %slice_bitcast_fusion.1), channel_id=1, source_target_pairs={{0,8},{4,12},{8,0},{12,4},{16,24},{20,28},{24,16},{28,20},{1,9},{5... | collective-permute-start | bytes 8257544 | tf_op jit(solution)/shard_map/ppermute | solution.py:361
  708.8 61.9 %collective-permute-start.58 = (f32[2,2,2,2,336,128]{5,4,3,2,1,0:T(8,128)}, f32[2,2,2,2,336,128]{5,4,3,2,1,0:T(8,128)}, u32[]{:S(2)}, u32[]{:S(2)}) collective-permute-start(f32[2,2,2,2,336,128]{5,4,3,2,1,0:T(8,128)} %slice_bitcast_fusion.2), channel_id=1, source_target_pairs={{0,4},{4,0},{8,12},{12,8},{16,20},{20,16},{24,28},{28,24},{1,5},{5... | collective-permute-start | bytes 8257544 | tf_op jit(solution)/shard_map/ppermute | solution.py:361
  711.2 64.4 %collective-permute-start.57 = (f32[2,2,2,2,352,128]{5,4,3,2,1,0:T(8,128)}, f32[2,2,2,2,352,128]{5,4,3,2,1,0:T(8,128)}, u32[]{:S(2)}, u32[]{:S(2)}) collective-permute-start(f32[2,2,2,2,352,128]{5,4,3,2,1,0:T(8,128)} %slice_bitcast_fusion), channel_id=1, source_target_pairs={{0,2},{2,0},{1,3},{3,1},{4,6},{6,4},{5,7},{7,5},{8,10},{10,8},{9,1... | collective-permute-start | bytes 8650760 | tf_op jit(solution)/shard_map/ppermute | solution.py:361
  779.0 31.3 %collective-permute-start.62 = (f32[2,2,2,336,128]{4,3,2,1,0:T(8,128)}, f32[2,2,2,336,128]{4,3,2,1,0:T(8,128)}, u32[]{:S(2)}, u32[]{:S(2)}) collective-permute-start(f32[2,2,2,336,128]{4,3,2,1,0:T(8,128)} %slice_bitcast_fusion.10), channel_id=1, source_target_pairs={{0,2},{2,0},{1,3},{3,1},{4,6},{6,4},{5,7},{7,5},{8,10},{10,8},{9,1... | collective-permute-start | bytes 4128776 | tf_op jit(solution)/shard_map/ppermute | solution.py:361
  780.5 33.4 %collective-permute-start.61 = (f32[2,2,2,336,128]{4,3,2,1,0:T(8,128)}, f32[2,2,2,336,128]{4,3,2,1,0:T(8,128)}, u32[]{:S(2)}, u32[]{:S(2)}) collective-permute-start(f32[2,2,2,336,128]{4,3,2,1,0:T(8,128)} %slice_bitcast_fusion.11), channel_id=1, source_target_pairs={{0,8},{4,12},{8,0},{12,4},{16,24},{20,28},{24,16},{28,20},{1,9},{5... | collective-permute-start | bytes 4128776 | tf_op jit(solution)/shard_map/ppermute | solution.py:361
  783.5 34.8 %collective-permute-start.60 = (f32[2,2,2,352,128]{4,3,2,1,0:T(8,128)}, f32[2,2,2,352,128]{4,3,2,1,0:T(8,128)}, u32[]{:S(2)}, u32[]{:S(2)}) collective-permute-start(f32[2,2,2,352,128]{4,3,2,1,0:T(8,128)} %slice_bitcast_fusion.5), channel_id=1, source_target_pairs={{0,4},{4,0},{8,12},{12,8},{16,20},{20,16},{24,28},{28,24},{1,5},{5... | collective-permute-start | bytes 4325384 | tf_op jit(solution)/shard_map/ppermute | solution.py:361
  805.3 73.5 %collective-permute-start.76 = (f32[2,2,2,1,336,128]{5,4,2,1,0,3:T(8,128)}, f32[2,2,2,1,336,128]{5,4,2,1,0,3:T(8,128)}, u32[]{:S(2)}, u32[]{:S(2)}) collective-permute-start(f32[2,2,2,1,336,128]{5,4,2,1,0,3:T(8,128)} %slice_bitcast_fusion.8), channel_id=1, source_target_pairs={{0,8},{4,12},{8,0},{12,4},{16,24},{20,28},{24,16},{28,20},{1,9},{5... | collective-permute-start | bytes 4128776 | tf_op jit(solution)/shard_map/ppermute | solution.py:361
  808.2 75.0 %collective-permute-start.75 = (f32[2,2,2,1,336,128]{5,4,2,1,0,3:T(8,128)}, f32[2,2,2,1,336,128]{5,4,2,1,0,3:T(8,128)}, u32[]{:S(2)}, u32[]{:S(2)}) collective-permute-start(f32[2,2,2,1,336,128]{5,4,2,1,0,3:T(8,128)} %slice_bitcast_fusion.9), channel_id=1, source_target_pairs={{0,4},{4,0},{8,12},{12,8},{16,20},{20,16},{24,28},{28,24},{1,5},{5... | collective-permute-start | bytes 4128776 | tf_op jit(solution)/shard_map/ppermute | solution.py:361
  827.7 31.8 %collective-permute-start.65 = (f32[2,2,336,128]{3,2,1,0:T(8,128)}, f32[2,2,336,128]{3,2,1,0:T(8,128)}, u32[]{:S(2)}, u32[]{:S(2)}) collective-permute-start(f32[2,2,336,128]{3,2,1,0:T(8,128)} %slice_bitcast_fusion.19), channel_id=1, source_target_pairs={{0,4},{4,0},{8,12},{12,8},{16,20},{20,16},{24,28},{28,24},{1,5},{5... | collective-permute-start | bytes 2064392 | tf_op jit(solution)/shard_map/ppermute | solution.py:361
  831.4 31.1 %collective-permute-start.64 = (f32[2,2,336,128]{3,2,1,0:T(8,128)}, f32[2,2,336,128]{3,2,1,0:T(8,128)}, u32[]{:S(2)}, u32[]{:S(2)}) collective-permute-start(f32[2,2,336,128]{3,2,1,0:T(8,128)} %slice_bitcast_fusion.20), channel_id=1, source_target_pairs={{0,2},{2,0},{1,3},{3,1},{4,6},{6,4},{5,7},{7,5},{8,10},{10,8},{9,1... | collective-permute-start | bytes 2064392 | tf_op jit(solution)/shard_map/ppermute | solution.py:361
  833.8 29.9 %collective-permute-start.63 = (f32[2,2,352,128]{3,2,1,0:T(8,128)}, f32[2,2,352,128]{3,2,1,0:T(8,128)}, u32[]{:S(2)}, u32[]{:S(2)}) collective-permute-start(f32[2,2,352,128]{3,2,1,0:T(8,128)} %slice_bitcast_fusion.14), channel_id=1, source_target_pairs={{0,8},{4,12},{8,0},{12,4},{16,24},{20,28},{24,16},{28,20},{1,9},{5... | collective-permute-start | bytes 2162696 | tf_op jit(solution)/shard_map/ppermute | solution.py:361
  859.6 30.7 %collective-permute-start.74 = (f32[2,2,2,1,352,128]{5,4,2,1,0,3:T(8,128)S(1)}, f32[2,2,2,1,352,128]{5,4,2,1,0,3:T(8,128)S(1)}, u32[]{:S(2)}, u32[]{:S(2)}) collective-permute-start(f32[2,2,2,1,352,128]{5,4,2,1,0,3:T(8,128)S(1)} %copy-done.59), channel_id=1, source_target_pairs={{0,2},{2,0},{1,3},{3,1},{4,6},{6,4},{5,7},{7,5},{8,10},{10,8},{9,1... | collective-permute-start | bytes 4325384 | tf_op jit(solution)/shard_map/ppermute | solution.py:361
  862.4 64.9 %collective-permute-start.80 = (f32[2,2,2,2,288,128]{5,4,3,2,1,0:T(8,128)S(1)}, f32[2,2,2,2,288,128]{5,4,3,2,1,0:T(8,128)S(1)}, u32[]{:S(2)}, u32[]{:S(2)}) collective-permute-start(f32[2,2,2,2,288,128]{5,4,3,2,1,0:T(8,128)S(1)} %dynamic-slice_bitcast_fusion), channel_id=1, source_target_pairs={{0,1},{1,0},{2,3},{3,2},{4,5},{5,4},{6,7},{7,6},{8,9},{9,8},{10,11... | collective-permute-start | bytes 7077896 | tf_op jit(solution)/shard_map/ppermute | solution.py:361
  878.4 33.1 %collective-permute-start.79 = (f32[2,336,128]{2,1,0:T(8,128)S(1)}, f32[2,336,128]{2,1,0:T(8,128)S(1)}, u32[]{:S(2)}, u32[]{:S(2)}) collective-permute-start(f32[2,336,128]{2,1,0:T(8,128)S(1)} %slice_bitcast_fusion.30), channel_id=1, source_target_pairs={{0,16},{4,20},{8,24},{12,28},{16,0},{20,4},{24,8},{28,12},{1,17},{... | collective-permute-start | bytes 1032200 | tf_op jit(solution)/shard_map/ppermute | solution.py:361
  878.8 40.0 %collective-permute-start.78 = (f32[2,336,128]{2,1,0:T(8,128)S(1)}, f32[2,336,128]{2,1,0:T(8,128)S(1)}, u32[]{:S(2)}, u32[]{:S(2)}) collective-permute-start(f32[2,336,128]{2,1,0:T(8,128)S(1)} %slice_bitcast_fusion.31), channel_id=1, source_target_pairs={{0,16},{4,20},{8,24},{12,28},{16,0},{20,4},{24,8},{28,12},{1,17},{... | collective-permute-start | bytes 1032200 | tf_op jit(solution)/shard_map/ppermute | solution.py:361
  883.2 43.3 %collective-permute-start.77 = (f32[2,352,128]{2,1,0:T(8,128)S(1)}, f32[2,352,128]{2,1,0:T(8,128)S(1)}, u32[]{:S(2)}, u32[]{:S(2)}) collective-permute-start(f32[2,352,128]{2,1,0:T(8,128)S(1)} %slice_bitcast_fusion.25), channel_id=1, source_target_pairs={{0,16},{4,20},{8,24},{12,28},{16,0},{20,4},{24,8},{28,12},{1,17},{... | collective-permute-start | bytes 1081352 | tf_op jit(solution)/shard_map/ppermute | solution.py:361
  890.2 37.0 %collective-permute-start.67 = (f32[2,2,2,32,384]{4,3,2,1,0:T(8,128)S(1)}, f32[2,2,2,32,384]{4,3,2,1,0:T(8,128)S(1)}, u32[]{:S(2)}, u32[]{:S(2)}) collective-permute-start(f32[2,2,2,32,384]{4,3,2,1,0:T(8,128)S(1)} %dynamic-slice_bitcast_fusion.4), channel_id=1, source_target_pairs={{0,4},{4,0},{8,12},{12,8},{16,20},{20,16},{24,28},{28,24},{1,5},{5... | collective-permute-start | bytes 1179656 | tf_op jit(solution)/shard_map/ppermute | solution.py:361
  927.7 30.9 %collective-permute-start.81 = (f32[2,2,2,288,128]{4,3,2,1,0:T(8,128)S(1)}, f32[2,2,2,288,128]{4,3,2,1,0:T(8,128)S(1)}, u32[]{:S(2)}, u32[]{:S(2)}) collective-permute-start(f32[2,2,2,288,128]{4,3,2,1,0:T(8,128)S(1)} %dynamic-slice_bitcast_fusion.1), channel_id=1, source_target_pairs={{0,2},{2,0},{1,3},{3,1},{4,6},{6,4},{5,7},{7,5},{8,10},{10,8},{9,1... | collective-permute-start | bytes 3538952 | tf_op jit(solution)/shard_map/ppermute | solution.py:361
  928.2 30.2 %collective-permute-start.71 = (f32[2,2,32,256]{3,2,0,1:T(8,128)S(1)}, f32[2,2,32,256]{3,2,0,1:T(8,128)S(1)}, u32[]{:S(2)}, u32[]{:S(2)}) collective-permute-start(f32[2,2,32,256]{3,2,0,1:T(8,128)S(1)} %bitcast.996), channel_id=1, source_target_pairs={{0,2},{2,0},{1,3},{3,1},{4,6},{6,4},{5,7},{7,5},{8,10},{10,8},{9,1... | collective-permute-start | bytes 393224 | tf_op jit(solution)/shard_map/ppermute | solution.py:361
  930.0 28.5 %collective-permute-start.70 = (f32[2,2,32,384]{3,2,0,1:T(8,128)S(1)}, f32[2,2,32,384]{3,2,0,1:T(8,128)S(1)}, u32[]{:S(2)}, u32[]{:S(2)}) collective-permute-start(f32[2,2,32,384]{3,2,0,1:T(8,128)S(1)} %bitcast.994), channel_id=1, source_target_pairs={{0,8},{4,12},{8,0},{12,4},{16,24},{20,28},{24,16},{28,20},{1,9},{5... | collective-permute-start | bytes 589832 | tf_op jit(solution)/shard_map/ppermute | solution.py:361
  930.1 28.4 %collective-permute-start.69 = (f32[2,2,32,384]{3,2,0,1:T(8,128)S(1)}, f32[2,2,32,384]{3,2,0,1:T(8,128)S(1)}, u32[]{:S(2)}, u32[]{:S(2)}) collective-permute-start(f32[2,2,32,384]{3,2,0,1:T(8,128)S(1)} %bitcast.995), channel_id=1, source_target_pairs={{0,4},{4,0},{8,12},{12,8},{16,20},{20,16},{24,28},{28,24},{1,5},{5... | collective-permute-start | bytes 589832 | tf_op jit(solution)/shard_map/ppermute | solution.py:361
  958.8 56.4 %collective-permute-start.91 = (f32[2,2,288,128]{3,2,1,0:T(8,128)S(1)}, f32[2,2,288,128]{3,2,1,0:T(8,128)S(1)}, u32[]{:S(2)}, u32[]{:S(2)}) collective-permute-start(f32[2,2,288,128]{3,2,1,0:T(8,128)S(1)} %dynamic-slice_bitcast_fusion.3), channel_id=1, source_target_pairs={{0,4},{4,0},{8,12},{12,8},{16,20},{20,16},{24,28},{28,24},{1,5},{5... | collective-permute-start | bytes 1769480 | tf_op jit(solution)/shard_map/ppermute | solution.py:361
  961.2 58.9 %collective-permute-start.90 = (f32[2,2,1,336,128]{4,3,1,0,2:T(8,128)}, f32[2,2,1,336,128]{4,3,1,0,2:T(8,128)}, u32[]{:S(2)}, u32[]{:S(2)}) collective-permute-start(f32[2,2,1,336,128]{4,3,1,0,2:T(8,128)} %slice_bitcast_fusion.17), channel_id=1, source_target_pairs={{0,2},{2,0},{1,3},{3,1},{4,6},{6,4},{5,7},{7,5},{8,10},{10,8},{9,1... | collective-permute-start | bytes 2064392 | tf_op jit(solution)/shard_map/ppermute | solution.py:361
  962.6 59.0 %collective-permute-start.89 = (f32[2,2,1,336,128]{4,3,1,0,2:T(8,128)}, f32[2,2,1,336,128]{4,3,1,0,2:T(8,128)}, u32[]{:S(2)}, u32[]{:S(2)}) collective-permute-start(f32[2,2,1,336,128]{4,3,1,0,2:T(8,128)} %slice_bitcast_fusion.18), channel_id=1, source_target_pairs={{0,8},{4,12},{8,0},{12,4},{16,24},{20,28},{24,16},{28,20},{1,9},{5... | collective-permute-start | bytes 2064392 | tf_op jit(solution)/shard_map/ppermute | solution.py:361
  963.5 59.5 %collective-permute-start.88 = (f32[2,2,1,352,128]{4,3,1,0,2:T(8,128)}, f32[2,2,1,352,128]{4,3,1,0,2:T(8,128)}, u32[]{:S(2)}, u32[]{:S(2)}) collective-permute-start(f32[2,2,1,352,128]{4,3,1,0,2:T(8,128)} %slice_bitcast_fusion.13), channel_id=1, source_target_pairs={{0,4},{4,0},{8,12},{12,8},{16,20},{20,16},{24,28},{28,24},{1,5},{5... | collective-permute-start | bytes 2162696 | tf_op jit(solution)/shard_map/ppermute | solution.py:361
  1016.0 174.8 %all-to-all-start.9 = ((f32[32,32,1024]{2,1,0:T(8,128)}), f32[32,32,1024]{2,1,0:T(8,128)}, u32[]{:S(2)}, u32[]{:S(2)}) async-start(f32[32,32,1024]{2,1,0:T(8,128)} %bitcast.931), calls=%async_computation.9 | async-start | bytes 8388608 | tf_op jit(solution)/shard_map/all_to_all | solution.py:333
  1024.2 111.4 %collective-permute-start.101 = (f32[2,288,128]{2,1,0:T(8,128)S(1)}, f32[2,288,128]{2,1,0:T(8,128)S(1)}, u32[]{:S(2)}, u32[]{:S(2)}) collective-permute-start(f32[2,288,128]{2,1,0:T(8,128)S(1)} %dynamic-slice_bitcast_fusion.6), channel_id=1, source_target_pairs={{0,8},{4,12},{8,0},{12,4},{16,24},{20,28},{24,16},{28,20},{1,9},{5... | collective-permute-start | bytes 884744 | tf_op jit(solution)/shard_map/ppermute | solution.py:361
  1026.1 109.6 %collective-permute-start.100 = (f32[2,1,336,128]{3,2,0,1:T(8,128)S(1)}, f32[2,1,336,128]{3,2,0,1:T(8,128)S(1)}, u32[]{:S(2)}, u32[]{:S(2)}) collective-permute-start(f32[2,1,336,128]{3,2,0,1:T(8,128)S(1)} %slice_bitcast_fusion.28), channel_id=1, source_target_pairs={{0,4},{4,0},{8,12},{12,8},{16,20},{20,16},{24,28},{28,24},{1,5},{5... | collective-permute-start | bytes 1032200 | tf_op jit(solution)/shard_map/ppermute | solution.py:361
  1027.7 89.3 %collective-permute-start.94 = (f32[1,32,256]{2,1,0:T(8,128)S(1)}, f32[1,32,256]{2,1,0:T(8,128)S(1)}, u32[]{:S(2)}, u32[]{:S(2)}) collective-permute-start(f32[1,32,256]{2,1,0:T(8,128)S(1)} %copy-done.87), channel_id=1, source_target_pairs={{0,16},{4,20},{8,24},{12,28},{16,0},{20,4},{24,8},{28,12},{1,17},{... | collective-permute-start | bytes 98312 | tf_op jit(solution)/shard_map/ppermute | solution.py:361
  1030.2 105.5 %collective-permute-start.99 = (f32[2,1,336,128]{3,2,0,1:T(8,128)S(1)}, f32[2,1,336,128]{3,2,0,1:T(8,128)S(1)}, u32[]{:S(2)}, u32[]{:S(2)}) collective-permute-start(f32[2,1,336,128]{3,2,0,1:T(8,128)S(1)} %slice_bitcast_fusion.29), channel_id=1, source_target_pairs={{0,2},{2,0},{1,3},{3,1},{4,6},{6,4},{5,7},{7,5},{8,10},{10,8},{9,1... | collective-permute-start | bytes 1032200 | tf_op jit(solution)/shard_map/ppermute | solution.py:361
  1031.7 85.8 %collective-permute-start.93 = (f32[1,32,384]{2,1,0:T(8,128)S(1)}, f32[1,32,384]{2,1,0:T(8,128)S(1)}, u32[]{:S(2)}, u32[]{:S(2)}) collective-permute-start(f32[1,32,384]{2,1,0:T(8,128)S(1)} %copy-done.79), channel_id=1, source_target_pairs={{0,16},{4,20},{8,24},{12,28},{16,0},{20,4},{24,8},{28,12},{1,17},{... | collective-permute-start | bytes 147464 | tf_op jit(solution)/shard_map/ppermute | solution.py:361
  1323.0 35.0 %collective-permute-start.132 = (bf16[8,352,256]{2,1,0:T(8,128)(2,1)S(1)}, bf16[8,352,256]{2,1,0:T(8,128)(2,1)}, u32[]{:S(2)}, u32[]{:S(2)}) collective-permute-start(bf16[8,352,256]{2,1,0:T(8,128)(2,1)S(1)} %pad_maximum_fusion.15), channel_id=1, source_target_pairs={{0,2},{2,0},{1,3},{3,1},{4,6},{6,4},{5,7},{7,5},{8,10},{10,8},{9,1... | collective-permute-start | bytes 4325384 | tf_op jit(solution)/shard_map/ppermute | solution.py:361
  1324.6 29.0 %collective-permute-start.133 = (bf16[8,336,256]{2,1,0:T(8,128)(2,1)}, bf16[8,336,256]{2,1,0:T(8,128)(2,1)}, u32[]{:S(2)}, u32[]{:S(2)}) collective-permute-start(bf16[8,336,256]{2,1,0:T(8,128)(2,1)} %pad_maximum_fusion.16), channel_id=1, source_target_pairs={{0,4},{4,0},{8,12},{12,8},{16,20},{20,16},{24,28},{28,24},{1,5},{5... | collective-permute-start | bytes 4128776 | tf_op jit(solution)/shard_map/ppermute | solution.py:361
  1325.1 30.7 %collective-permute-start.134 = (bf16[8,336,256]{2,1,0:T(8,128)(2,1)}, bf16[8,336,256]{2,1,0:T(8,128)(2,1)}, u32[]{:S(2)}, u32[]{:S(2)}) collective-permute-start(bf16[8,336,256]{2,1,0:T(8,128)(2,1)} %pad_maximum_fusion.17), channel_id=1, source_target_pairs={{0,8},{4,12},{8,0},{12,4},{16,24},{20,28},{24,16},{28,20},{1,9},{5... | collective-permute-start | bytes 4128776 | tf_op jit(solution)/shard_map/ppermute | solution.py:361
  (229 other events, 3744.8 us)
Sparse Core Ops, SparseCore 0:
  11.4 92.5 all-gather.4
  107.4 144.6 all-gather.6

commit v6 on v5

--- a/solution.py
+++ b/solution.py
@@ -1022,37 +1022,25 @@
     )
     other_part = scatter_flat(front, grad_head_w.reshape(-1, lanes), size, devices)
 
-    place_grad = flat_embed.reshape(group, per_place, D)
+    place_grad = lax.psum(flat_embed, ("wide", "pair"))
     sent = add_rows(now, flat_embed, devices * slots)
     arrived = swap_all(sent.reshape(devices, slots, D))
-    place_parts = route_parts(place_grad.reshape(group, per_place, D), wide_count)
     steps = len(routes(wide_count)[0])
-
-    def place_step(parts, turn):
-        if turn < steps:
-            parts = route_step(parts, wide_count, turn, False)
-            if turn + 1 == steps:
-                parts = gather_start(jnp.concatenate(parts, axis=-1), 1, lanes)
-            return parts
-        return gather_step(parts, wide_count, turn - steps)
 
     for step in range(steps):
         if step + 3 < steps:
             ffn_parts = reduce_step(ffn_parts, wide_count, step + 3)
-        attn_parts = reduce_step(attn_parts, wide_count, step)
-        other_part = other_step(other_part, wide_count, step)
-        (place_parts,) = lockstep(place_step(place_parts, 2 * step))
-        place_parts, attn_parts, ffn_parts, (other_part,) = lockstep(
-            place_step(place_parts, 2 * step + 1), attn_parts, ffn_parts, [other_part]
+        attn_parts, ffn_parts, (other_part,) = lockstep(
+            reduce_step(attn_parts, wide_count, step),
+            ffn_parts,
+            [other_step(other_part, wide_count, step)],
         )
+    place_grad, attn_parts = tied(place_grad, attn_parts)
     ffn_grad = jnp.concatenate(ffn_parts, axis=1)
     attn_grad = jnp.concatenate(attn_parts, axis=1)
     other_grad = own_share(other_part, size, device)
-    place_grad = gather_end(place_parts, wide_count, 1)
-    place_grad = jnp.concatenate([place_grad, exchange(place_grad, side_bit)])
-    turn = jnp.arange(devices, dtype=jnp.int32)[:, None]
-    place_ids = (turn // group ^ side) * WINDOW + (turn % group ^ here) * per_place
-    place_ids = place_ids + jnp.arange(per_place, dtype=jnp.int32)[None, :]
+    place_grad = jnp.stack([place_grad, exchange(place_grad, side_bit)])
+    place_ids = (jnp.arange(2, dtype=jnp.int32)[:, None] ^ side) * WINDOW + order[None, :]
     place_ids = (V - device * owned + place_ids).reshape(-1)
     table_grad = grad_words + add_rows(asked, arrived.reshape(-1, D), owned)
     table_grad = table_grad + add_rows(place_ids, place_grad.reshape(SEQ, D), owned)

time: 1420 us -> 1340 us (0.944)
  waiting for transfers between devices: 626 us -> 566 us
  starting transfers between devices: 156 us -> 141 us
    ppermute x136 -> x112, waiting for transfers between devices: 596 us -> 538 us  [exchange(): return lax.ppermute(values, axis, steps)]
    ppermute x136 -> x112, starting transfers between devices: 125 us -> 111 us  [exchange(): return lax.ppermute(values, axis, steps)]
  transfers between devices with their start and end apart: 145 -> 122, of which waited for: 86 -> 73; matrix products, arithmetic and copies ran while one was open for 26% -> 26% of each run, Pallas kernels for 6% -> 6%
where the time goes in v6:
time: 1340 us; the launch traced here: 1330 us
  waiting for transfers between devices  566 us (42%)
  matrix products  205 us (15%)
  other arithmetic  155 us (12%)
  starting transfers between devices  141 us (11%)
  Pallas kernels  125 us (9%)
  local copies, waits for them, and re-layouts  109 us (8%)
  between operations  29.4 us (2%)
    ppermute x112, waiting for transfers between devices, exchange(): return lax.ppermute(values, axis, steps)  538 us
    ppermute x112, starting transfers between devices, exchange(): return lax.ppermute(values, axis, steps)  111 us
    dot_general x6, matrix products, project(): jnp.einsum('bsd,df->bsf', inputs, weight, preferred_element_type=jnp.floa...  49.1 us
    all_to_all x7, starting transfers between devices, swap_all(): return lax.all_to_all(blocks, axes, 0, 0, tiled=True)  30 us
    add x24, other arithmetic, reduce_step(): part[0] + exchange(part[1], route[step])  29.5 us
    pallas_call x2, Pallas kernels, weight_grads(): pl.pallas_call(kernel, grid_spec=pltpu.PrefetchScalarGridSpec(num_scalar_...  28.4 us
    all_to_all x7, waiting for transfers between devices, swap_all(): return lax.all_to_all(blocks, axes, 0, 0, tiled=True)  27.9 us
  transfers between devices with their start and end apart: 122, of which 73 were waited for; matrix products, arithmetic and copies ran while one was open for 26% of the time, Pallas kernels for 6%

profile of v6, /device:TPU:0, one launch (start us, length us, event | category | flops | bytes accessed | tf_op | source)
XLA Modules:
  0.0 1330.1 jit_solution(13054700994886831267)
XLA Ops:
  26.9 7.2 all-to-all-start.4
  35.3 5.9 all-to-all-done.4
  53.6 8.6 collective-permute-done.3
  97.6 10.5 reshape.1403
  108.1 7.8 copy.361
  134.5 47.3 %collective-permute-done.14 = bf16[2,32,384]{2,1,0:T(8,128)(2,1)S(1)} collective-permute-done((bf16[2,32,384]{2,1,0:T(8,128)(2,1)S(1)}, bf16[2,32,384]{2,1,0:T(8,128)(2,1)S(1)}, u32[]{:S(2)}, u32[]{:S(2)}) %collective-permute-start.14) | collective-permute-done | bytes 49184 | tf_op jit(solution)/shard_map/ppermute | solution.py:361
  207.8 7.9 shard_map.266
  232.4 16.5 %shard_map.267 = (bf16[512,1024]{1,0:T(8,128)(2,1)}, f32[16,512,1]{2,1,0:T(8,128)}) custom-call(bf16[512,1024]{1,0:T(8,128)(2,1)} %add_convert_fusion.3.q_ref, bf16[512,1024]{1,0:T(8,128)(2,1)} %convolution_convert_fusion.1.k_ref, bf16[512,1024]{1,0:T(8,128)(2,1)} %add_convert_fusion.2.v_ref, f32[512,512]{1,0:T(8,128)} %fusion.178.allow_ref), custom_call_target="tpu_custom_call" | custom-call | tf_op jit(solution)/shard_map/pallas_call | solution.py:140
  259.4 17.9 %shard_map.268 = (bf16[1024,4096]{1,0:T(8,128)(2,1)}, bf16[1024,4096]{1,0:T(8,128)(2,1)}) custom-call(bf16[32,2,1024,128]{3,2,1,0:T(8,128)(2,1)} %bitcast.809, bf16[32,2,1024,128]{3,2,1,0:T(8,128)(2,1)} %bitcast.810, bf16[32,2,1024,128]{3,2,1,0:T(8,128)(2,1)} %bitcast.811, bf16[32,2,1024,128]{3,2,1,0:T(8,128)(2,1)} %bitcast.812), custom_call_target="tpu_custom_call" | custom-call | tf_op jit(solution)/shard_map/pallas_call | solution.py:725
  277.3 27.9 %multiply_convert_fusion = (bf16[512,4096]{1,0:T(8,128)(2,1)S(1)}, f32[512,4096]{1,0:T(8,128)}, f32[512,4096]{1,0:T(8,128)}) fusion(f32[4096]{0:T(1024)S(1)} %bitcast.915, bf16[1024,4096]{1,0:T(8,128)(2,1)} %get-tuple-element.378, f32[512,1024]{1,0:T(8,128)} %copy-done.2, f32[1024]{0:T(1024)S(1)} %get-tuple-element.634, f32[1024]{0:T(1024)S(1)} %get-tuple-element.635, ...), kind=kOutput, calls=%fused_computation.39 | convolution fusion | flops 4436000768 | bytes 31485952 | tf_op jit(solution)/shard_map/bsd,df->bsf/dot_general | solution.py:60
  327.5 111.3 %collective-permute-done.27 = bf16[1,80,256]{2,1,0:T(8,128)(2,1)S(1)} collective-permute-done((bf16[1,80,256]{2,1,0:T(8,128)(2,1)S(1)}, bf16[1,80,256]{2,1,0:T(8,128)(2,1)S(1)}, u32[]{:S(2)}, u32[]{:S(2)}) %collective-permute-start.27) | collective-permute-done | bytes 40992 | tf_op jit(solution)/shard_map/ppermute | solution.py:361
  456.0 5.9 collective-permute-done.32
  463.1 6.9 collective-permute-done.31
  494.2 8.8 fusion.273
  514.2 7.0 all-to-all-done.7
  525.4 6.9 all-to-all-done.8
  534.4 26.2 %shard_map.269 = (bf16[2560,992]{1,0:T(8,128)(2,1)}, f32[1,992]{1,0:T(1,128)}, f32[1,992]{1,0:T(1,128)}) custom-call(s32[3]{0:T(128)} %pad_add_fusion.facts, f32[2560,992]{1,0:T(8,128)} %get-tuple-element.660.logits_ref, bf16[32,80,992]{2,1,0:T(8,128)(2,1)} %all-to-all-done.6.source_ref, f32[2560,4]{1,0:T(8,128)} %copy.302.rows_ref), custom_call_target="tpu_custom_call" | custom-call | tf_op jit(solution)/shard_map/pallas_call | solution.py:621
  565.6 8.5 collective-permute-done.42
  580.8 7.1 fusion.282
  587.9 6.7 collective-permute-done.45
  594.7 7.5 collective-permute-done.44
  630.2 6.0 collective-permute-done.54
  647.0 11.0 convert_reduce_fusion
  684.0 17.3 %shard_map.270 = (f32[2,2,2,2,2,352,128]{6,5,4,3,2,1,0:T(8,128)}, f32[2,2,2,2,2,336,128]{6,5,4,3,2,1,0:T(8,128)}, f32[2,2,2,2,2,336,128]{6,5,4,3,2,1,0:T(8,128)}) custom-call(s32[2]{0:T(128)} %pad_add_fusion.1.here, bf16[1024,1024]{1,0:T(8,128)(2,1)} %copy.309.up_rows, bf16[1024,1024]{1,0:T(8,128)(2,1)} %copy.310.down_rows, ...), custom_call_target="tpu_custom_call" | custom-call | tf_op jit(solution)/shard_map/pallas_call | solution.py:496
  712.0 8.2 fusion.86
  724.1 19.5 %shard_map.271 = (bf16[512,1024]{1,0:T(8,128)(2,1)}, bf16[512,1024]{1,0:T(8,128)(2,1)}, bf16[512,1024]{1,0:T(8,128)(2,1)}) custom-call(bf16[512,1024]{1,0:T(8,128)(2,1)} %add_convert_fusion.3.q_ref, bf16[512,1024]{1,0:T(8,128)(2,1)} %convolution_convert_fusion.1.k_ref, bf16[512,1024]{1,0:T(8,128)(2,1)} %add_convert_fusion.2.v_ref, ...), custom_call_target="tpu_custom_call" | custom-call | tf_op jit(solution)/shard_map/pallas_call | solution.py:157
  791.7 11.0 shard_map.272
  842.3 10.8 collective-permute-done.65
  878.5 12.3 collective-permute-done.69
  899.1 12.5 collective-permute-done.73
  912.4 7.7 collective-permute-done.72
  920.8 9.4 collective-permute-done.71
  941.4 44.9 %collective-permute-done.79 = f32[2,2,288,128]{3,2,1,0:T(8,128)S(1)} collective-permute-done((f32[2,2,288,128]{3,2,1,0:T(8,128)S(1)}, f32[2,2,288,128]{3,2,1,0:T(8,128)S(1)}, u32[]{:S(2)}, u32[]{:S(2)}) %collective-permute-start.79) | collective-permute-done | bytes 589856 | tf_op jit(solution)/shard_map/ppermute | solution.py:361
  989.4 36.9 %collective-permute-done.77 = f32[2,2,1,336,128]{4,3,1,0,2:T(8,128)S(1)} collective-permute-done((f32[2,2,1,336,128]{4,3,1,0,2:T(8,128)S(1)}, f32[2,2,1,336,128]{4,3,1,0,2:T(8,128)S(1)}, u32[]{:S(2)}, u32[]{:S(2)}) %collective-permute-start.77) | collective-permute-done | bytes 688160 | tf_op jit(solution)/shard_map/ppermute | solution.py:361
  1033.4 22.8 %collective-permute-done.83 = f32[2,288,128]{2,1,0:T(8,128)S(1)} collective-permute-done((f32[2,288,128]{2,1,0:T(8,128)S(1)}, f32[2,288,128]{2,1,0:T(8,128)S(1)}, u32[]{:S(2)}, u32[]{:S(2)}) %collective-permute-start.83) | collective-permute-done | bytes 294944 | tf_op jit(solution)/shard_map/ppermute | solution.py:361
  1056.3 7.4 collective-permute-done.80
  1069.9 14.2 %collective-permute-done.87 = f32[288,128]{1,0:T(8,128)S(1)} collective-permute-done((f32[288,128]{1,0:T(8,128)S(1)}, f32[288,128]{1,0:T(8,128)S(1)}, u32[]{:S(2)}, u32[]{:S(2)}) %collective-permute-start.87) | collective-permute-done | bytes 147488 | tf_op jit(solution)/shard_map/ppermute | solution.py:361
  1104.8 7.1 fusion.65
  1112.0 6.3 add_add_fusion
  1129.4 6.5 all-to-all-done.10
  1145.5 8.2 collective-permute-done.91
  1160.6 13.2 collective-permute-done.95
  1181.8 7.6 divide_subtract_fusion
  1194.3 10.5 collective-permute-done.96
  1220.1 6.6 collective-permute-done.102
  1243.1 7.3 bitcast_add_fusion.5
  1275.8 11.5 fusion.25
  1288.0 6.2 fusion.69
  (875 shorter events, 597.6 us)
Async XLA Ops:
  7.2 197.1 %all-gather.5.cloned.1.call-start = ((), (), s32[]{:S(2)}) async-start(), calls=%async_computation.12 | async-start | bytes 11083776 | tf_op jit(solution)/shard_map/all_gather | solution.py:807
  10.9 248.5 %all-gather.7.cloned.1.call-start = ((), (), s32[]{:S(2)}) async-start(), calls=%async_computation.13 | async-start | bytes 17301504 | tf_op jit(solution)/shard_map/all_gather | solution.py:816
  20.9 29.1 %collective-permute-start = (bf16[16,32,1024]{2,1,0:T(8,128)(2,1)S(1)}, bf16[16,32,1024]{2,1,0:T(8,128)(2,1)}, u32[]{:S(2)}, u32[]{:S(2)}) collective-permute-start(bf16[16,32,1024]{2,1,0:T(8,128)(2,1)S(1)} %dynamic-slice_bitcast_fusion.2), channel_id=1, source_target_pairs={{0,1},{1,0},{2,3},{3,2},{4,5},{5,4},{6,7},{7,6},{8,9},{9,8},{10,11... | collective-permute-start | bytes 3145736 | tf_op jit(solution)/shard_map/ppermute | solution.py:361
  91.9 26.9 %collective-permute-start.21 = (bf16[32,256]{1,0:T(8,128)(2,1)S(1)}, bf16[32,256]{1,0:T(8,128)(2,1)S(1)}, u32[]{:S(2)}, u32[]{:S(2)}) collective-permute-start(bf16[32,256]{1,0:T(8,128)(2,1)S(1)} %bitcast_add_fusion.49), channel_id=1, source_target_pairs={{0,16},{4,20},{8,24},{12,28},{16,0},{20,4},{24,8},{28,12},{1,17},{... | collective-permute-start | bytes 49160 | tf_op jit(solution)/shard_map/ppermute | solution.py:361
  118.8 80.5 %all-to-all-start.5 = ((bf16[32,32,1024]{2,1,0:T(8,128)(2,1)}), bf16[32,32,1024]{2,1,0:T(8,128)(2,1)S(1)}, u32[]{:S(2)}, u32[]{:S(2)}) async-start(bf16[32,32,1024]{2,1,0:T(8,128)(2,1)} %bitcast.17), calls=%async_computation.5 | async-start | bytes 4194304 | tf_op jit(solution)/shard_map/all_to_all | solution.py:333
  124.9 57.0 %collective-permute-start.14 = (bf16[2,32,384]{2,1,0:T(8,128)(2,1)S(1)}, bf16[2,32,384]{2,1,0:T(8,128)(2,1)S(1)}, u32[]{:S(2)}, u32[]{:S(2)}) collective-permute-start(bf16[2,32,384]{2,1,0:T(8,128)(2,1)S(1)} %pad_maximum_fusion.60), channel_id=1, source_target_pairs={{0,8},{4,12},{8,0},{12,4},{16,24},{20,28},{24,16},{28,20},{1,9},{5... | collective-permute-start | bytes 147464 | tf_op jit(solution)/shard_map/ppermute | solution.py:361
  126.4 55.9 %collective-permute-start.18 = (bf16[2,32,384]{2,1,0:T(8,128)(2,1)S(1)}, bf16[2,32,384]{2,1,0:T(8,128)(2,1)S(1)}, u32[]{:S(2)}, u32[]{:S(2)}) collective-permute-start(bf16[2,32,384]{2,1,0:T(8,128)(2,1)S(1)} %pad_maximum_fusion.61), channel_id=1, source_target_pairs={{0,2},{2,0},{1,3},{3,1},{4,6},{6,4},{5,7},{7,5},{8,10},{10,8},{9,1... | collective-permute-start | bytes 147464 | tf_op jit(solution)/shard_map/ppermute | solution.py:361
  133.7 51.3 %collective-permute-start.23 = (bf16[2,2,32,256]{3,2,1,0:T(8,128)(2,1)S(1)}, bf16[2,2,32,256]{3,2,1,0:T(8,128)(2,1)S(1)}, u32[]{:S(2)}, u32[]{:S(2)}) collective-permute-start(bf16[2,2,32,256]{3,2,1,0:T(8,128)(2,1)S(1)} %pad_maximum_fusion.59), channel_id=1, source_target_pairs={{0,2},{2,0},{1,3},{3,1},{4,6},{6,4},{5,7},{7,5},{8,10},{10,8},{9,1... | collective-permute-start | bytes 196616 | tf_op jit(solution)/shard_map/ppermute | solution.py:361
  224.3 246.7 %collective-permute-start.39 = (bf16[1024,512]{0,1:T(8,128)(2,1)}, bf16[1024,512]{0,1:T(8,128)(2,1)}, u32[]{:S(2)}, u32[]{:S(2)}) collective-permute-start(bf16[1024,512]{0,1:T(8,128)(2,1)} %fusion.346), channel_id=1, source_target_pairs={{0,1},{1,0},{2,3},{3,2},{4,5},{5,4},{6,7},{7,6},{8,9},{9,8},{10,11... | collective-permute-start | bytes 3145736 | tf_op jit(solution)/shard_map/ppermute | solution.py:361
  255.2 218.9 %collective-permute-start.37 = (bf16[1024,512]{0,1:T(8,128)(2,1)}, bf16[1024,512]{0,1:T(8,128)(2,1)}, u32[]{:S(2)}, u32[]{:S(2)}) collective-permute-start(bf16[1024,512]{0,1:T(8,128)(2,1)} %fusion.245), channel_id=1, source_target_pairs={{0,1},{1,0},{2,3},{3,2},{4,5},{5,4},{6,7},{7,6},{8,9},{9,8},{10,11... | collective-permute-start | bytes 3145736 | tf_op jit(solution)/shard_map/ppermute | solution.py:361
  312.1 197.0 %all-to-all-start.6 = ((bf16[32,80,992]{2,1,0:T(8,128)(2,1)}), bf16[32,80,992]{2,1,0:T(8,128)(2,1)}, u32[]{:S(2)}, u32[]{:S(2)}) async-start(bf16[32,80,992]{2,1,0:T(8,128)(2,1)} %bitcast.819), calls=%async_computation.6 | async-start | bytes 10485760 | tf_op jit(solution)/shard_map/all_to_all | solution.py:333
  321.6 117.1 %collective-permute-start.27 = (bf16[1,80,256]{2,1,0:T(8,128)(2,1)S(1)}, bf16[1,80,256]{2,1,0:T(8,128)(2,1)S(1)}, u32[]{:S(2)}, u32[]{:S(2)}) collective-permute-start(bf16[1,80,256]{2,1,0:T(8,128)(2,1)S(1)} %slice_bitcast_fusion.51), channel_id=1, source_target_pairs={{0,16},{4,20},{8,24},{12,28},{16,0},{20,4},{24,8},{28,12},{1,17},{... | collective-permute-start | bytes 122888 | tf_op jit(solution)/shard_map/ppermute | solution.py:361
  324.5 115.6 %collective-permute-start.26 = (bf16[1,80,384]{2,1,0:T(8,128)(2,1)S(1)}, bf16[1,80,384]{2,1,0:T(8,128)(2,1)S(1)}, u32[]{:S(2)}, u32[]{:S(2)}) collective-permute-start(bf16[1,80,384]{2,1,0:T(8,128)(2,1)S(1)} %get-tuple-element.618), channel_id=1, source_target_pairs={{0,16},{4,20},{8,24},{12,28},{16,0},{20,4},{24,8},{28,12},{1,17},{... | collective-permute-start | bytes 184328 | tf_op jit(solution)/shard_map/ppermute | solution.py:361
  324.7 116.1 %collective-permute-start.25 = (bf16[1,80,384]{2,1,0:T(8,128)(2,1)S(1)}, bf16[1,80,384]{2,1,0:T(8,128)(2,1)S(1)}, u32[]{:S(2)}, u32[]{:S(2)}) collective-permute-start(bf16[1,80,384]{2,1,0:T(8,128)(2,1)S(1)} %get-tuple-element.619), channel_id=1, source_target_pairs={{0,16},{4,20},{8,24},{12,28},{16,0},{20,4},{24,8},{28,12},{1,17},{... | collective-permute-start | bytes 184328 | tf_op jit(solution)/shard_map/ppermute | solution.py:361
  444.5 40.0 %collective-permute-start.38 = (bf16[512,2048]{1,0:T(8,128)(2,1)S(1)}, bf16[512,2048]{1,0:T(8,128)(2,1)S(1)}, u32[]{:S(2)}, u32[]{:S(2)}) collective-permute-start(bf16[512,2048]{1,0:T(8,128)(2,1)S(1)} %get-tuple-element.584), channel_id=1, source_target_pairs={{0,1},{1,0},{2,3},{3,2},{4,5},{5,4},{6,7},{7,6},{8,9},{9,8},{10,11... | collective-permute-start | bytes 6291464 | tf_op jit(solution)/shard_map/ppermute | solution.py:361
  452.2 27.7 %collective-permute-start.40 = (bf16[1024,512]{0,1:T(8,128)(2,1)S(1)}, bf16[1024,512]{0,1:T(8,128)(2,1)S(1)}, u32[]{:S(2)}, u32[]{:S(2)}) collective-permute-start(bf16[1024,512]{0,1:T(8,128)(2,1)S(1)} %get-tuple-element.591), channel_id=1, source_target_pairs={{0,1},{1,0},{2,3},{3,2},{4,5},{5,4},{6,7},{7,6},{8,9},{9,8},{10,11... | collective-permute-start | bytes 3145736 | tf_op jit(solution)/shard_map/ppermute | solution.py:361
  525.0 570.3 %all-reduce.5.cloned.1.call-start = ((), (), s32[]{:S(2)}) async-start(), calls=%async_computation.11 | async-start | bytes 4194304 | tf_op jit(solution)/shard_map/psum | solution.py:1025
  578.6 23.6 %collective-permute-start.44 = (f32[2,2,2,80,384]{4,3,0,2,1:T(8,128)S(1)}, f32[2,2,2,80,384]{4,3,0,2,1:T(8,128)S(1)}, u32[]{:S(2)}, u32[]{:S(2)}) collective-permute-start(f32[2,2,2,80,384]{4,3,0,2,1:T(8,128)S(1)} %bitcast.887), channel_id=1, source_target_pairs={{0,4},{4,0},{8,12},{12,8},{16,20},{20,16},{24,28},{28,24},{1,5},{5... | collective-permute-start | bytes 2949128 | tf_op jit(solution)/shard_map/ppermute | solution.py:361
  579.4 23.3 %collective-permute-start.43 = (f32[2,2,2,80,384]{4,3,0,1,2:T(8,128)S(1)}, f32[2,2,2,80,384]{4,3,0,1,2:T(8,128)S(1)}, u32[]{:S(2)}, u32[]{:S(2)}) collective-permute-start(f32[2,2,2,80,384]{4,3,0,1,2:T(8,128)S(1)} %bitcast.888), channel_id=1, source_target_pairs={{0,2},{2,0},{1,3},{3,1},{4,6},{6,4},{5,7},{7,5},{8,10},{10,8},{9,1... | collective-permute-start | bytes 2949128 | tf_op jit(solution)/shard_map/ppermute | solution.py:361
  705.1 61.9 %collective-permute-start.59 = (f32[2,2,2,2,336,128]{5,4,3,2,1,0:T(8,128)}, f32[2,2,2,2,336,128]{5,4,3,2,1,0:T(8,128)}, u32[]{:S(2)}, u32[]{:S(2)}) collective-permute-start(f32[2,2,2,2,336,128]{5,4,3,2,1,0:T(8,128)} %slice_bitcast_fusion.1), channel_id=1, source_target_pairs={{0,8},{4,12},{8,0},{12,4},{16,24},{20,28},{24,16},{28,20},{1,9},{5... | collective-permute-start | bytes 8257544 | tf_op jit(solution)/shard_map/ppermute | solution.py:361
  708.8 61.9 %collective-permute-start.58 = (f32[2,2,2,2,336,128]{5,4,3,2,1,0:T(8,128)}, f32[2,2,2,2,336,128]{5,4,3,2,1,0:T(8,128)}, u32[]{:S(2)}, u32[]{:S(2)}) collective-permute-start(f32[2,2,2,2,336,128]{5,4,3,2,1,0:T(8,128)} %slice_bitcast_fusion.2), channel_id=1, source_target_pairs={{0,4},{4,0},{8,12},{12,8},{16,20},{20,16},{24,28},{28,24},{1,5},{5... | collective-permute-start | bytes 8257544 | tf_op jit(solution)/shard_map/ppermute | solution.py:361
  711.1 64.4 %collective-permute-start.57 = (f32[2,2,2,2,352,128]{5,4,3,2,1,0:T(8,128)}, f32[2,2,2,2,352,128]{5,4,3,2,1,0:T(8,128)}, u32[]{:S(2)}, u32[]{:S(2)}) collective-permute-start(f32[2,2,2,2,352,128]{5,4,3,2,1,0:T(8,128)} %slice_bitcast_fusion), channel_id=1, source_target_pairs={{0,2},{2,0},{1,3},{3,1},{4,6},{6,4},{5,7},{7,5},{8,10},{10,8},{9,1... | collective-permute-start | bytes 8650760 | tf_op jit(solution)/shard_map/ppermute | solution.py:361
  778.9 31.3 %collective-permute-start.62 = (f32[2,2,2,336,128]{4,3,2,1,0:T(8,128)}, f32[2,2,2,336,128]{4,3,2,1,0:T(8,128)}, u32[]{:S(2)}, u32[]{:S(2)}) collective-permute-start(f32[2,2,2,336,128]{4,3,2,1,0:T(8,128)} %slice_bitcast_fusion.10), channel_id=1, source_target_pairs={{0,2},{2,0},{1,3},{3,1},{4,6},{6,4},{5,7},{7,5},{8,10},{10,8},{9,1... | collective-permute-start | bytes 4128776 | tf_op jit(solution)/shard_map/ppermute | solution.py:361
  780.4 33.4 %collective-permute-start.61 = (f32[2,2,2,336,128]{4,3,2,1,0:T(8,128)}, f32[2,2,2,336,128]{4,3,2,1,0:T(8,128)}, u32[]{:S(2)}, u32[]{:S(2)}) collective-permute-start(f32[2,2,2,336,128]{4,3,2,1,0:T(8,128)} %slice_bitcast_fusion.11), channel_id=1, source_target_pairs={{0,8},{4,12},{8,0},{12,4},{16,24},{20,28},{24,16},{28,20},{1,9},{5... | collective-permute-start | bytes 4128776 | tf_op jit(solution)/shard_map/ppermute | solution.py:361
  783.3 33.4 %collective-permute-start.60 = (f32[2,2,2,352,128]{4,3,2,1,0:T(8,128)}, f32[2,2,2,352,128]{4,3,2,1,0:T(8,128)}, u32[]{:S(2)}, u32[]{:S(2)}) collective-permute-start(f32[2,2,2,352,128]{4,3,2,1,0:T(8,128)} %slice_bitcast_fusion.5), channel_id=1, source_target_pairs={{0,4},{4,0},{8,12},{12,8},{16,20},{20,16},{24,28},{28,24},{1,5},{5... | collective-permute-start | bytes 4325384 | tf_op jit(solution)/shard_map/ppermute | solution.py:361
  805.4 63.3 %collective-permute-start.70 = (f32[2,2,2,1,336,128]{5,4,2,1,0,3:T(8,128)}, f32[2,2,2,1,336,128]{5,4,2,1,0,3:T(8,128)}, u32[]{:S(2)}, u32[]{:S(2)}) collective-permute-start(f32[2,2,2,1,336,128]{5,4,2,1,0,3:T(8,128)} %slice_bitcast_fusion.8), channel_id=1, source_target_pairs={{0,8},{4,12},{8,0},{12,4},{16,24},{20,28},{24,16},{28,20},{1,9},{5... | collective-permute-start | bytes 4128776 | tf_op jit(solution)/shard_map/ppermute | solution.py:361
  834.0 39.2 %collective-permute-start.74 = (f32[2,2,2,2,288,128]{5,4,3,2,1,0:T(8,128)}, f32[2,2,2,2,288,128]{5,4,3,2,1,0:T(8,128)}, u32[]{:S(2)}, u32[]{:S(2)}) collective-permute-start(f32[2,2,2,2,288,128]{5,4,3,2,1,0:T(8,128)} %dynamic-slice_bitcast_fusion), channel_id=1, source_target_pairs={{0,1},{1,0},{2,3},{3,2},{4,5},{5,4},{6,7},{7,6},{8,9},{9,8},{10,11... | collective-permute-start | bytes 7077896 | tf_op jit(solution)/shard_map/ppermute | solution.py:361
  853.1 37.7 %collective-permute-start.69 = (f32[2,2,2,1,336,128]{5,4,2,1,0,3:T(8,128)}, f32[2,2,2,1,336,128]{5,4,2,1,0,3:T(8,128)}, u32[]{:S(2)}, u32[]{:S(2)}) collective-permute-start(f32[2,2,2,1,336,128]{5,4,2,1,0,3:T(8,128)} %slice_bitcast_fusion.9), channel_id=1, source_target_pairs={{0,4},{4,0},{8,12},{12,8},{16,20},{20,16},{24,28},{28,24},{1,5},{5... | collective-permute-start | bytes 4128776 | tf_op jit(solution)/shard_map/ppermute | solution.py:361
  856.0 40.5 %collective-permute-start.68 = (f32[2,2,2,1,352,128]{5,4,2,1,0,3:T(8,128)}, f32[2,2,2,1,352,128]{5,4,2,1,0,3:T(8,128)}, u32[]{:S(2)}, u32[]{:S(2)}) collective-permute-start(f32[2,2,2,1,352,128]{5,4,2,1,0,3:T(8,128)} %slice_bitcast_fusion.4), channel_id=1, source_target_pairs={{0,2},{2,0},{1,3},{3,1},{4,6},{6,4},{5,7},{7,5},{8,10},{10,8},{9,1... | collective-permute-start | bytes 4325384 | tf_op jit(solution)/shard_map/ppermute | solution.py:361
  861.9 49.7 %collective-permute-start.73 = (f32[2,336,128]{2,1,0:T(8,128)}, f32[2,336,128]{2,1,0:T(8,128)S(1)}, u32[]{:S(2)}, u32[]{:S(2)}) collective-permute-start(f32[2,336,128]{2,1,0:T(8,128)} %slice_bitcast_fusion.30), channel_id=1, source_target_pairs={{0,16},{4,20},{8,24},{12,28},{16,0},{20,4},{24,8},{28,12},{1,17},{... | collective-permute-start | bytes 1032200 | tf_op jit(solution)/shard_map/ppermute | solution.py:361
  868.7 51.3 %collective-permute-start.72 = (f32[2,336,128]{2,1,0:T(8,128)}, f32[2,336,128]{2,1,0:T(8,128)S(1)}, u32[]{:S(2)}, u32[]{:S(2)}) collective-permute-start(f32[2,336,128]{2,1,0:T(8,128)} %slice_bitcast_fusion.31), channel_id=1, source_target_pairs={{0,16},{4,20},{8,24},{12,28},{16,0},{20,4},{24,8},{28,12},{1,17},{... | collective-permute-start | bytes 1032200 | tf_op jit(solution)/shard_map/ppermute | solution.py:361
  873.2 57.0 %collective-permute-start.71 = (f32[2,352,128]{2,1,0:T(8,128)S(1)}, f32[2,352,128]{2,1,0:T(8,128)S(1)}, u32[]{:S(2)}, u32[]{:S(2)}) collective-permute-start(f32[2,352,128]{2,1,0:T(8,128)S(1)} %slice_bitcast_fusion.25), channel_id=1, source_target_pairs={{0,16},{4,20},{8,24},{12,28},{16,0},{20,4},{24,8},{28,12},{1,17},{... | collective-permute-start | bytes 1081352 | tf_op jit(solution)/shard_map/ppermute | solution.py:361
  890.8 43.2 %collective-permute-start.75 = (f32[2,2,2,288,128]{4,3,2,1,0:T(8,128)}, f32[2,2,2,288,128]{4,3,2,1,0:T(8,128)}, u32[]{:S(2)}, u32[]{:S(2)}) collective-permute-start(f32[2,2,2,288,128]{4,3,2,1,0:T(8,128)} %dynamic-slice_bitcast_fusion.1), channel_id=1, source_target_pairs={{0,2},{2,0},{1,3},{3,1},{4,6},{6,4},{5,7},{7,5},{8,10},{10,8},{9,1... | collective-permute-start | bytes 3538952 | tf_op jit(solution)/shard_map/ppermute | solution.py:361
  930.2 174.5 %all-to-all-start.9 = ((f32[32,32,1024]{2,1,0:T(8,128)}), f32[32,32,1024]{2,1,0:T(8,128)}, u32[]{:S(2)}, u32[]{:S(2)}) async-start(f32[32,32,1024]{2,1,0:T(8,128)} %bitcast.847), calls=%async_computation.9 | async-start | bytes 8388608 | tf_op jit(solution)/shard_map/all_to_all | solution.py:333
  935.7 50.6 %collective-permute-start.79 = (f32[2,2,288,128]{3,2,1,0:T(8,128)S(1)}, f32[2,2,288,128]{3,2,1,0:T(8,128)S(1)}, u32[]{:S(2)}, u32[]{:S(2)}) collective-permute-start(f32[2,2,288,128]{3,2,1,0:T(8,128)S(1)} %dynamic-slice_bitcast_fusion.3), channel_id=1, source_target_pairs={{0,4},{4,0},{8,12},{12,8},{16,20},{20,16},{24,28},{28,24},{1,5},{5... | collective-permute-start | bytes 1769480 | tf_op jit(solution)/shard_map/ppermute | solution.py:361
  937.5 51.8 %collective-permute-start.78 = (f32[2,2,1,336,128]{4,3,1,0,2:T(8,128)S(1)}, f32[2,2,1,336,128]{4,3,1,0,2:T(8,128)S(1)}, u32[]{:S(2)}, u32[]{:S(2)}) collective-permute-start(f32[2,2,1,336,128]{4,3,1,0,2:T(8,128)S(1)} %slice_bitcast_fusion.17), channel_id=1, source_target_pairs={{0,2},{2,0},{1,3},{3,1},{4,6},{6,4},{5,7},{7,5},{8,10},{10,8},{9,1... | collective-permute-start | bytes 2064392 | tf_op jit(solution)/shard_map/ppermute | solution.py:361
  939.1 87.2 %collective-permute-start.77 = (f32[2,2,1,336,128]{4,3,1,0,2:T(8,128)S(1)}, f32[2,2,1,336,128]{4,3,1,0,2:T(8,128)S(1)}, u32[]{:S(2)}, u32[]{:S(2)}) collective-permute-start(f32[2,2,1,336,128]{4,3,1,0,2:T(8,128)S(1)} %slice_bitcast_fusion.18), channel_id=1, source_target_pairs={{0,8},{4,12},{8,0},{12,4},{16,24},{20,28},{24,16},{28,20},{1,9},{5... | collective-permute-start | bytes 2064392 | tf_op jit(solution)/shard_map/ppermute | solution.py:361
  940.8 85.6 %collective-permute-start.76 = (f32[2,2,1,352,128]{4,3,1,0,2:T(8,128)S(1)}, f32[2,2,1,352,128]{4,3,1,0,2:T(8,128)S(1)}, u32[]{:S(2)}, u32[]{:S(2)}) collective-permute-start(f32[2,2,1,352,128]{4,3,1,0,2:T(8,128)S(1)} %slice_bitcast_fusion.13), channel_id=1, source_target_pairs={{0,4},{4,0},{8,12},{12,8},{16,20},{20,16},{24,28},{28,24},{1,5},{5... | collective-permute-start | bytes 2162696 | tf_op jit(solution)/shard_map/ppermute | solution.py:361
  1026.6 29.5 %collective-permute-start.83 = (f32[2,288,128]{2,1,0:T(8,128)S(1)}, f32[2,288,128]{2,1,0:T(8,128)S(1)}, u32[]{:S(2)}, u32[]{:S(2)}) collective-permute-start(f32[2,288,128]{2,1,0:T(8,128)S(1)} %dynamic-slice_bitcast_fusion.4), channel_id=1, source_target_pairs={{0,8},{4,12},{8,0},{12,4},{16,24},{20,28},{24,16},{28,20},{1,9},{5... | collective-permute-start | bytes 884744 | tf_op jit(solution)/shard_map/ppermute | solution.py:361
  1029.2 27.0 %collective-permute-start.82 = (f32[2,1,336,128]{3,2,0,1:T(8,128)S(1)}, f32[2,1,336,128]{3,2,0,1:T(8,128)S(1)}, u32[]{:S(2)}, u32[]{:S(2)}) collective-permute-start(f32[2,1,336,128]{3,2,0,1:T(8,128)S(1)} %slice_bitcast_fusion.28), channel_id=1, source_target_pairs={{0,4},{4,0},{8,12},{12,8},{16,20},{20,16},{24,28},{28,24},{1,5},{5... | collective-permute-start | bytes 1032200 | tf_op jit(solution)/shard_map/ppermute | solution.py:361
  1030.7 25.5 %collective-permute-start.81 = (f32[2,1,336,128]{3,2,0,1:T(8,128)S(1)}, f32[2,1,336,128]{3,2,0,1:T(8,128)S(1)}, u32[]{:S(2)}, u32[]{:S(2)}) collective-permute-start(f32[2,1,336,128]{3,2,0,1:T(8,128)S(1)} %slice_bitcast_fusion.29), channel_id=1, source_target_pairs={{0,2},{2,0},{1,3},{3,1},{4,6},{6,4},{5,7},{7,5},{8,10},{10,8},{9,1... | collective-permute-start | bytes 1032200 | tf_op jit(solution)/shard_map/ppermute | solution.py:361
  1033.3 30.4 %collective-permute-start.80 = (f32[2,1,352,128]{3,2,0,1:T(8,128)S(1)}, f32[2,1,352,128]{3,2,0,1:T(8,128)S(1)}, u32[]{:S(2)}, u32[]{:S(2)}) collective-permute-start(f32[2,1,352,128]{3,2,0,1:T(8,128)S(1)} %slice_bitcast_fusion.24), channel_id=1, source_target_pairs={{0,8},{4,12},{8,0},{12,4},{16,24},{20,28},{24,16},{28,20},{1,9},{5... | collective-permute-start | bytes 1081352 | tf_op jit(solution)/shard_map/ppermute | solution.py:361
  1064.0 23.8 %collective-permute-start.86 = (f32[1,336,128]{2,1,0:T(8,128)S(1)}, f32[1,336,128]{2,1,0:T(8,128)S(1)}, u32[]{:S(2)}, u32[]{:S(2)}) collective-permute-start(f32[1,336,128]{2,1,0:T(8,128)S(1)} %slice_bitcast_fusion.42), channel_id=1, source_target_pairs={{0,16},{4,20},{8,24},{12,28},{16,0},{20,4},{24,8},{28,12},{1,17},{... | collective-permute-start | bytes 516104 | tf_op jit(solution)/shard_map/ppermute | solution.py:361
  1066.8 24.7 %collective-permute-start.85 = (f32[1,336,128]{2,1,0:T(8,128)S(1)}, f32[1,336,128]{2,1,0:T(8,128)S(1)}, u32[]{:S(2)}, u32[]{:S(2)}) collective-permute-start(f32[1,336,128]{2,1,0:T(8,128)S(1)} %slice_bitcast_fusion.43), channel_id=1, source_target_pairs={{0,16},{4,20},{8,24},{12,28},{16,0},{20,4},{24,8},{28,12},{1,17},{... | collective-permute-start | bytes 516104 | tf_op jit(solution)/shard_map/ppermute | solution.py:361
  1067.1 28.1 %collective-permute-start.84 = (f32[1,352,128]{2,1,0:T(8,128)S(1)}, f32[1,352,128]{2,1,0:T(8,128)S(1)}, u32[]{:S(2)}, u32[]{:S(2)}) collective-permute-start(f32[1,352,128]{2,1,0:T(8,128)S(1)} %slice_bitcast_fusion.37), channel_id=1, source_target_pairs={{0,16},{4,20},{8,24},{12,28},{16,0},{20,4},{24,8},{28,12},{1,17},{... | collective-permute-start | bytes 540680 | tf_op jit(solution)/shard_map/ppermute | solution.py:361
  1238.9 35.1 %collective-permute-start.108 = (bf16[8,352,256]{2,1,0:T(8,128)(2,1)S(1)}, bf16[8,352,256]{2,1,0:T(8,128)(2,1)}, u32[]{:S(2)}, u32[]{:S(2)}) collective-permute-start(bf16[8,352,256]{2,1,0:T(8,128)(2,1)S(1)} %pad_maximum_fusion.14), channel_id=1, source_target_pairs={{0,2},{2,0},{1,3},{3,1},{4,6},{6,4},{5,7},{7,5},{8,10},{10,8},{9,1... | collective-permute-start | bytes 4325384 | tf_op jit(solution)/shard_map/ppermute | solution.py:361
  1240.5 29.0 %collective-permute-start.109 = (bf16[8,336,256]{2,1,0:T(8,128)(2,1)}, bf16[8,336,256]{2,1,0:T(8,128)(2,1)}, u32[]{:S(2)}, u32[]{:S(2)}) collective-permute-start(bf16[8,336,256]{2,1,0:T(8,128)(2,1)} %pad_maximum_fusion.15), channel_id=1, source_target_pairs={{0,4},{4,0},{8,12},{12,8},{16,20},{20,16},{24,28},{28,24},{1,5},{5... | collective-permute-start | bytes 4128776 | tf_op jit(solution)/shard_map/ppermute | solution.py:361
  1241.0 30.7 %collective-permute-start.110 = (bf16[8,336,256]{2,1,0:T(8,128)(2,1)}, bf16[8,336,256]{2,1,0:T(8,128)(2,1)}, u32[]{:S(2)}, u32[]{:S(2)}) collective-permute-start(bf16[8,336,256]{2,1,0:T(8,128)(2,1)} %pad_maximum_fusion.16), channel_id=1, source_target_pairs={{0,8},{4,12},{8,0},{12,4},{16,24},{20,28},{24,16},{28,20},{1,9},{5... | collective-permute-start | bytes 4128776 | tf_op jit(solution)/shard_map/ppermute | solution.py:361
  (198 other events, 3133.6 us)
Sparse Core Ops, SparseCore 0:
  11.4 92.8 all-gather.4
  107.7 144.0 all-gather.6
  868.8 188.5 all-reduce.4
